TPU v7x, 32 devices: a whole 2x2x4 slice. The times are simulated.
32 devices in a mesh: groups: 2 (over x), ctx: 16 (over z, y, core).
Axes of the slice: x: 2, y: 2, z: 4, core: 2. Of those that a mesh axis runs over, the one named last changes fastest.
Arguments:
- tokens: bfloat16 [16384, 1024], P(('groups', 'ctx')), parts along dimension 0
- w_qkv: bfloat16 [1024, 3072], P('ctx'), may hold values from -0.1875 to 0.1875
- w_out: bfloat16 [1024, 1024], P('ctx'), may hold values from -0.1875 to 0.1875
- var_bias: float32 [2, 16], replicated, may hold values from -2 to 2
- seg_id: int32 [16384], P(('groups', 'ctx')), parts along dimension 0, may hold values from 0 to 3, as said below
- var_id: int32 [16384], P(('groups', 'ctx')), parts along dimension 0, may hold values from 0 to 511
- time_id: int32 [16384], P(('groups', 'ctx')), parts along dimension 0, may hold values from 0 to 67
Outputs:
- mixed: bfloat16 [16384, 1024], P(('groups', 'ctx')), parts along dimension 0
There are 2 independent parts, one for each index of `groups`. A program takes and returns all parts, laid end to end along the dimension named above; an argument that names none is the same for every part. Nothing has to cross between parts.
Inputs may be any that keep to these rules, and one draw needn't show every extreme that they name: seg_id starts at 0, never falls, and rises by at most one from a token to the next.
All inputs are finite; a program needn't handle non-finite values.
Results may differ from a plain program's by a relative error of at most 0.004.
The roundings to bfloat16 on the way count: a program that leaves them out, or rounds other values in their place, can miss the bound.
Values may be sent and summed in bfloat16 or wider, within the bound.
No kernel may reach another device: no remote copies, remote signals or barrier semaphores. Data moves between devices by JAX's collectives and lax.ppermute only.
A program may use at most 256 MiB of HBM per device.

v0:
```python
import math

import jax
import jax.numpy as jnp
from jax import lax
from jax.sharding import PartitionSpec as P


def as_sent(value):
    return jax.tree.map(lambda a: a.astype(jnp.bfloat16) if a.dtype == jnp.float32 else a, value)


def passed_along(value, axis, by):
    devices = lax.axis_size(axis)
    return lax.ppermute(value, axis, [(i, (i + by) % devices) for i in range(devices)])


def gather_near(payload):

    def relay(item, step):
        return passed_along((item[0], as_sent(item[1])), "ctx", step)

    before_one = relay(payload, 1)
    before_two = relay(before_one, 1)
    after_one = relay(payload, -1)
    after_two = relay(after_one, -1)
    return (before_two, before_one, after_one, after_two)


def local(tokens, w_qkv, w_out, var_bias, seg_id, var_id, time_id):
    rows = tokens.shape[0]
    width = tokens.shape[1]
    heads = var_bias.shape[1]
    hsize = width // heads
    idents = jnp.stack([seg_id, var_id, time_id], 0)
    center = lax.axis_index("ctx")
    count = lax.axis_size("ctx")
    columns = tokens
    qkv = jnp.dot(
        columns,
        lax.all_gather(w_qkv, "ctx", axis=0, tiled=True),
        preferred_element_type=jnp.float32,
    )
    qkv = qkv.astype(jnp.bfloat16)
    query = qkv[:, :width]
    keyval = qkv[:, width:]
    near = gather_near((keyval, idents))
    kv_list = [near[0][0], near[1][0], keyval, near[2][0], near[3][0]]
    id_list = [near[0][1], near[1][1], idents, near[2][1], near[3][1]]
    win_kv = jnp.concatenate(kv_list, 0)
    win_ids = jnp.concatenate(id_list, 1)
    span = 5 * rows
    q_pos = center * rows + jnp.arange(rows, dtype=jnp.int32)
    k_pos = (center - 2) * rows + jnp.arange(span, dtype=jnp.int32)
    inside = (k_pos >= 0) & (k_pos < count * rows)
    allowed = (seg_id[:, None] == win_ids[0][None, :]) & (win_ids[2][None, :] <= time_id[:, None])
    allowed = allowed & (jnp.abs(q_pos[:, None] - k_pos[None, :]) <= 2 * rows - 1) & inside[None, :]
    same = var_id[:, None] == win_ids[1][None, :]
    query_heads = query.reshape(rows, heads, hsize)
    key_heads = win_kv[:, :width].reshape(span, heads, hsize)
    value_heads = win_kv[:, width:].reshape(span, heads, hsize)
    scale = 1.0 / math.sqrt(hsize)
    group = math.gcd(4, heads)
    results = []
    for first in range(0, heads, group):
        q_grp = query_heads[:, first : first + group]
        k_grp = key_heads[:, first : first + group]
        v_grp = value_heads[:, first : first + group]
        bias = jnp.where(
            same[None, :, :],
            var_bias[0, first : first + group][:, None, None],
            var_bias[1, first : first + group][:, None, None],
        )
        score = (
            jnp.einsum("qhe,khe->hqk", q_grp, k_grp, preferred_element_type=jnp.float32) * scale
            + bias
        )
        score = jnp.where(allowed[None, :, :], score, -1e30)
        peak = jnp.max(score, axis=-1, keepdims=True)
        weight = jnp.where(allowed[None, :, :], jnp.exp(score - peak), 0.0)
        total = jnp.sum(weight, axis=-1)
        weight_bf = weight.astype(jnp.bfloat16)
        summed = jnp.einsum("hqk,khe->qhe", weight_bf, v_grp, preferred_element_type=jnp.float32)
        results.append(summed / jnp.transpose(total)[:, :, None])
    attended = jnp.concatenate(results, 1).reshape(rows, width).astype(jnp.bfloat16)
    columns = attended
    mixed = jnp.dot(
        columns,
        lax.all_gather(w_out, "ctx", axis=0, tiled=True),
        preferred_element_type=jnp.float32,
    )
    return mixed.astype(jnp.bfloat16)


def solution(mesh):
    in_specs = (
        P(("groups", "ctx"), None),
        P("ctx", None),
        P("ctx", None),
        P(),
        P(("groups", "ctx")),
        P(("groups", "ctx")),
        P(("groups", "ctx")),
    )
    out_specs = P(("groups", "ctx"), None)
    return jax.shard_map(local, mesh=mesh, in_specs=in_specs, out_specs=out_specs, check_vma=False)
```

profile of v0, /device:TPU:1, one launch (start us, length us, event | category | flops | bytes accessed | tf_op | source)
XLA Modules:
  0.0 518.9 jit_solution(13979249160202723776)
XLA Ops:
  6.5 0.7 all-gather.3.cloned.1.call-update
  7.3 0.0 all-gather.5.cloned.1.call-start
  7.3 66.7 %all-gather.3.cloned.1.call-done = bf16[1024,3072]{1,0:T(8,128)(2,1)} async-done(((bf16[64,3072]{1,0:T(8,128)(2,1)}), bf16[1024,3072]{1,0:T(8,128)(2,1)}) %all-gather.3.cloned.1.call-update) | async-done | bytes 6291472 | tf_op jit(solution)/shard_map/all_gather | solution.py:41
  74.0 6.4 %convolution_convert_fusion = bf16[512,3072]{1,0:T(8,128)(2,1)S(1)} fusion(bf16[512,1024]{1,0:T(8,128)(2,1)S(1)} %copy-done, bf16[1024,3072]{1,0:T(8,128)(2,1)} %all-gather.3.cloned.1.call-done), kind=kOutput, calls=%fused_computation.51 | convolution fusion | flops 3222798336 | bytes 10485760 | tf_op jit(solution)/shard_map/dot_general | solution.py:39
  80.4 1.7 copy-done.2
  82.2 1.5 slice.117
  83.7 0.4 collective-permute-start
  84.1 0.1 collective-permute-start.2
  84.2 1.7 collective-permute-start.4
  85.9 2.6 collective-permute-start.6
  88.5 0.0 all-gather.5.cloned.1.call-update
  88.6 0.6 slice_bitcast_fusion.7
  89.2 47.8 %collective-permute-done.4 = s32[3,512]{1,0:T(4,128)S(1)} collective-permute-done((s32[3,512]{1,0:T(4,128)S(1)}, s32[3,512]{1,0:T(4,128)S(1)}, u32[]{:S(2)}, u32[]{:S(2)}) %collective-permute-start.4) | collective-permute-done | bytes 6176 | tf_op jit(solution)/shard_map/ppermute | solution.py:15
  137.0 2.5 collective-permute-start.5
  139.4 0.5 collective-permute-done.6
  139.9 1.7 collective-permute-start.1
  141.7 2.5 collective-permute-done.7
  144.2 0.1 slice_reduce_fusion.2
  144.3 5.6 %fusion.41 = pred[512,2560]{1,0:T(8,128)(4,1)} fusion(s32[2560]{0:T(1024)S(1)} %iota_add_fusion, s32[512]{0:T(512)S(1)} %iota_add_fusion.1, s32[2560]{0:T(1024)S(1)} %get-tuple-element.7, s32[2560]{0:T(1024)S(1)} %get-tuple-element.5, s32[512]{0:T(512)S(1)} %copy-done.6, s32[512]{0:T(512)S(1)} %copy-done.7, pred[2560]{0:T(1024)(128)(4,1)S(1)} %compare_and_fusion), kind=kLoop, calls=%fused_computation.50 | loop fusion | flops 10485760 | bytes 1350144 | tf_op jit(solution)/shard_map/and | solution.py:57
  149.9 0.2 collective-permute-start.3
  150.0 2.0 broadcast_compare_fusion
  152.0 1.3 slice.121
  153.3 1.3 copy.21
  154.6 32.8 %collective-permute-done.1 = bf16[512,2048]{1,0:T(8,128)(2,1)} collective-permute-done((bf16[512,2048]{1,0:T(8,128)(2,1)}, bf16[512,2048]{1,0:T(8,128)(2,1)}, u32[]{:S(2)}, u32[]{:S(2)}) %collective-permute-start.1) | collective-permute-done | bytes 2097184 | tf_op jit(solution)/shard_map/ppermute | solution.py:15
  187.4 3.2 constant_dynamic-update-slice_fusion.4
  190.6 3.1 constant_dynamic-update-slice_fusion.3
  193.8 3.2 constant_dynamic-update-slice_fusion.2
  196.9 1.5 constant_dynamic-update-slice_fusion.1
  198.4 3.2 constant_dynamic-update-slice_fusion
  201.6 9.2 %fusion.118 = (bf16[2560,1024]{1,0:T(8,128)(2,1)}, bf16[2560,1024]{1,0:T(8,128)(2,1)}) fusion(bf16[2560,2048]{1,0:T(8,128)(2,1)} %constant_dynamic-update-slice_fusion), kind=kLoop, calls=%fused_computation.124 | loop fusion | bytes 20971520 | tf_op jit(solution)/shard_map/slice | solution.py:60
  210.9 8.0 %copy.22 = bf16[2560,1024]{0,1:T(8,128)(2,1)} copy(bf16[2560,1024]{1,0:T(8,128)(2,1)} %get-tuple-element.8) | data formatting | bytes 10485760 | tf_op jit(solution)/shard_map/slice | solution.py:60
  218.9 10.1 %fusion.42 = f32[4,512,2560]{2,1,0:T(8,128)} fusion(bf16[512,16,64]{0,2,1:T(8,128)(2,1)S(1)} %bitcast.72, bf16[2560,16,64]{0,2,1:T(8,128)(2,1)} %bitcast.67), kind=kOutput, calls=%fused_computation.54 | convolution fusion | flops 671088640 | bytes 23330816 | tf_op jit(solution)/shard_map/qhe,khe->hqk/dot_general | solution.py:75
  229.0 8.8 %fusion.44 = f32[4,512,2560]{2,1,0:T(8,128)} fusion(bf16[512,16,64]{0,2,1:T(8,128)(2,1)S(1)} %bitcast.73, bf16[2560,16,64]{0,2,1:T(8,128)(2,1)S(1)} %bitcast.68), kind=kOutput, calls=%fused_computation.56 | convolution fusion | flops 671088640 | bytes 23330816 | tf_op jit(solution)/shard_map/qhe,khe->hqk/dot_general | solution.py:75
  237.8 8.6 %fusion.46 = f32[4,512,2560]{2,1,0:T(8,128)} fusion(bf16[512,16,64]{0,2,1:T(8,128)(2,1)S(1)} %bitcast.74, bf16[2560,16,64]{0,2,1:T(8,128)(2,1)S(1)} %bitcast.69), kind=kOutput, calls=%fused_computation.58 | convolution fusion | flops 671088640 | bytes 23330816 | tf_op jit(solution)/shard_map/qhe,khe->hqk/dot_general | solution.py:75
  246.4 8.7 %fusion.48 = f32[4,512,2560]{2,1,0:T(8,128)} fusion(bf16[512,16,64]{0,2,1:T(8,128)(2,1)S(1)} %bitcast.75, bf16[2560,16,64]{0,2,1:T(8,128)(2,1)S(1)} %bitcast.70), kind=kOutput, calls=%fused_computation.60 | convolution fusion | flops 671088640 | bytes 23330816 | tf_op jit(solution)/shard_map/qhe,khe->hqk/dot_general | solution.py:75
  255.1 7.9 %copy.20 = bf16[2560,1024]{0,1:T(8,128)(2,1)} copy(bf16[2560,1024]{1,0:T(8,128)(2,1)} %get-tuple-element.9) | data formatting | bytes 10485760 | tf_op jit(solution)/shard_map/slice | solution.py:61
  263.0 31.4 %fusion.119 = f32[4,512]{1,0:T(4,128)S(1)} fusion(f32[4,512,2560]{2,1,0:T(8,128)} %fusion.42, f32[4]{0:T(128)S(1)} %get-tuple-element.16, f32[4]{0:T(128)S(1)} %get-tuple-element.17, pred[512,2560]{1,0:T(8,128)(4,1)} %broadcast_compare_fusion, pred[512,2560]{1,0:T(8,128)(4,1)S(1)} %copy-done.4), kind=kOutput, calls=%fused_computation.125 | output fusion | flops 36702720 | bytes 23601184 | tf_op jit(solution)/shard_map/sub | solution.py:80
  294.5 29.6 %fusion.65 = bf16[512,4,64]{0,2,1:T(8,128)(2,1)S(1)} fusion(bf16[2560,16,64]{0,2,1:T(8,128)(2,1)} %bitcast.63, f32[4,512,2560]{2,1,0:T(8,128)} %fusion.42, f32[4]{0:T(128)S(1)} %get-tuple-element.16, f32[4]{0:T(128)S(1)} %get-tuple-element.17, pred[512,2560]{1,0:T(8,128)(4,1)} %broadcast_compare_fusion, pred[512,2560]{1,0:T(8,128)(4,1)S(1)} %copy-done.4, ...), kind=kOutput, calls=%fused_computation.68 | convolution fusion | flops 708055552 | bytes 29106208 | tf_op jit(solution)/shard_map/hqk,khe->qhe/dot_general | solution.py:83
  324.0 31.1 %fusion.120 = f32[4,512]{1,0:T(4,128)S(1)} fusion(f32[4,512,2560]{2,1,0:T(8,128)} %fusion.44, f32[4]{0:T(128)S(1)} %get-tuple-element.11, f32[4]{0:T(128)S(1)} %get-tuple-element.12, pred[512,2560]{1,0:T(8,128)(4,1)} %broadcast_compare_fusion, pred[512,2560]{1,0:T(8,128)(4,1)S(1)} %copy-done.4), kind=kOutput, calls=%fused_computation.126 | output fusion | flops 36702720 | bytes 23601184 | tf_op jit(solution)/shard_map/sub | solution.py:80
  355.1 29.7 %fusion.71 = bf16[512,4,64]{0,2,1:T(8,128)(2,1)S(1)} fusion(bf16[2560,16,64]{0,2,1:T(8,128)(2,1)} %bitcast.64, f32[4,512,2560]{2,1,0:T(8,128)} %fusion.44, f32[4]{0:T(128)S(1)} %get-tuple-element.11, f32[4]{0:T(128)S(1)} %get-tuple-element.12, pred[512,2560]{1,0:T(8,128)(4,1)} %broadcast_compare_fusion, pred[512,2560]{1,0:T(8,128)(4,1)S(1)} %copy-done.4, ...), kind=kOutput, calls=%fused_computation.70 | convolution fusion | flops 708055552 | bytes 29106208 | tf_op jit(solution)/shard_map/hqk,khe->qhe/dot_general | solution.py:83
  384.9 31.7 %fusion.121 = f32[4,512]{1,0:T(4,128)S(1)} fusion(f32[4,512,2560]{2,1,0:T(8,128)} %fusion.46, f32[4]{0:T(128)S(1)} %get-tuple-element.13, f32[4]{0:T(128)S(1)} %get-tuple-element.14, pred[512,2560]{1,0:T(8,128)(4,1)} %broadcast_compare_fusion, pred[512,2560]{1,0:T(8,128)(4,1)S(1)} %copy-done.4), kind=kOutput, calls=%fused_computation.127 | output fusion | flops 36702720 | bytes 23601184 | tf_op jit(solution)/shard_map/sub | solution.py:80
  416.6 29.5 %fusion.77 = bf16[512,4,64]{0,2,1:T(8,128)(2,1)S(1)} fusion(bf16[2560,16,64]{0,2,1:T(8,128)(2,1)} %bitcast.65, f32[4,512,2560]{2,1,0:T(8,128)} %fusion.46, f32[4]{0:T(128)S(1)} %get-tuple-element.13, f32[4]{0:T(128)S(1)} %get-tuple-element.14, pred[512,2560]{1,0:T(8,128)(4,1)} %broadcast_compare_fusion, pred[512,2560]{1,0:T(8,128)(4,1)S(1)} %copy-done.4, ...), kind=kOutput, calls=%fused_computation.72 | convolution fusion | flops 708055552 | bytes 29106208 | tf_op jit(solution)/shard_map/hqk,khe->qhe/dot_general | solution.py:83
  446.1 31.6 %fusion.122 = f32[4,512]{1,0:T(4,128)S(1)} fusion(f32[4,512,2560]{2,1,0:T(8,128)} %fusion.48, f32[4]{0:T(128)S(1)} %copy-done.11, f32[4]{0:T(128)S(1)} %copy-done.10, pred[512,2560]{1,0:T(8,128)(4,1)} %broadcast_compare_fusion, pred[512,2560]{1,0:T(8,128)(4,1)S(1)} %copy-done.4), kind=kOutput, calls=%fused_computation.128 | output fusion | flops 36702720 | bytes 23601184 | tf_op jit(solution)/shard_map/sub | solution.py:80
  477.7 0.0 copy-start.1
  477.7 29.9 %fusion.83 = bf16[512,4,64]{0,2,1:T(8,128)(2,1)S(1)} fusion(bf16[2560,16,64]{0,2,1:T(8,128)(2,1)} %bitcast.66, f32[4,512,2560]{2,1,0:T(8,128)} %fusion.48, f32[4]{0:T(128)S(1)} %copy-done.11, f32[4]{0:T(128)S(1)} %copy-done.10, pred[512,2560]{1,0:T(8,128)(4,1)} %broadcast_compare_fusion, pred[512,2560]{1,0:T(8,128)(4,1)S(1)} %copy-done.4, ...), kind=kOutput, calls=%fused_computation.74 | convolution fusion | flops 708055552 | bytes 29106208 | tf_op jit(solution)/shard_map/hqk,khe->qhe/dot_general | solution.py:83
  507.6 0.1 pad_maximum_fusion
  507.8 0.0 all-gather.5.cloned.1.call-done
  507.8 3.8 convolution_convert_fusion.1
  (37 shorter events, 0.1 us)
Async XLA Ops:
  6.5 67.5 %copy-start = (bf16[512,1024]{1,0:T(8,128)(2,1)S(1)}, bf16[512,1024]{1,0:T(8,128)(2,1)}, u32[]{:S(2)}) copy-start(bf16[512,1024]{1,0:T(8,128)(2,1)} %param.7) | copy-start | bytes 3145732
  6.5 67.5 %all-gather.3.cloned.1.call-start = ((), (), s32[]{:S(2)}) async-start(), calls=%async_computation | async-start | bytes 6684672 | tf_op jit(solution)/shard_map/all_gather | solution.py:41
  7.3 76.9 %copy-start.6 = (s32[512]{0:T(512)S(1)}, s32[512]{0:T(512)}, u32[]{:S(2)}) copy-start(s32[512]{0:T(512)} %param.13) | copy-start | bytes 6148
  7.3 76.9 %copy-start.7 = (s32[512]{0:T(512)S(1)}, s32[512]{0:T(512)}, u32[]{:S(2)}) copy-start(s32[512]{0:T(512)} %param.11) | copy-start | bytes 6148
  7.3 76.9 %copy-start.8 = (s32[512]{0:T(512)S(1)}, s32[512]{0:T(512)}, u32[]{:S(2)}) copy-start(s32[512]{0:T(512)} %param.12) | copy-start | bytes 6148
  7.3 81.3 %copy-start.9 = (f32[2,16]{1,0:T(2,128)S(1)}, f32[2,16]{1,0:T(2,128)}, u32[]{:S(2)}) copy-start(f32[2,16]{1,0:T(2,128)} %param.10) | copy-start | bytes 388
  7.3 500.5 %all-gather.5.cloned.1.call-start = ((), (), s32[]{:S(2)}) async-start(), calls=%async_computation.1 | async-start | bytes 2228224 | tf_op jit(solution)/shard_map/all_gather | solution.py:89
  80.4 1.8 copy-start.2
  83.7 56.2 %collective-permute-start = (bf16[512,2048]{1,0:T(8,128)(2,1)}, bf16[512,2048]{1,0:T(8,128)(2,1)}, u32[]{:S(2)}, u32[]{:S(2)}) collective-permute-start(bf16[512,2048]{1,0:T(8,128)(2,1)} %slice.117), channel_id=1, source_target_pairs={{0,1},{1,2},{2,3},{3,4},{4,5},{5,6},{6,7},{7,8},{8,9},{9,10},{10,1... | collective-permute-start | bytes 6291464 | tf_op jit(solution)/shard_map/ppermute | solution.py:15
  84.1 65.8 %collective-permute-start.2 = (bf16[512,2048]{1,0:T(8,128)(2,1)}, bf16[512,2048]{1,0:T(8,128)(2,1)S(1)}, u32[]{:S(2)}, u32[]{:S(2)}) collective-permute-start(bf16[512,2048]{1,0:T(8,128)(2,1)} %slice.117), channel_id=1, source_target_pairs={{0,15},{1,0},{2,1},{3,2},{4,3},{5,4},{6,5},{7,6},{8,7},{9,8},{10,9... | collective-permute-start | bytes 6291464 | tf_op jit(solution)/shard_map/ppermute | solution.py:15
  84.2 52.7 %collective-permute-start.4 = (s32[3,512]{1,0:T(4,128)S(1)}, s32[3,512]{1,0:T(4,128)S(1)}, u32[]{:S(2)}, u32[]{:S(2)}) collective-permute-start(s32[3,512]{1,0:T(4,128)S(1)} %pad_add_fusion), channel_id=1, source_target_pairs={{0,1},{1,2},{2,3},{3,4},{4,5},{5,6},{6,7},{7,8},{8,9},{9,10},{10,1... | collective-permute-start | bytes 18440 | tf_op jit(solution)/shard_map/ppermute | solution.py:15
  85.9 54.0 %collective-permute-start.6 = (s32[3,512]{1,0:T(4,128)S(1)}, s32[3,512]{1,0:T(4,128)S(1)}, u32[]{:S(2)}, u32[]{:S(2)}) collective-permute-start(s32[3,512]{1,0:T(4,128)S(1)} %pad_add_fusion), channel_id=1, source_target_pairs={{0,15},{1,0},{2,1},{3,2},{4,3},{5,4},{6,5},{7,6},{8,7},{9,8},{10,9... | collective-permute-start | bytes 18440 | tf_op jit(solution)/shard_map/ppermute | solution.py:15
  137.0 4.7 collective-permute-start.5
  139.9 4.3 collective-permute-start.7
  139.9 47.5 %collective-permute-start.1 = (bf16[512,2048]{1,0:T(8,128)(2,1)}, bf16[512,2048]{1,0:T(8,128)(2,1)}, u32[]{:S(2)}, u32[]{:S(2)}) collective-permute-start(bf16[512,2048]{1,0:T(8,128)(2,1)} %collective-permute-done), channel_id=1, source_target_pairs={{0,1},{1,2},{2,3},{3,4},{4,5},{5,6},{6,7},{7,8},{8,9},{9,10},{10,1... | collective-permute-start | bytes 6291464 | tf_op jit(solution)/shard_map/ppermute | solution.py:15
  149.9 48.5 %collective-permute-start.3 = (bf16[512,2048]{1,0:T(8,128)(2,1)S(1)}, bf16[512,2048]{1,0:T(8,128)(2,1)}, u32[]{:S(2)}, u32[]{:S(2)}) collective-permute-start(bf16[512,2048]{1,0:T(8,128)(2,1)S(1)} %collective-permute-done.2), channel_id=1, source_target_pairs={{0,15},{1,0},{2,1},{3,2},{4,3},{5,4},{6,5},{7,6},{8,7},{9,8},{10,9... | collective-permute-start | bytes 6291464 | tf_op jit(solution)/shard_map/ppermute | solution.py:15
  210.9 8.0 %copy-start.5 = (bf16[512,1024]{0,1:T(8,128)(2,1)S(1)}, bf16[512,1024]{0,1:T(8,128)(2,1)}, u32[]{:S(2)}) copy-start(bf16[512,1024]{0,1:T(8,128)(2,1)} %copy.21) | copy-start | bytes 3145732
  218.9 10.1 %copy-start.3 = (bf16[2560,1024]{0,1:T(8,128)(2,1)S(1)}, bf16[2560,1024]{0,1:T(8,128)(2,1)}, u32[]{:S(2)}) copy-start(bf16[2560,1024]{0,1:T(8,128)(2,1)} %copy.22) | copy-start | bytes 15728644
  255.1 7.9 %copy-start.4 = (pred[512,2560]{1,0:T(8,128)(4,1)S(1)}, pred[512,2560]{1,0:T(8,128)(4,1)}, u32[]{:S(2)}) copy-start(pred[512,2560]{1,0:T(8,128)(4,1)} %fusion.41) | copy-start | bytes 3932164
  416.6 29.5 %copy-start.10 = (f32[4]{0:T(128)S(1)}, f32[4]{0:T(128)}, u32[]{:S(2)}) copy-start(f32[4]{0:T(128)} %get-tuple-element.10) | copy-start | bytes 52
  416.6 29.5 %copy-start.11 = (f32[4]{0:T(128)S(1)}, f32[4]{0:T(128)}, u32[]{:S(2)}) copy-start(f32[4]{0:T(128)} %get-tuple-element.15) | copy-start | bytes 52
  477.7 33.9 %copy-start.1 = (bf16[512,1024]{1,0:T(8,128)(2,1)S(1)}, bf16[512,1024]{1,0:T(8,128)(2,1)}, u32[]{:S(2)}) copy-start(bf16[512,1024]{1,0:T(8,128)(2,1)} %param.7) | copy-start | bytes 3145732
Sparse Core Ops, SparseCore 0:
  9.6 64.3 all-gather.2
  88.7 55.8 all-gather.4
where the time goes:
time: 523 us; the launch traced here: 519 us
  matrix products  165 us (32%)
  waiting for transfers between devices  151 us (29%)
  other arithmetic  134 us (26%)
  local copies, waits for them, and re-layouts  45.9 us (9%)
  between operations  14.1 us (3%)
  starting transfers between devices  9.23 us (2%)
    sub x4, other arithmetic, local(): weight = jnp.where(allowed[None, :, :], jnp.exp(score - peak), 0.0)  126 us
    dot_general x4, matrix products, local(): jnp.einsum('hqk,khe->qhe', weight_bf, v_grp, preferred_element_type=jnp.f...  119 us
    ppermute x8, waiting for transfers between devices, passed_along(): lax.ppermute(value, axis, [(i, (i + by) % devices) for i in range(devices)])  83.6 us
    all_gather x1, waiting for transfers between devices, local(): lax.all_gather(w_qkv, 'ctx', axis=0, tiled=True)  66.7 us
    dot_general x4, matrix products, local(): jnp.einsum('qhe,khe->hqk', q_grp, k_grp, preferred_element_type=jnp.float32)  36.2 us
    slice x2, local copies, waits for them, and re-layouts, local(): key_heads = win_kv[:, :width].reshape(span, heads, hsize)  17.3 us
    unnamed x31, local copies, waits for them, and re-layouts  12.8 us
  transfers between devices with their start and end apart: 10, of which 5 were waited for; matrix products, arithmetic and copies ran while one was open for 64% of the time, Pallas kernels for 0%

commit v1 on v0

v1 whole, which is shorter than its diff:
```python
import functools
import math

import jax
import jax.numpy as jnp
from jax import lax
from jax.experimental import pallas as pl
from jax.experimental.pallas import tpu as pltpu
from jax.sharding import Mesh, PartitionSpec as P

BIG = 2.0**100
TIMES = 104
SEG_BITS = 8
TILE = 256
LOG2E = math.log2(math.e)
F32 = jnp.float32
BF16 = jnp.bfloat16


def project_kernel(hq, x0, x1, x2, x3, x4, x5, w_ref, k_ref, vt_ref, qt_ref):
    rows = x0.shape[0]
    for i, x in enumerate((x0, x1, x2, x3, x4, x5)):
        own = i in (1, 4)

        def body(j, carry, i=i, x=x, own=own):
            r = pl.multiple_of(j * TILE, TILE)
            xt = x[pl.ds(r, TILE), :]
            at = pl.multiple_of(i * rows + r, TILE)
            k_ref[pl.ds(at, TILE), :] = jnp.dot(xt, w_ref[:, hq : 2 * hq], preferred_element_type=F32).astype(BF16)
            v = lax.dot_general(xt, w_ref[:, 2 * hq :], (((1,), (0,)), ((), ())), preferred_element_type=F32)
            vt_ref[:, pl.ds(at, TILE)] = v.T.astype(BF16)
            if own:
                q = jnp.dot(xt, w_ref[:, :hq], preferred_element_type=F32).astype(BF16).astype(F32) * 0.125
                qt_ref[:, pl.ds(pl.multiple_of((0 if i == 1 else rows) + r, TILE), TILE)] = q.T.astype(BF16)
            return carry

        lax.fori_loop(0, rows // TILE, body, 0)


def attend_kernel(hsize, wide, tab_ref, delta_ref, k_ref, vt_ref, qt_ref, fk_ref, fqt_ref, vk_ref, vq_ref, o_ref, qa, sc):
    pair = pl.program_id(0)
    qi = pl.program_id(1)
    nt = sc.shape[0]
    zero = jnp.zeros((hsize, TILE), BF16)
    qa[0:hsize, 0:TILE] = qt_ref[0:hsize, :]
    qa[hsize : 2 * hsize, 0:TILE] = zero
    qa[0:hsize, TILE:] = zero
    qa[hsize : 2 * hsize, TILE:] = qt_ref[hsize : 2 * hsize, :]
    qa[2 * hsize :, 0:TILE] = fqt_ref[...]
    qa[2 * hsize :, TILE:] = fqt_ref[...]
    first = tab_ref[qi * wide]
    last = tab_ref[qi * wide + 1]
    da = delta_ref[2 * pair]
    db = delta_ref[2 * pair + 1]

    def place(kk):
        return pl.multiple_of(tab_ref[qi * wide + 2 + kk], TILE)

    def scores(kk, edge):
        at = place(kk)
        lhs = jnp.concatenate([k_ref[pl.ds(at, TILE), :], fk_ref[pl.ds(at, TILE), :]], axis=1)
        s = jnp.dot(lhs, qa[...], preferred_element_type=F32)
        if edge:
            r = lax.broadcasted_iota(jnp.int32, (TILE, TILE), 0)
            p = lax.broadcasted_iota(jnp.int32, (TILE, TILE), 1)
            ok = (r > p) if edge < 0 else (r < p)
            ok = jnp.concatenate([ok, ok], axis=1)
            s = jnp.where(ok, s, -BIG)
        sc[kk] = s

        @pl.when(tab_ref[qi * wide + 2 + nt + kk] != 0)
        def _():
            vk = vk_ref[pl.ds(at, TILE), :]
            same = jnp.concatenate([vk, vk], axis=1) == vq_ref[...]
            sc[kk, :, 0:TILE] += jnp.where(same, da, 0.0)
            sc[kk, :, TILE:] += jnp.where(same, db, 0.0)

    @pl.when(first == 0)
    def _():
        scores(0, -1)

    @pl.when(last == nt)
    def _():
        scores(nt - 1, 1)

    def inner(kk, carry):
        scores(kk, 0)
        return carry

    lax.fori_loop(jnp.maximum(first, 1), jnp.minimum(last, nt - 1), inner, 0)

    def peak(kk, m):
        return jnp.maximum(m, jnp.max(sc[kk].reshape(TILE // 8, 8, 2 * TILE), axis=0))

    m = lax.fori_loop(first, last, peak, jnp.full((8, 2 * TILE), -BIG, F32))
    m = jnp.max(m, axis=0, keepdims=True)

    def mix(kk, carry):
        tot, oa, ob = carry
        w = jnp.exp2((sc[kk] - m) * LOG2E)
        tot = tot + jnp.sum(w.reshape(TILE // 8, 8, 2 * TILE), axis=0)
        wb = w.astype(BF16)
        vt = vt_ref[:, pl.ds(place(kk), TILE)]
        oa = oa + jnp.dot(vt[0:hsize], wb[:, 0:TILE], preferred_element_type=F32)
        ob = ob + jnp.dot(vt[hsize:], wb[:, TILE:], preferred_element_type=F32)
        return tot, oa, ob

    z = jnp.zeros((hsize, TILE), F32)
    tot, oa, ob = lax.fori_loop(first, last, mix, (jnp.zeros((8, 2 * TILE), F32), z, z))
    tot = jnp.sum(tot, axis=0, keepdims=True)
    o_ref[0:hsize, :] = (oa / tot[:, 0:TILE]).astype(BF16)
    o_ref[hsize:, :] = (ob / tot[:, TILE:]).astype(BF16)


def local(chips, tokens, w_qkv, w_out, var_bias, seg_id, var_id, time_id):
    rows, width = tokens.shape
    heads = var_bias.shape[1]
    hsize = width // heads
    hq = width // 2
    core = lax.axis_index("core")
    chip = lax.axis_index("chip")
    swap = [(0, 1), (1, 0)]
    up = [(i, i + 1) for i in range(chips - 1)]
    down = [(i + 1, i) for i in range(chips - 1)]

    def half(w, c):
        return jnp.concatenate([lax.dynamic_slice_in_dim(w, a * width + c * hq, hq, 1) for a in range(3)], 1)

    got = lax.ppermute(half(w_qkv, 1 - core), "core", swap)
    mine = half(w_qkv, core)
    both = jnp.where(core == 0, jnp.concatenate([mine, got], 0), jnp.concatenate([got, mine], 0))
    w = lax.all_gather(both, "chip", axis=0, tiled=True)
    w_o = lax.all_gather(w_out, ("chip", "core"), axis=0, tiled=True)

    def spread(a):
        before = lax.ppermute(a, "chip", up)
        after = lax.ppermute(a, "chip", down)
        return [before, a, after] + [lax.ppermute(t, "core", swap) for t in (before, a, after)]

    ids = jnp.stack([seg_id, var_id, time_id], 0)
    xs = spread(tokens)
    seg, var, time = jnp.concatenate(spread(ids), 1)

    nk = 6 * rows
    per = rows // TILE
    nt = 2 * ((2 * rows) // TILE) + 1
    nq = 2 * per
    there = jnp.stack([chip > 0, chip >= 0, chip < chips - 1]).astype(jnp.int32)
    there = jnp.repeat(jnp.tile(there, 2), rows)
    bits = jnp.arange(SEG_BITS, dtype=jnp.int32)
    seg_bit = ((seg[:, None] >> bits[None, :]) & 1).astype(F32)
    late = (time[:, None] > jnp.arange(TIMES, dtype=jnp.int32)[None, :]).astype(F32)
    pad = jnp.zeros((nk, 128 - TIMES - 2 * SEG_BITS - 1), F32)
    fk = -BIG * jnp.concatenate([late, seg_bit, 1.0 - seg_bit, 1.0 - there.astype(F32)[:, None], pad], 1)
    fk = fk.astype(BF16)

    def mine_of(a):
        return jnp.concatenate([a[rows : 2 * rows], a[4 * rows : 5 * rows]], 0)

    seg_q, var_q, time_q = mine_of(seg), mine_of(var), mine_of(time)
    qbit = ((seg_q[None, :] >> bits[:, None]) & 1).astype(F32)
    at_time = (time_q[None, :] == jnp.arange(TIMES, dtype=jnp.int32)[:, None]).astype(F32)
    fqt = jnp.concatenate([at_time, 1.0 - qbit, qbit, jnp.ones((1, 2 * rows), F32), jnp.zeros((128 - TIMES - 2 * SEG_BITS - 1, 2 * rows), F32)], 0)
    fqt = fqt.astype(BF16)

    qtile = jnp.arange(nq, dtype=jnp.int32)
    q_core = jnp.where(qtile // per == 0, core, 1 - core)
    q_win = (2 + q_core) * per + qtile % per
    k_win = q_win[:, None] - 2 * per + jnp.arange(nt, dtype=jnp.int32)[None, :]
    kblock = k_win // per
    kplace = (jnp.where(kblock % 2 == core, 0, 3) + kblock // 2) * per + k_win % per
    code = seg * 1024 + var
    tiles = code.reshape(nk // TILE, TILE)
    lo, hi = tiles.min(1), tiles.max(1)
    slo, shi = lo // 1024, hi // 1024
    ok = there.reshape(nk // TILE, TILE)[:, 0]
    qlo, qhi = mine_of_tiles(lo, per), mine_of_tiles(hi, per)
    use = (ok[kplace] > 0) & (slo[kplace] <= (qhi // 1024)[:, None]) & (shi[kplace] >= (qlo // 1024)[:, None])
    share = (lo[kplace] <= qhi[:, None]) & (hi[kplace] >= qlo[:, None])
    index = jnp.arange(nt, dtype=jnp.int32)[None, :]
    first = jnp.min(jnp.where(use, index, nt), 1)
    last = jnp.max(jnp.where(use, index + 1, 0), 1)
    wide = 2 + 2 * nt
    table = jnp.concatenate([first[:, None], last[:, None], kplace * TILE, share.astype(jnp.int32)], 1).reshape(-1)
    delta = lax.dynamic_slice_in_dim(var_bias[0] - var_bias[1], core * (heads // 2), heads // 2, 0)
    vk = jnp.broadcast_to(var[:, None], (nk, 128))

    vm = pl.BlockSpec(memory_space=pltpu.VMEM)
    k, vt, qt = pl.pallas_call(
        functools.partial(project_kernel, hq),
        out_shape=[
            jax.ShapeDtypeStruct((nk, hq), BF16),
            jax.ShapeDtypeStruct((hq, nk), BF16),
            jax.ShapeDtypeStruct((hq, 2 * rows), BF16),
        ],
        in_specs=[vm] * 7,
        out_specs=[vm] * 3,
        compiler_params=pltpu.CompilerParams(vmem_limit_bytes=48 << 20),
        name="project",
    )(*xs, w)

    att = pl.pallas_call(
        functools.partial(attend_kernel, hsize, wide),
        out_shape=jax.ShapeDtypeStruct((hq, 2 * rows), BF16),
        grid_spec=pltpu.PrefetchScalarGridSpec(
            num_scalar_prefetch=2,
            grid=(heads // 4, nq),
            in_specs=[
                pl.BlockSpec((nk, 2 * hsize), lambda p, q, *_: (0, p)),
                pl.BlockSpec((2 * hsize, nk), lambda p, q, *_: (p, 0)),
                pl.BlockSpec((2 * hsize, TILE), lambda p, q, *_: (p, q)),
                pl.BlockSpec((nk, 128), lambda p, q, *_: (0, 0)),
                pl.BlockSpec((128, TILE), lambda p, q, *_: (0, q)),
                pl.BlockSpec((nk, 128), lambda p, q, *_: (0, 0)),
                pl.BlockSpec((1, TILE), lambda p, q, *_: (0, q)),
            ],
            out_specs=pl.BlockSpec((2 * hsize, TILE), lambda p, q, *_: (p, q)),
            scratch_shapes=[
                pltpu.VMEM((2 * hsize + 128, 2 * TILE), BF16),
                pltpu.VMEM((nt, TILE, 2 * TILE), F32),
            ],
        ),
        compiler_params=pltpu.CompilerParams(vmem_limit_bytes=48 << 20),
        name="attend",
    )(table, delta, k, vt, qt, fk, fqt, vk, var_q[None, :])

    mine_att = att[:, :rows]
    got_att = lax.ppermute(att[:, rows:], "core", swap)
    w_mine = lax.dynamic_slice_in_dim(w_o, core * hq, hq, 0)
    w_got = lax.dynamic_slice_in_dim(w_o, (1 - core) * hq, hq, 0)

    def down_dot(a, b):
        return lax.dot_general(a, b, (((0,), (0,)), ((), ())), preferred_element_type=F32)

    return (down_dot(mine_att, w_mine) + down_dot(got_att, w_got)).astype(BF16)


def mine_of_tiles(a, per):
    return jnp.concatenate([a[per : 2 * per], a[4 * per : 5 * per]], 0)


def solution(mesh):
    groups, ctx = mesh.shape["groups"], mesh.shape["ctx"]
    chips = ctx // 2
    mesh3 = Mesh(mesh.devices.reshape(groups, chips, 2), ("groups", "chip", "core"))
    toks = ("groups", "chip", "core")
    par = ("chip", "core")
    in_specs = (P(toks, None), P(par, None), P(par, None), P(), P(toks), P(toks), P(toks))
    return jax.shard_map(
        functools.partial(local, chips), mesh=mesh3, in_specs=in_specs, out_specs=P(toks, None), check_vma=False
    )
```

time: 523 us -> 196 us (0.37)
  the two profiles are of different devices: /device:TPU:1 before, /device:TPU:7 now
where the time goes in v1:
time: 196 us
  Pallas kernels  88.8 us (45%)
  waiting for transfers between devices  46.6 us (24%)
  starting transfers between devices  16.8 us (9%)
  local copies, waits for them, and re-layouts  16.5 us (8%)
  between operations  13.7 us (7%)
  other arithmetic  10.2 us (5%)
  matrix products  3.7 us (2%)
    pallas_call x1, Pallas kernels, local(): pl.pallas_call(functools.partial(attend_kernel, hsize, wide), out_shape=j...  72.7 us
    ppermute x2, waiting for transfers between devices, spread(): before = lax.ppermute(a, 'chip', up)  37.1 us
    pallas_call x1, Pallas kernels, local(): pl.pallas_call(functools.partial(project_kernel, hq), out_shape=[jax.Shap...  16.1 us
    ppermute x2, starting transfers between devices, spread(): before = lax.ppermute(a, 'chip', up)  7.13 us
    concatenate x1, local copies, waits for them, and re-layouts, local(): jnp.concatenate([late, seg_bit, 1.0 - seg_bit, 1.0 - there.astype(F32)[:,...  6.37 us
    all_gather x1, waiting for transfers between devices, local(): w = lax.all_gather(both, 'chip', axis=0, tiled=True)  5.8 us
    ppermute x2, starting transfers between devices, spread(): after = lax.ppermute(a, 'chip', down)  4.11 us
  transfers between devices with their start and end apart: 14, of which 6 were waited for; matrix products, arithmetic and copies ran while one was open for 13% of the time, Pallas kernels for 45%

profile of v1, /device:TPU:7, one launch (start us, length us, event | category | flops | bytes accessed | tf_op | source)
XLA Modules:
  0.0 196.2 jit_solution(10829544546808851371)
XLA Ops:
  6.6 1.1 constant_dynamic-slice_fusion.5
  7.7 0.7 collective-permute-start.10
  8.5 1.1 collective-permute-done.10
  9.6 0.8 maximum_select_fusion
  10.5 3.1 %collective-permute-start.5 = (bf16[512,1024]{1,0:T(8,128)(2,1)S(1)}, bf16[512,1024]{1,0:T(8,128)(2,1)S(1)}, u32[]{:S(2)}, u32[]{:S(2)}) collective-permute-start(bf16[512,1024]{1,0:T(8,128)(2,1)S(1)} %copy-done), channel_id=1, source_target_pairs={{0,2},{2,4},{4,6},{6,8},{8,10},{10,12},{12,14},{1,3},{3,5},{5,7},{... | collective-permute-start | bytes 3145736 | tf_op jit(solution)/shard_map/ppermute | solution.py:136
  13.6 2.2 %collective-permute-start.6 = (bf16[512,1024]{1,0:T(8,128)(2,1)S(1)}, bf16[512,1024]{1,0:T(8,128)(2,1)}, u32[]{:S(2)}, u32[]{:S(2)}) collective-permute-start(bf16[512,1024]{1,0:T(8,128)(2,1)S(1)} %copy-done), channel_id=1, source_target_pairs={{2,0},{4,2},{6,4},{8,6},{10,8},{12,10},{14,12},{3,1},{5,3},{7,5},{... | collective-permute-start | bytes 3145736 | tf_op jit(solution)/shard_map/ppermute | solution.py:137
  15.8 1.0 collective-permute-start.8
  16.8 4.0 %collective-permute-start = (s32[3,512]{1,0:T(4,128)S(1)}, s32[3,512]{1,0:T(4,128)S(1)}, u32[]{:S(2)}, u32[]{:S(2)}) collective-permute-start(s32[3,512]{1,0:T(4,128)S(1)} %pad_add_fusion), channel_id=1, source_target_pairs={{0,2},{2,4},{4,6},{6,8},{8,10},{10,12},{12,14},{1,3},{3,5},{5,7},{... | collective-permute-start | bytes 18440 | tf_op jit(solution)/shard_map/ppermute | solution.py:136
  20.8 0.4 collective-permute-start.3
  21.3 0.1 compare_select_fusion
  21.4 0.1 fusion.15
  21.6 0.1 tile.10
  21.9 0.8 gather_fusion
  22.8 0.1 reshape.462
  22.9 1.8 copy.21
  24.7 1.9 collective-permute-start.1
  26.7 37.1 %collective-permute-done = s32[3,512]{1,0:T(4,128)S(1)} collective-permute-done((s32[3,512]{1,0:T(4,128)S(1)}, s32[3,512]{1,0:T(4,128)S(1)}, u32[]{:S(2)}, u32[]{:S(2)}) %collective-permute-start) | collective-permute-done | bytes 6176 | tf_op jit(solution)/shard_map/ppermute | solution.py:136
  63.9 0.1 concatenate.81.fqt_ref
  64.0 1.3 collective-permute-start.2
  65.3 0.1 collective-permute-start.4
  65.4 0.7 collective-permute-done.2
  66.1 0.3 collective-permute-done.4
  66.5 2.3 %and_convert_fusion = f32[3072,8]{1,0:T(8,128)} fusion(s32[3072]{0:T(1024)S(1)} %bitcast.27), kind=kLoop, calls=%fused_computation.7 | loop fusion | flops 73728 | bytes 110592 | tf_op jit(solution)/shard_map/convert_element_type | solution.py:151
  68.8 0.1 fusion.29
  69.0 2.3 %broadcast_subtract_fusion = f32[3072,8]{1,0:T(8,128)} fusion(s32[3072]{0:T(1024)S(1)} %bitcast.28), kind=kLoop, calls=%fused_computation.13 | loop fusion | flops 98304 | bytes 110592 | tf_op jit(solution)/shard_map/sub | solution.py:154
  71.3 0.8 gather_fusion.3
  72.1 0.8 gather_fusion.4
  72.9 0.8 gather_fusion.1
  73.8 0.8 gather_fusion.2
  74.6 0.1 and_select_fusion
  74.7 0.2 select_reduce_fusion.1
  74.9 0.1 copy.16
  75.0 0.1 copy.17
  75.3 2.2 %fusion = f32[3072,104]{1,0:T(8,128)} fusion(s32[3072]{0:T(1024)S(1)} %bitcast.31), kind=kLoop, calls=%fused_computation.9 | loop fusion | flops 638976 | bytes 1290240 | tf_op jit(solution)/shard_map/convert_element_type | solution.py:152
  77.5 0.2 collective-permute-start.7
  77.7 0.3 collective-permute-start.9
  78.2 0.1 reshape.415.tab_ref
  78.3 1.4 broadcast_in_dim.94
  79.6 6.4 %concatenate.78 = f32[3072,128]{1,0:T(8,128)} concatenate(f32[3072,104]{1,0:T(8,128)} %fusion, f32[3072,8]{1,0:T(8,128)} %and_convert_fusion, f32[3072,8]{1,0:T(8,128)} %broadcast_subtract_fusion, f32[3072,1]{1,0:T(8,128)} %bitcast.26, f32[3072,7]{1,0:T(8,128)} %broadcast_in_dim.94), dimensions={1} | concatenate | bytes 3145728 | tf_op jit(solution)/shard_map/concatenate | solution.py:154
  86.0 1.5 multiply_convert_fusion.fk_ref
  87.5 5.8 %all-gather.3.cloned.1.call-done.w_ref = bf16[1024,1536]{1,0:T(8,128)(2,1)} async-done(((bf16[128,1536]{1,0:T(8,128)(2,1)}), bf16[1024,1536]{1,0:T(8,128)(2,1)}) %all-gather.3.cloned.1.call-update) | async-done | bytes 3145744 | tf_op jit(solution)/shard_map/all_gather | solution.py:132
  93.3 16.1 %project.1 = (bf16[3072,512]{1,0:T(8,128)(2,1)}, bf16[512,3072]{1,0:T(8,128)(2,1)}, bf16[512,1024]{1,0:T(8,128)(2,1)S(1)}) custom-call(bf16[512,1024]{1,0:T(8,128)(2,1)S(1)} %collective-permute-done.5.x0, bf16[512,1024]{1,0:T(8,128)(2,1)S(1)} %copy-done, bf16[512,1024]{1,0:T(8,128)(2,1)} %collective-permute-done.6.x2, ...), custom_call_target="tpu_custom_call" | custom-call | tf_op jit(solution)/shard_map/project/pallas_call | solution.py:189
  109.4 0.5 broadcast_in_dim.98.vk_ref
  109.9 72.7 %attend.1 = bf16[512,1024]{1,0:T(8,128)(2,1)S(1)} custom-call(s32[80]{0:T(128)S(1)} %reshape.415.tab_ref, f32[8]{0:T(128)S(1)} %fusion.28.delta_ref, bf16[3072,512]{1,0:T(8,128)(2,1)} %get-tuple-element.8.k_ref, bf16[512,3072]{1,0:T(8,128)(2,1)} %get-tuple-element.9.vt_ref, bf16[512,1024]{1,0:T(8,128)(2,1)S(1)} %get-tuple-element.10.qt_ref, ...), custom_call_target="tpu_custom_call" | custom-call | tf_op jit(solution)/shard_map/attend/pallas_call | solution.py:202
  182.6 1.5 collective-permute-start.11
  184.2 1.5 collective-permute-done.11
  185.7 1.9 fusion.1
  187.7 1.8 add_convert_fusion
  (67 shorter events, 1.6 us)
Async XLA Ops:
  6.5 3.9 %copy-start = (bf16[512,1024]{1,0:T(8,128)(2,1)S(1)}, bf16[512,1024]{1,0:T(8,128)(2,1)}, u32[]{:S(2)}) copy-start(bf16[512,1024]{1,0:T(8,128)(2,1)} %x1.1) | copy-start | bytes 3145732
  6.5 10.3 %copy-start.2 = (s32[512]{0:T(512)S(1)}, s32[512]{0:T(512)}, u32[]{:S(2)}) copy-start(s32[512]{0:T(512)} %param.11) | copy-start | bytes 6148
  6.5 10.3 %copy-start.4 = (s32[512]{0:T(512)S(1)}, s32[512]{0:T(512)}, u32[]{:S(2)}) copy-start(s32[512]{0:T(512)} %param.12) | copy-start | bytes 6148
  6.5 10.3 %copy-start.3 = (s32[512]{0:T(512)S(1)}, s32[512]{0:T(512)}, u32[]{:S(2)}) copy-start(s32[512]{0:T(512)} %param.13) | copy-start | bytes 6148
  6.5 86.8 %all-gather.3.cloned.1.call-start = ((), (), s32[]{:S(2)}) async-start(), calls=%async_computation | async-start | bytes 3538944 | tf_op jit(solution)/shard_map/all_gather | solution.py:132
  7.7 1.8 collective-permute-start.10
  9.6 13.2 %copy-start.5 = (f32[2,16]{1,0:T(2,128)S(1)}, f32[2,16]{1,0:T(2,128)}, u32[]{:S(2)}) copy-start(f32[2,16]{1,0:T(2,128)} %param.10) | copy-start | bytes 388
  10.4 173.8 %all-gather.5.cloned.1.call-start = ((), (), s32[]{:S(2)}) async-start(), calls=%async_computation.1 | async-start | bytes 2228224 | tf_op jit(solution)/shard_map/all_gather | solution.py:133
  10.5 67.1 %collective-permute-start.5 = (bf16[512,1024]{1,0:T(8,128)(2,1)S(1)}, bf16[512,1024]{1,0:T(8,128)(2,1)S(1)}, u32[]{:S(2)}, u32[]{:S(2)}) collective-permute-start(bf16[512,1024]{1,0:T(8,128)(2,1)S(1)} %copy-done), channel_id=1, source_target_pairs={{0,2},{2,4},{4,6},{6,8},{8,10},{10,12},{12,14},{1,3},{3,5},{5,7},{... | collective-permute-start | bytes 3145736 | tf_op jit(solution)/shard_map/ppermute | solution.py:136
  13.6 64.1 %collective-permute-start.6 = (bf16[512,1024]{1,0:T(8,128)(2,1)S(1)}, bf16[512,1024]{1,0:T(8,128)(2,1)}, u32[]{:S(2)}, u32[]{:S(2)}) collective-permute-start(bf16[512,1024]{1,0:T(8,128)(2,1)S(1)} %copy-done), channel_id=1, source_target_pairs={{2,0},{4,2},{6,4},{8,6},{10,8},{12,10},{14,12},{3,1},{5,3},{7,5},{... | collective-permute-start | bytes 3145736 | tf_op jit(solution)/shard_map/ppermute | solution.py:137
  15.8 71.7 %collective-permute-start.8 = (bf16[512,1024]{1,0:T(8,128)(2,1)S(1)}, bf16[512,1024]{1,0:T(8,128)(2,1)}, u32[]{:S(2)}, u32[]{:S(2)}) collective-permute-start(bf16[512,1024]{1,0:T(8,128)(2,1)S(1)} %copy-done), channel_id=1, source_target_pairs={{0,1},{1,0},{2,3},{3,2},{4,5},{5,4},{6,7},{7,6},{8,9},{9,8},{10,11... | collective-permute-start | bytes 3145736 | tf_op jit(solution)/shard_map/ppermute | solution.py:138
  16.8 46.9 %collective-permute-start = (s32[3,512]{1,0:T(4,128)S(1)}, s32[3,512]{1,0:T(4,128)S(1)}, u32[]{:S(2)}, u32[]{:S(2)}) collective-permute-start(s32[3,512]{1,0:T(4,128)S(1)} %pad_add_fusion), channel_id=1, source_target_pairs={{0,2},{2,4},{4,6},{6,8},{8,10},{10,12},{12,14},{1,3},{3,5},{5,7},{... | collective-permute-start | bytes 18440 | tf_op jit(solution)/shard_map/ppermute | solution.py:136
  20.8 3.9 %collective-permute-start.3 = (s32[3,512]{1,0:T(4,128)S(1)}, s32[3,512]{1,0:T(4,128)S(1)}, u32[]{:S(2)}, u32[]{:S(2)}) collective-permute-start(s32[3,512]{1,0:T(4,128)S(1)} %pad_add_fusion), channel_id=1, source_target_pairs={{0,1},{1,0},{2,3},{3,2},{4,5},{5,4},{6,7},{7,6},{8,9},{9,8},{10,11... | collective-permute-start | bytes 18440 | tf_op jit(solution)/shard_map/ppermute | solution.py:138
  24.7 40.6 %collective-permute-start.1 = (s32[3,512]{1,0:T(4,128)S(1)}, s32[3,512]{1,0:T(4,128)S(1)}, u32[]{:S(2)}, u32[]{:S(2)}) collective-permute-start(s32[3,512]{1,0:T(4,128)S(1)} %pad_add_fusion), channel_id=1, source_target_pairs={{2,0},{4,2},{6,4},{8,6},{10,8},{12,10},{14,12},{3,1},{5,3},{7,5},{... | collective-permute-start | bytes 18440 | tf_op jit(solution)/shard_map/ppermute | solution.py:137
  64.0 2.1 %collective-permute-start.2 = (s32[3,512]{1,0:T(4,128)S(1)}, s32[3,512]{1,0:T(4,128)S(1)}, u32[]{:S(2)}, u32[]{:S(2)}) collective-permute-start(s32[3,512]{1,0:T(4,128)S(1)} %collective-permute-done), channel_id=1, source_target_pairs={{0,1},{1,0},{2,3},{3,2},{4,5},{5,4},{6,7},{7,6},{8,9},{9,8},{10,11... | collective-permute-start | bytes 18440 | tf_op jit(solution)/shard_map/ppermute | solution.py:138
  65.3 1.2 collective-permute-start.4
  77.5 10.0 %collective-permute-start.7 = (bf16[512,1024]{1,0:T(8,128)(2,1)S(1)}, bf16[512,1024]{1,0:T(8,128)(2,1)}, u32[]{:S(2)}, u32[]{:S(2)}) collective-permute-start(bf16[512,1024]{1,0:T(8,128)(2,1)S(1)} %collective-permute-done.5.x0), channel_id=1, source_target_pairs={{0,1},{1,0},{2,3},{3,2},{4,5},{5,4},{6,7},{7,6},{8,9},{9,8},{10,11... | collective-permute-start | bytes 3145736 | tf_op jit(solution)/shard_map/ppermute | solution.py:138
  77.7 9.8 %collective-permute-start.9 = (bf16[512,1024]{1,0:T(8,128)(2,1)}, bf16[512,1024]{1,0:T(8,128)(2,1)}, u32[]{:S(2)}, u32[]{:S(2)}) collective-permute-start(bf16[512,1024]{1,0:T(8,128)(2,1)} %collective-permute-done.6.x2), channel_id=1, source_target_pairs={{0,1},{1,0},{2,3},{3,2},{4,5},{5,4},{6,7},{7,6},{8,9},{9,8},{10,11... | collective-permute-start | bytes 3145736 | tf_op jit(solution)/shard_map/ppermute | solution.py:138
  182.6 3.1 %collective-permute-start.11 = (bf16[512,512]{1,0:T(8,128)(2,1)S(1)}, bf16[512,512]{1,0:T(8,128)(2,1)S(1)}, u32[]{:S(2)}, u32[]{:S(2)}) collective-permute-start(bf16[512,512]{1,0:T(8,128)(2,1)S(1)} %slice.89), channel_id=1, source_target_pairs={{0,1},{1,0},{2,3},{3,2},{4,5},{5,4},{6,7},{7,6},{8,9},{9,8},{10,11... | collective-permute-start | bytes 1572872 | tf_op jit(solution)/shard_map/ppermute | solution.py:228
  184.2 3.5 %copy-start.1 = (bf16[1024,1024]{1,0:T(8,128)(2,1)S(1)}, bf16[1024,1024]{1,0:T(8,128)(2,1)}, u32[]{:S(2)}) copy-start(bf16[1024,1024]{1,0:T(8,128)(2,1)} %all-gather.5.cloned.1.call-done) | copy-start | bytes 6291460
Sparse Core Ops, SparseCore 0:
  10.5 82.7 all-gather.2
  95.5 41.4 all-gather.4

commit v2 on v0

v2 whole, which is shorter than its diff:
```python
import functools
import math

import jax
import jax.numpy as jnp
from jax import lax
from jax.experimental import pallas as pl
from jax.experimental.pallas import tpu as pltpu
from jax.sharding import Mesh, PartitionSpec as P

BIG = 2.0**100
TIMES = 104
SEG_BITS = 8
TILE = 256
CHUNKS = 2
LOG2E = math.log2(math.e)
F32 = jnp.float32
BF16 = jnp.bfloat16
I32 = jnp.int32


def pick_kernel(width, cols, wide, pairs, who_ref, w_ref, *outs):
    me, half = who_ref[0], who_ref[1]
    for step, out in enumerate(outs):
        to = me ^ step
        for a in range(3):
            for b in range(pairs):
                at = pl.multiple_of(a * width + to * cols + (half ^ b if pairs == 1 else b) * wide, wide)
                out[:, (a * pairs + b) * wide : (a * pairs + b + 1) * wide] = w_ref[:, pl.ds(at, wide)]


def project_kernel(cols, plan, queries, planes, couple, who_ref, *refs):
    n = len(plan)
    k_ref, vt_ref, qt_ref, w = refs[-4:]
    xs, parts = refs[:n], refs[n:-4]
    me, plane, half = who_ref[0], who_ref[1], who_ref[2]
    wide = cols // 2
    rows = w.shape[0] // (4 * planes)
    for i, part in enumerate(parts):
        pair = half if i == 0 else 1 - half
        for p in range(planes):
            source = lax.rem(plane + planes - p, planes)
            for step in range(4):
                to = pl.multiple_of((4 * source + (me ^ step)) * rows, rows)
                block = part[(4 * p + step) * rows : (4 * p + step + 1) * rows, :]
                if couple:
                    for a in range(3):
                        at = pl.multiple_of(a * cols + pair * wide, wide)
                        w[pl.ds(to, rows), pl.ds(at, wide)] = block[:, a * wide : (a + 1) * wide]
                else:
                    w[pl.ds(to, rows), :] = block
    for x, at in zip(xs, plan):
        rows = x.shape[0]
        out = jnp.dot(x[...], w[...], preferred_element_type=F32)
        k_ref[at : at + rows, :] = out[:, cols : 2 * cols].astype(BF16)
        vt_ref[:, at : at + rows] = out[:, 2 * cols :].astype(BF16).T
        if at in queries:
            q = (out[:, :cols].astype(BF16) * 0.125).astype(BF16)
            qt_ref[:, queries[at] : queries[at] + rows] = q.T


def attend_kernel(
    hsize, q0, nq, tab_ref, delta_ref, k_ref, vt_ref, qt_ref, fk_ref, fqt_ref, vk_ref, vq_ref, o_ref, qa0, qa1, sc0, sc1, m0, m1
):
    qi = pl.program_id(0)
    qas, scs, ms = (qa0, qa1), (sc0, sc1), (m0, m1)
    nt = sc0.shape[0]
    wide = nt + 1
    two = 2 * hsize

    def place(q, kk):
        return pl.multiple_of(tab_ref[(q0 + q) * wide + kk], TILE)

    def lanes(q):
        return pl.ds(pl.multiple_of((q0 + q) * TILE, TILE), TILE)

    def prep():
        zero = jnp.zeros((hsize, TILE), BF16)
        for j, qa in enumerate(qas):
            qa[0:hsize, 0:TILE] = qt_ref[two * j : two * j + hsize, lanes(qi)]
            qa[0:hsize, TILE:] = zero
            qa[hsize:two, 0:TILE] = zero
            qa[hsize:two, TILE:] = qt_ref[two * j + hsize : two * (j + 1), lanes(qi)]
            f = fqt_ref[:, lanes(qi)]
            qa[two:, 0:TILE] = f
            qa[two:, TILE:] = f

    def scores(j, kk, share, m):
        at = place(qi, kk)
        lhs = jnp.concatenate([k_ref[pl.ds(at, TILE), two * j : two * (j + 1)], fk_ref[pl.ds(at, TILE), :]], axis=1)
        s = jnp.dot(lhs, qas[j][...], preferred_element_type=F32)
        if kk in (0, nt - 1):
            r = lax.broadcasted_iota(I32, (TILE, TILE), 0)
            p = lax.broadcasted_iota(I32, (TILE, TILE), 1)
            ok = (r > p) if kk == 0 else (r < p)
            s = jnp.where(jnp.concatenate([ok, ok], axis=1), s, -BIG)
        if share:
            vk = vk_ref[pl.ds(at, TILE), :]
            same = jnp.concatenate([vk, vk], axis=1) == vq_ref[:, lanes(qi)]
            s = s + jnp.concatenate(
                [jnp.where(same, delta_ref[2 * j], 0.0), jnp.where(same, delta_ref[2 * j + 1], 0.0)], axis=1
            )
        scs[j][kk] = s
        return jnp.maximum(m, jnp.max(s.reshape(TILE // 8, 8, 2 * TILE), axis=0))

    def mix(j, q, kk, top, state):
        tot, oa, ob = state
        vt = vt_ref[two * j : two * (j + 1), pl.ds(place(q, kk), TILE)]
        w = jnp.exp2((scs[j][kk] - top) * LOG2E)
        tot = tot + jnp.sum(w.reshape(TILE // 8, 8, 2 * TILE), axis=0)
        wb = w.astype(BF16)
        oa = oa + jnp.dot(vt[:hsize], wb[:, :TILE], preferred_element_type=F32)
        ob = ob + jnp.dot(vt[hsize:], wb[:, TILE:], preferred_element_type=F32)
        return tot, oa, ob

    def phase(j, old, q, share):
        m = jnp.full((8, 2 * TILE), -BIG, F32)
        z = jnp.zeros((hsize, TILE), F32)
        state = (jnp.zeros((8, 2 * TILE), F32), z, z)
        if old is not None:
            top = jnp.max(ms[old][...], axis=0, keepdims=True)
        for kk in range(nt):
            if j is not None:
                m = scores(j, kk, share or abs(kk - nt // 2) <= 1, m)
            if old is not None:
                state = mix(old, q, kk, top, state)
        if j is not None:
            ms[j][...] = m
        if old is not None:
            tot, oa, ob = state
            tot = jnp.sum(tot, axis=0, keepdims=True)
            o = jnp.concatenate([oa / tot[:, :TILE], ob / tot[:, TILE:]], axis=0)
            o_ref[pl.ds(pl.multiple_of(q * TILE, TILE), TILE), two * old : two * (old + 1)] = o.T.astype(BF16)

    prep()
    far = tab_ref[(q0 + qi) * wide + nt]
    for share in (False, True):

        @pl.when((far != 0) == share)
        def _(share=share):
            @pl.when(qi == 0)
            def _():
                phase(0, None, 0, share)

            @pl.when(qi > 0)
            def _():
                phase(0, 1, qi - 1, share)

            phase(1, 0, qi, share)

    @pl.when(qi == nq - 1)
    def _():
        phase(None, 1, qi, False)


def out_kernel(planes, who_ref, a0, a1, a2, a3, w0, w1, w2, o_ref, w):
    me, plane = who_ref[0], who_ref[1]
    for part, place in ((w0, me), (w1.at[0], me ^ 1), (w2, me ^ 2), (w1.at[1], me ^ 3)):
        rows = part.shape[0] // planes
        for i in range(planes):
            source = lax.rem(plane + planes - i, planes)
            at = pl.multiple_of((4 * source + place) * rows, rows)
            w[pl.ds(at, rows), :] = part[i * rows : (i + 1) * rows, :]
    total = None
    for a, place in ((a0, me), (a1, me ^ 1), (a2, me ^ 2), (a3, me ^ 3)):
        cols = a.shape[1]
        part = jnp.dot(a[...], w[pl.ds(pl.multiple_of(place * cols, cols), cols), :], preferred_element_type=F32)
        total = part if total is None else total + part
    o_ref[...] = total.astype(BF16)


def in_plane(blocks):
    swap = [(0, 1), (1, 0)]
    cross = [(0, 3), (1, 2), (2, 1), (3, 0)]
    return [
        lax.ppermute(blocks[0], "core", swap),
        lax.ppermute(blocks[1], "side", swap),
        lax.ppermute(blocks[2], ("side", "core"), cross),
    ]


def work(micros):
    return pl.CostEstimate(flops=int(micros * 1.1e9), transcendentals=0, bytes_accessed=1 << 20)


def turns(block, planes):
    return [block] + [
        lax.ppermute(block, "plane", [(i, (i + s) % planes) for i in range(planes)]) for s in range(1, planes)
    ]


def local(groups, planes, tokens, w_qkv, w_out, var_bias, seg_id, var_id, time_id):
    rows, width = tokens.shape
    heads = var_bias.shape[1]
    hsize = width // heads
    cols = width // 4
    core = lax.axis_index("core")
    side = lax.axis_index("side")
    plane = lax.axis_index("plane")
    swap = [(0, 1), (1, 0)]
    cross = [(0, 3), (1, 2), (2, 1), (3, 0)]
    pair = ("plane", "side")
    native, passed, direct = [], [], []
    for p in range(planes - 1):
        native += [(2 * (p + 1), 2 * p), (2 * p + 1, 2 * (p + 1) + 1)]
        passed += [(2 * p, 2 * (p + 1)), (2 * (p + 1) + 1, 2 * p + 1)]
        direct += [(2 * p + 1, 2 * (p + 1)), (2 * (p + 1), 2 * p + 1)]

    group = lax.axis_index("groups")
    me = 2 * side + core
    wide = cols // 2
    mate = [(g, g ^ 1) for g in range(groups)]
    couple = groups % 2 == 0
    picked = pl.pallas_call(
        functools.partial(pick_kernel, width, cols, wide, 1 if couple else 2),
        out_shape=[jax.ShapeDtypeStruct((w_qkv.shape[0], (3 if couple else 6) * wide), BF16)] * 4,
        in_specs=[pl.BlockSpec(memory_space=pltpu.SMEM), pl.BlockSpec(memory_space=pltpu.VMEM)],
        out_specs=[pl.BlockSpec(memory_space=pltpu.VMEM)] * 4,
        cost_estimate=work(1),
        name="pick",
    )(jnp.stack([me, group % 2]).astype(I32), w_qkv)
    came = in_plane(picked[1:])
    plane_w = jnp.concatenate([picked[0]] + came, 0)
    w_parts = turns(plane_w, planes)
    turned = w_parts[1:]
    if couple:
        half_w = jnp.concatenate(w_parts, 0)
        w_parts = [half_w, lax.ppermute(half_w, "groups", mate)]
    else:
        w_parts = [jnp.concatenate(w_parts, 0)]

    ids = jnp.stack([seg_id, var_id, time_id], 0)
    ids = [ids] + [lax.ppermute(ids, a, to) for a, to in (("side", swap), (pair, native), (pair, direct))]
    tokens_y = lax.optimization_barrier((tokens, came, ids))[0]
    tokens_z = lax.optimization_barrier((tokens, turned))[0]
    ids = jnp.concatenate(ids, 1)
    ids = jnp.concatenate([ids, lax.ppermute(ids, "core", swap)], 1)

    cut = rows // CHUNKS
    pieces = [tokens_y[c * cut : (c + 1) * cut] for c in range(CHUNKS)]
    other = [lax.ppermute(x, "side", swap) for x in pieces]
    mine = lax.ppermute(tokens_z, pair, native)
    theirs = [lax.ppermute(x, pair, passed) for x in other]
    xs = [(0, tokens)] + [(rows + c * cut, x) for c, x in enumerate(other)]
    xs = xs + [(2 * rows, mine)] + [(3 * rows + c * cut, x) for c, x in enumerate(theirs)]
    tokens_c = lax.optimization_barrier((tokens, other))[0]
    xs = xs + [(4 * rows + at, lax.ppermute(x if at else tokens_c, "core", swap)) for at, x in xs]
    plan = tuple(at for at, _ in xs)
    xs = [x for _, x in xs]

    nk = 8 * rows
    per = rows // TILE
    nt = 4 * per + 1
    nq = 2 * per
    seg, var, time = ids
    below = jnp.where(side == 0, 3, 2)
    stream = jnp.arange(4, dtype=I32)
    there = jnp.where(stream == below, plane > 0, jnp.where(stream == 5 - below, plane < planes - 1, True))
    there = jnp.tile(there, 2)
    gone = jnp.repeat(~there, rows)
    col = lax.broadcasted_iota(I32, (1, 128), 1)
    bit0, bit1, last = TIMES, TIMES + SEG_BITS, TIMES + 2 * SEG_BITS
    one = (seg[:, None] >> jnp.clip(col - bit0, 0, 30)) & 1
    zero = 1 - ((seg[:, None] >> jnp.clip(col - bit1, 0, 30)) & 1)
    off = jnp.where(
        col < bit0,
        time[:, None] > col,
        jnp.where(col < bit1, one == 1, jnp.where(col < last, zero == 1, (col == last) & gone[:, None])),
    )
    fk = jnp.where(off, -BIG, 0.0).astype(BF16)

    def asked(a):
        return jnp.concatenate([a[0:rows], a[4 * rows : 5 * rows], a[rows : 2 * rows], a[5 * rows : 6 * rows]], 0)

    seg_q, var_q, time_q = asked(seg)[None, :], asked(var)[None, :], asked(time)[None, :]
    row = lax.broadcasted_iota(I32, (128, 1), 0)
    qone = ((seg_q >> jnp.clip(row - bit1, 0, 30)) & 1) == 1
    qzero = ((seg_q >> jnp.clip(row - bit0, 0, 30)) & 1) == 0
    on = jnp.where(row < bit0, time_q == row, jnp.where(row < bit1, qzero, jnp.where(row < last, qone, row == last)))
    fqt = jnp.where(on, 1.0, 0.0).astype(BF16)
    vk = jnp.broadcast_to(var[:, None], (nk, 128))

    qtile = jnp.arange(4 * per, dtype=I32)
    qblock = qtile // per
    q_side = jnp.where(qblock // 2 == 0, side, 1 - side)
    q_core = jnp.where(qblock % 2 == 0, core, 1 - core)
    q_win = (2 + 2 * q_side + q_core) * per + qtile % per
    k_win = q_win[:, None] - 2 * per + jnp.arange(nt, dtype=I32)[None, :]
    k_block = k_win // per
    k_token = k_block // 2
    k_stream = jnp.where(
        side == 0,
        jnp.where(k_token == 0, 3, k_token - 1),
        jnp.where(k_token == 3, 3, 2 - k_token),
    )
    k_place = (jnp.where(k_block % 2 == core, 0, 4) + k_stream) * per + k_win % per
    code = (seg * 1024 + var).reshape(nk // TILE, TILE)
    lo, hi = code.min(1), code.max(1)
    ask = jnp.concatenate([jnp.arange(per, dtype=I32) + b * per for b in (0, 4, 1, 5)])
    share = (lo[k_place] <= hi[ask][:, None]) & (hi[k_place] >= lo[ask][:, None])
    share = share & jnp.repeat(there, per)[k_place]
    share = share & (jnp.abs(jnp.arange(nt, dtype=I32) - nt // 2) > 1)[None, :]
    table = jnp.concatenate([k_place * TILE, share.any(1, keepdims=True).astype(I32)], 1).reshape(-1)
    delta = lax.dynamic_slice_in_dim(var_bias[0] - var_bias[1], (2 * side + core) * (heads // 4), heads // 4, 0)

    vm = pl.BlockSpec(memory_space=pltpu.VMEM)
    limit = pltpu.CompilerParams(vmem_limit_bytes=48 << 20)
    queries = {}
    for at, x in zip(plan, xs):
        block = at // rows
        if block in (0, 1, 4, 5):
            queries[at] = {0: 0, 4: rows, 1: 2 * rows, 5: 3 * rows}[block] + at % rows
    k, vt, qt = pl.pallas_call(
        functools.partial(project_kernel, cols, plan, queries, planes, couple),
        out_shape=[
            jax.ShapeDtypeStruct((nk, cols), BF16),
            jax.ShapeDtypeStruct((cols, nk), BF16),
            jax.ShapeDtypeStruct((cols, 4 * rows), BF16),
        ],
        in_specs=[pl.BlockSpec(memory_space=pltpu.SMEM)] + [vm] * (len(xs) + len(w_parts)),
        out_specs=[vm] * 3,
        scratch_shapes=[pltpu.VMEM((width, 3 * cols), BF16)],
        compiler_params=limit,
        cost_estimate=work(12),
        name="project",
    )(jnp.stack([me, plane, group % 2]).astype(I32), *xs, *w_parts)

    late_w, qt = lax.optimization_barrier((w_out, qt))
    wo = jnp.concatenate(turns(late_w, planes), 0)
    wo_side = lax.ppermute(wo, "side", swap)
    wo_core = lax.ppermute(jnp.stack([wo, wo_side]), "core", swap)
    wo_parts = [wo, wo_core, wo_side]

    def attend(q0):
        return pl.pallas_call(
            functools.partial(attend_kernel, hsize, q0, nq),
            out_shape=jax.ShapeDtypeStruct((2 * rows, cols), BF16),
            grid_spec=pltpu.PrefetchScalarGridSpec(
                num_scalar_prefetch=2,
                grid=(nq,),
                in_specs=[vm] * 7,
                out_specs=vm,
                scratch_shapes=[pltpu.VMEM((2 * hsize + 128, 2 * TILE), BF16)] * 2
                + [pltpu.VMEM((nt, TILE, 2 * TILE), F32)] * 2
                + [pltpu.VMEM((8, 2 * TILE), F32)] * 2,
            ),
            compiler_params=limit,
            cost_estimate=work(16),
            name="attend",
        )(table, delta, k, vt, qt, fk, fqt, vk, var_q)

    far = attend(nq)
    far_side = lax.ppermute(far[:rows], "side", swap)
    far_cross = lax.ppermute(far[rows:], ("side", "core"), cross)
    near = attend(0)
    near_core = lax.ppermute(near[rows:], "core", swap)
    return pl.pallas_call(
        functools.partial(out_kernel, planes),
        out_shape=jax.ShapeDtypeStruct((rows, width), BF16),
        in_specs=[pl.BlockSpec(memory_space=pltpu.SMEM)] + [vm] * 7,
        out_specs=vm,
        scratch_shapes=[pltpu.VMEM((width, width), BF16)],
        compiler_params=limit,
        cost_estimate=work(3),
        name="mixed",
    )(jnp.stack([me, plane]).astype(I32), near[:rows], near_core, far_side, far_cross, *wo_parts)


def solution(mesh):
    groups, ctx = mesh.shape["groups"], mesh.shape["ctx"]
    planes = ctx // 4
    mesh4 = Mesh(mesh.devices.reshape(groups, planes, 2, 2), ("groups", "plane", "side", "core"))
    toks = ("groups", "plane", "side", "core")
    par = ("plane", "side", "core")
    in_specs = (P(toks, None), P(par, None), P(par, None), P(), P(toks), P(toks), P(toks))
    return jax.shard_map(
        functools.partial(local, groups, planes), mesh=mesh4, in_specs=in_specs, out_specs=P(toks, None), check_vma=False
    )
```

time: 523 us -> 165 us (0.32)
  matrix products: 165 us -> 0 us
  other arithmetic: 134 us -> 6.72 us
  waiting for transfers between devices: 151 us -> 54.6 us
  Pallas kernels: 0 us -> 47.3 us
  local copies, waits for them, and re-layouts: 45.9 us -> 13.1 us
  starting transfers between devices: 9.23 us -> 40.9 us
  between operations: 14.1 us -> 0.51 us
    dot_general x10 -> x0, matrix products: 165 us -> none  [the longest x4 119 us: local(): jnp.einsum('hqk,khe->qhe', weight_bf, v_grp, preferred_element_type=jnp.f...]
    sub x4 -> x2, other arithmetic: 126 us -> 0.02 us  [the longest x1 0.02 us: local(): k_win = q_win[:, None] - 2 * per + jnp.arange(nt, dtype=I32)[None, :]]
    all_gather x2 -> x0, waiting for transfers between devices: 66.7 us -> none  [the longest x1 66.7 us: local(): lax.all_gather(w_qkv, 'ctx', axis=0, tiled=True)]
    pallas_call x0 -> x5, Pallas kernels: none -> 47.3 us  [the longest x2 31.6 us: attend(): pl.pallas_call(functools.partial(attend_kernel, hsize, q0, nq), out_shape...]
    ppermute x8 -> x30, starting transfers between devices: 9.19 us -> 40.9 us  [the longest x6 9.76 us: turns(): lax.ppermute(block, 'plane', [(i, (i + s) % planes) for i in range(planes)])]
    ppermute x8 -> x30, waiting for transfers between devices: 83.6 us -> 54.6 us  [the longest x6 17.7 us: turns(): lax.ppermute(block, 'plane', [(i, (i + s) % planes) for i in range(planes)])]
    slice x7 -> x5, local copies, waits for them, and re-layouts: 29.3 us -> 1.35 us  [the longest x1 1.27 us: local(): pieces = [tokens_y[c * cut:(c + 1) * cut] for c in range(CHUNKS)]]
    unnamed x31 -> x32, local copies, waits for them, and re-layouts: 12.8 us -> 2.94 us
  transfers between devices with their start and end apart: 10 -> 30, of which waited for: 5 -> 13; matrix products, arithmetic and copies ran while one was open for 64% -> 10% of each run, Pallas kernels for 0% -> 20%
where the time goes in v2:
time: 165 us; the launch traced here: 163 us
  waiting for transfers between devices  54.6 us (33%)
  Pallas kernels  47.3 us (29%)
  starting transfers between devices  40.9 us (25%)
  local copies, waits for them, and re-layouts  13.1 us (8%)
  other arithmetic  6.72 us (4%)
    pallas_call x2, Pallas kernels, attend(): pl.pallas_call(functools.partial(attend_kernel, hsize, q0, nq), out_shape...  31.6 us
    ppermute x6, waiting for transfers between devices, turns(): lax.ppermute(block, 'plane', [(i, (i + s) % planes) for i in range(planes)])  17.7 us
    pallas_call x1, Pallas kernels, local(): pl.pallas_call(functools.partial(project_kernel, cols, plan, queries, pla...  11.1 us
    ppermute x6, starting transfers between devices, turns(): lax.ppermute(block, 'plane', [(i, (i + s) % planes) for i in range(planes)])  9.76 us
    ppermute x2, waiting for transfers between devices, local(): theirs = [lax.ppermute(x, pair, passed) for x in other]  8.48 us
    ppermute x1, waiting for transfers between devices, local(): mine = lax.ppermute(tokens_z, pair, native)  7.57 us
    ppermute x2, waiting for transfers between devices, local(): other = [lax.ppermute(x, 'side', swap) for x in pieces]  6.26 us
    ppermute x1, waiting for transfers between devices, local(): far_side = lax.ppermute(far[:rows], 'side', swap)  5.9 us
  transfers between devices with their start and end apart: 30, of which 13 were waited for; matrix products, arithmetic and copies ran while one was open for 10% of the time, Pallas kernels for 20%

profile of v2, /device:TPU:1, one launch (start us, length us, event | category | flops | bytes accessed | tf_op | source)
XLA Modules:
  0.0 163.1 jit_solution(11890292900464284945)
XLA Ops:
  0.0 0.7 pad_add_fusion.1
  0.7 2.1 %collective-permute-start = (s32[3,512]{1,0:T(4,128)S(1)}, s32[3,512]{1,0:T(4,128)S(1)}, u32[]{:S(2)}, u32[]{:S(2)}) collective-permute-start(s32[3,512]{1,0:T(4,128)S(1)} %get-tuple-element.58), channel_id=1, source_target_pairs={{0,2},{2,0},{1,3},{3,1},{4,6},{6,4},{5,7},{7,5},{8,10},{10,8},{9,1... | collective-permute-start | bytes 18440 | tf_op jit(solution)/shard_map/ppermute | solution.py:233
  2.9 1.3 collective-permute-start.1
  5.5 1.8 %pick.1 = (bf16[64,384]{1,0:T(8,128)(2,1)}, bf16[64,384]{1,0:T(8,128)(2,1)}, bf16[64,384]{1,0:T(8,128)(2,1)}, bf16[64,384]{1,0:T(8,128)(2,1)}) custom-call(s32[2]{0:T(128)} %pad_add_fusion.8.who_ref, bf16[64,3072]{1,0:T(8,128)(2,1)} %w_ref.1), custom_call_target="tpu_custom_call" | custom-call | flops 1100000000 | bytes 1048576 | tf_op jit(solution)/shard_map/pick/pallas_call | solution.py:214
  7.3 1.0 collective-permute-start.4
  8.2 5.1 %collective-permute-start.5 = (bf16[64,384]{1,0:T(8,128)(2,1)}, bf16[64,384]{1,0:T(8,128)(2,1)S(1)}, u32[]{:S(2)}, u32[]{:S(2)}) collective-permute-start(bf16[64,384]{1,0:T(8,128)(2,1)} %get-tuple-element.18), channel_id=1, source_target_pairs={{0,2},{2,0},{1,3},{3,1},{4,6},{6,4},{5,7},{7,5},{8,10},{10,8},{9,1... | collective-permute-start | bytes 147464 | tf_op jit(solution)/shard_map/ppermute | solution.py:177
  13.6 0.8 constant_dynamic-update-slice_fusion.15
  15.1 1.2 gather_fusion.4
  17.1 0.8 collective-permute-done.3
  18.1 1.2 gather_fusion
  19.4 1.2 gather_fusion.2
  22.4 1.7 %collective-permute-start.9 = (bf16[256,384]{1,0:T(8,128)(2,1)S(1)}, bf16[256,384]{1,0:T(8,128)(2,1)S(1)}, u32[]{:S(2)}, u32[]{:S(2)}) collective-permute-start(bf16[256,384]{1,0:T(8,128)(2,1)S(1)} %get-tuple-element.42), channel_id=1, source_target_pairs={{0,4},{4,8},{8,12},{12,0},{1,5},{5,9},{9,13},{13,1},{2,6},{6,10},{... | collective-permute-start | bytes 589832 | tf_op jit(solution)/shard_map/ppermute | solution.py:188
  24.0 2.3 %collective-permute-start.10 = (bf16[256,384]{1,0:T(8,128)(2,1)S(1)}, bf16[256,384]{1,0:T(8,128)(2,1)S(1)}, u32[]{:S(2)}, u32[]{:S(2)}) collective-permute-start(bf16[256,384]{1,0:T(8,128)(2,1)S(1)} %get-tuple-element.42), channel_id=1, source_target_pairs={{0,8},{4,12},{8,0},{12,4},{1,9},{5,13},{9,1},{13,5},{2,10},{6,14},... | collective-permute-start | bytes 589832 | tf_op jit(solution)/shard_map/ppermute | solution.py:188
  26.4 1.1 collective-permute-start.11
  27.4 1.3 fusion.32
  28.7 1.3 collective-permute-start.7
  30.2 1.0 collective-permute-done.9
  31.3 8.7 %collective-permute-done.10 = bf16[256,384]{1,0:T(8,128)(2,1)S(1)} collective-permute-done((bf16[256,384]{1,0:T(8,128)(2,1)S(1)}, bf16[256,384]{1,0:T(8,128)(2,1)S(1)}, u32[]{:S(2)}, u32[]{:S(2)}) %collective-permute-start.10) | collective-permute-done | bytes 196640 | tf_op jit(solution)/shard_map/ppermute | solution.py:188
  39.9 1.3 collective-permute-start.12
  41.3 1.3 collective-permute-start.21
  42.6 3.6 %select_convert_fusion.fk_ref = bf16[4096,128]{1,0:T(8,128)(2,1)S(1)} fusion(s32[128]{0:T(128)S(1)} %get-tuple-element.64, s32[128]{0:T(128)S(1)} %get-tuple-element.65, s32[4096]{0:T(1024)S(1)} %bitcast.44, s32[4096]{0:T(1024)S(1)} %bitcast.43, pred[128]{0:T(512)(128)(4,1)S(1)} %get-tuple-element.62, pred[128]{0:T(512)(128)(4,1)S(1)} %get-tuple-element.63, ...), kind=kLoop, calls=%fused_computation.5 | loop fusion | flops 7340032 | bytes 1086976 | tf_op jit(solution)/shard_map/convert_element_type | solution.py:270
  46.2 6.3 %collective-permute-done.8.refs_2_ = bf16[256,1024]{1,0:T(8,128)(2,1)} collective-permute-done((bf16[256,1024]{1,0:T(8,128)(2,1)S(1)}, bf16[256,1024]{1,0:T(8,128)(2,1)}, u32[]{:S(2)}, u32[]{:S(2)}) %collective-permute-start.8) | collective-permute-done | bytes 524320 | tf_op jit(solution)/shard_map/ppermute | solution.py:241
  52.5 2.0 %collective-permute-start.15 = (bf16[512,1024]{1,0:T(8,128)(2,1)}, bf16[512,1024]{1,0:T(8,128)(2,1)}, u32[]{:S(2)}, u32[]{:S(2)}) collective-permute-start(bf16[512,1024]{1,0:T(8,128)(2,1)} %refs_0_.1), channel_id=1, source_target_pairs={{0,1},{1,0},{2,3},{3,2},{4,5},{5,4},{6,7},{7,6},{8,9},{9,8},{10,11... | collective-permute-start | bytes 3145736 | tf_op jit(solution)/shard_map/ppermute | solution.py:247
  54.4 3.1 %collective-permute-start.13 = (bf16[256,1024]{1,0:T(8,128)(2,1)S(1)}, bf16[256,1024]{1,0:T(8,128)(2,1)}, u32[]{:S(2)}, u32[]{:S(2)}) collective-permute-start(bf16[256,1024]{1,0:T(8,128)(2,1)S(1)} %collective-permute-done.7.refs_1_), channel_id=1, source_target_pairs={{0,4},{6,2},{4,8},{10,6},{8,12},{14,10},{1,5},{7,3},{5,9},{11,7},{... | collective-permute-start | bytes 1572872 | tf_op jit(solution)/shard_map/ppermute | solution.py:243
  57.6 2.1 %collective-permute-start.14 = (bf16[256,1024]{1,0:T(8,128)(2,1)}, bf16[256,1024]{1,0:T(8,128)(2,1)}, u32[]{:S(2)}, u32[]{:S(2)}) collective-permute-start(bf16[256,1024]{1,0:T(8,128)(2,1)} %collective-permute-done.8.refs_2_), channel_id=1, source_target_pairs={{0,4},{6,2},{4,8},{10,6},{8,12},{14,10},{1,5},{7,3},{5,9},{11,7},{... | collective-permute-start | bytes 1572872 | tf_op jit(solution)/shard_map/ppermute | solution.py:243
  60.0 1.3 collective-permute-start.16
  61.4 0.8 copy-done
  62.1 7.6 %collective-permute-done.12.refs_3_ = bf16[512,1024]{1,0:T(8,128)(2,1)} collective-permute-done((bf16[512,1024]{1,0:T(8,128)(2,1)}, bf16[512,1024]{1,0:T(8,128)(2,1)}, u32[]{:S(2)}, u32[]{:S(2)}) %collective-permute-start.12) | collective-permute-done | bytes 1048608 | tf_op jit(solution)/shard_map/ppermute | solution.py:242
  69.7 1.0 collective-permute-start.18
  70.9 8.5 %collective-permute-done.14.refs_5_ = bf16[256,1024]{1,0:T(8,128)(2,1)} collective-permute-done((bf16[256,1024]{1,0:T(8,128)(2,1)}, bf16[256,1024]{1,0:T(8,128)(2,1)}, u32[]{:S(2)}, u32[]{:S(2)}) %collective-permute-start.14) | collective-permute-done | bytes 524320 | tf_op jit(solution)/shard_map/ppermute | solution.py:243
  79.4 0.8 collective-permute-start.19
  80.9 1.0 collective-permute-done.19.refs_10_
  82.0 0.7 collective-permute-done.20.refs_11_
  82.7 1.0 copy-done.1
  83.7 11.1 %project.1 = (bf16[4096,256]{1,0:T(8,128)(2,1)}, bf16[256,4096]{1,0:T(8,128)(2,1)}, bf16[256,2048]{1,0:T(8,128)(2,1)}) custom-call(s32[3]{0:T(128)S(1)} %pad_add_fusion.7.who_ref, bf16[512,1024]{1,0:T(8,128)(2,1)} %refs_0_.1, bf16[256,1024]{1,0:T(8,128)(2,1)S(1)} %copy-done.1, bf16[256,1024]{1,0:T(8,128)(2,1)} %collective-permute-done.8.refs_2_, ...), custom_call_target="tpu_custom_call" | custom-call | flops 13200000000 | bytes 1048576 | tf_op jit(solution)/shard_map/project/pallas_call | solution.py:313
  94.8 2.3 %collective-permute-start.25 = (bf16[64,1024]{1,0:T(8,128)(2,1)S(1)}, bf16[64,1024]{1,0:T(8,128)(2,1)S(1)}, u32[]{:S(2)}, u32[]{:S(2)}) collective-permute-start(bf16[64,1024]{1,0:T(8,128)(2,1)S(1)} %copy-done.4), channel_id=1, source_target_pairs={{0,4},{4,8},{8,12},{12,0},{1,5},{5,9},{9,13},{13,1},{2,6},{6,10},{... | collective-permute-start | bytes 393224 | tf_op jit(solution)/shard_map/ppermute | solution.py:188
  97.3 2.3 %collective-permute-start.27 = (bf16[64,1024]{1,0:T(8,128)(2,1)S(1)}, bf16[64,1024]{1,0:T(8,128)(2,1)S(1)}, u32[]{:S(2)}, u32[]{:S(2)}) collective-permute-start(bf16[64,1024]{1,0:T(8,128)(2,1)S(1)} %copy-done.4), channel_id=1, source_target_pairs={{0,12},{4,0},{8,4},{12,8},{1,13},{5,1},{9,5},{13,9},{2,14},{6,2},{... | collective-permute-start | bytes 393224 | tf_op jit(solution)/shard_map/ppermute | solution.py:188
  99.7 1.7 %collective-permute-done.25 = bf16[64,1024]{1,0:T(8,128)(2,1)S(1)} collective-permute-done((bf16[64,1024]{1,0:T(8,128)(2,1)S(1)}, bf16[64,1024]{1,0:T(8,128)(2,1)S(1)}, u32[]{:S(2)}, u32[]{:S(2)}) %collective-permute-start.25) | collective-permute-done | bytes 131104 | tf_op jit(solution)/shard_map/ppermute | solution.py:188
  101.4 6.3 %collective-permute-done.26 = bf16[64,1024]{1,0:T(8,128)(2,1)S(1)} collective-permute-done((bf16[64,1024]{1,0:T(8,128)(2,1)S(1)}, bf16[64,1024]{1,0:T(8,128)(2,1)S(1)}, u32[]{:S(2)}, u32[]{:S(2)}) %collective-permute-start.26) | collective-permute-done | bytes 131104 | tf_op jit(solution)/shard_map/ppermute | solution.py:188
  107.7 1.8 %collective-permute-start.28 = (bf16[256,1024]{1,0:T(8,128)(2,1)S(1)}, bf16[256,1024]{1,0:T(8,128)(2,1)S(1)}, u32[]{:S(2)}, u32[]{:S(2)}) collective-permute-start(bf16[256,1024]{1,0:T(8,128)(2,1)S(1)} %constant_dynamic-update-slice_fusion.16.w0), channel_id=1, source_target_pairs={{0,2},{2,0},{1,3},{3,1},{4,6},{6,4},{5,7},{7,5},{8,10},{10,8},{9,1... | collective-permute-start | bytes 1572872 | tf_op jit(solution)/shard_map/ppermute | solution.py:330
  109.5 2.9 %broadcast_in_dim.158.vk_ref = s32[4096,128]{1,0:T(8,128)} broadcast(s32[4096]{0:T(1024)S(1)} %bitcast.42), dimensions={0} | broadcast | bytes 2113536 | tf_op jit(solution)/shard_map/broadcast_in_dim | solution.py:281
  112.4 15.9 %attend.3 = bf16[1024,256]{1,0:T(8,128)(2,1)S(1)} custom-call(s32[80]{0:T(128)S(1)} %reshape.484.tab_ref, f32[4]{0:T(128)S(1)} %dynamic-slice_bitcast_fusion.delta_ref, bf16[4096,256]{1,0:T(8,128)(2,1)S(1)} %copy-done.2, bf16[256,4096]{1,0:T(8,128)(2,1)} %get-tuple-element.25.vt_ref, bf16[256,2048]{1,0:T(8,128)(2,1)S(1)} %copy-done.3, ...), custom_call_target="tpu_custom_call" | custom-call | flops 17600000000 | bytes 1048576 | tf_op jit(solution)/shard_map/attend/pallas_call | solution.py:335
  128.5 2.2 %collective-permute-start.29 = (bf16[2,256,1024]{2,1,0:T(8,128)(2,1)S(1)}, bf16[2,256,1024]{2,1,0:T(8,128)(2,1)S(1)}, u32[]{:S(2)}, u32[]{:S(2)}) collective-permute-start(bf16[2,256,1024]{2,1,0:T(8,128)(2,1)S(1)} %pad_maximum_fusion), channel_id=1, source_target_pairs={{0,1},{1,0},{2,3},{3,2},{4,5},{5,4},{6,7},{7,6},{8,9},{9,8},{10,11... | collective-permute-start | bytes 3145736 | tf_op jit(solution)/shard_map/ppermute | solution.py:331
  130.7 15.7 %attend.2 = bf16[1024,256]{1,0:T(8,128)(2,1)S(1)} custom-call(s32[80]{0:T(128)S(1)} %reshape.484.tab_ref, f32[4]{0:T(128)S(1)} %dynamic-slice_bitcast_fusion.delta_ref, bf16[4096,256]{1,0:T(8,128)(2,1)S(1)} %copy-done.2, bf16[256,4096]{1,0:T(8,128)(2,1)} %get-tuple-element.25.vt_ref, bf16[256,2048]{1,0:T(8,128)(2,1)S(1)} %copy-done.3, ...), custom_call_target="tpu_custom_call" | custom-call | flops 17600000000 | bytes 1048576 | tf_op jit(solution)/shard_map/attend/pallas_call | solution.py:335
  146.5 1.6 %collective-permute-start.24 = (bf16[512,256]{1,0:T(8,128)(2,1)S(1)}, bf16[512,256]{1,0:T(8,128)(2,1)S(1)}, u32[]{:S(2)}, u32[]{:S(2)}) collective-permute-start(bf16[512,256]{1,0:T(8,128)(2,1)S(1)} %get-tuple-element.33), channel_id=1, source_target_pairs={{0,3},{1,2},{2,1},{3,0},{4,7},{5,6},{6,5},{7,4},{8,11},{9,10},{10,... | collective-permute-start | bytes 786440 | tf_op jit(solution)/shard_map/ppermute | solution.py:354
  148.6 5.9 %collective-permute-done.23.a2 = bf16[512,256]{1,0:T(8,128)(2,1)S(1)} collective-permute-done((bf16[512,256]{1,0:T(8,128)(2,1)S(1)}, bf16[512,256]{1,0:T(8,128)(2,1)S(1)}, u32[]{:S(2)}, u32[]{:S(2)}) %collective-permute-start.23) | collective-permute-done | bytes 262176 | tf_op jit(solution)/shard_map/ppermute | solution.py:353
  154.5 5.7 %collective-permute-done.24.a3 = bf16[512,256]{1,0:T(8,128)(2,1)S(1)} collective-permute-done((bf16[512,256]{1,0:T(8,128)(2,1)S(1)}, bf16[512,256]{1,0:T(8,128)(2,1)S(1)}, u32[]{:S(2)}, u32[]{:S(2)}) %collective-permute-start.24) | collective-permute-done | bytes 262176 | tf_op jit(solution)/shard_map/ppermute | solution.py:354
  160.2 2.9 %mixed.1 = bf16[512,1024]{1,0:T(8,128)(2,1)} custom-call(s32[2]{0:T(128)S(1)} %pad_add_fusion.6.who_ref, bf16[512,256]{1,0:T(8,128)(2,1)S(1)} %get-tuple-element.36.a0, bf16[512,256]{1,0:T(8,128)(2,1)S(1)} %collective-permute-done.22.a1, bf16[512,256]{1,0:T(8,128)(2,1)S(1)} %collective-permute-done.23.a2, bf16[512,256]{1,0:T(8,128)(2,1)S(1)} %collective-permute-done.24.a3, ...), custom_call_target="tpu_custom_call" | custom-call | flops 3300000000 | bytes 1048576 | tf_op jit(solution)/shard_map/mixed/pallas_call | solution.py:357
  (106 shorter events, 7.3 us)
Async XLA Ops:
  0.7 15.7 %collective-permute-start = (s32[3,512]{1,0:T(4,128)S(1)}, s32[3,512]{1,0:T(4,128)S(1)}, u32[]{:S(2)}, u32[]{:S(2)}) collective-permute-start(s32[3,512]{1,0:T(4,128)S(1)} %get-tuple-element.58), channel_id=1, source_target_pairs={{0,2},{2,0},{1,3},{3,1},{4,6},{6,4},{5,7},{7,5},{8,10},{10,8},{9,1... | collective-permute-start | bytes 18440 | tf_op jit(solution)/shard_map/ppermute | solution.py:233
  2.9 13.7 %collective-permute-start.1 = (s32[3,512]{1,0:T(4,128)S(1)}, s32[3,512]{1,0:T(4,128)S(1)}, u32[]{:S(2)}, u32[]{:S(2)}) collective-permute-start(s32[3,512]{1,0:T(4,128)S(1)} %get-tuple-element.58), channel_id=1, source_target_pairs={{4,0},{2,6},{8,4},{6,10},{12,8},{10,14},{5,1},{3,7},{9,5},{7,11},{... | collective-permute-start | bytes 18440 | tf_op jit(solution)/shard_map/ppermute | solution.py:233
  4.2 12.4 %collective-permute-start.2 = (s32[3,512]{1,0:T(4,128)S(1)}, s32[3,512]{1,0:T(4,128)S(1)}, u32[]{:S(2)}, u32[]{:S(2)}) collective-permute-start(s32[3,512]{1,0:T(4,128)S(1)} %get-tuple-element.58), channel_id=1, source_target_pairs={{2,4},{4,2},{6,8},{8,6},{10,12},{12,10},{3,5},{5,3},{7,9},{9,7},{1... | collective-permute-start | bytes 18440 | tf_op jit(solution)/shard_map/ppermute | solution.py:233
  5.5 9.3 %copy-start.8 = (f32[2,16]{1,0:T(2,128)S(1)}, f32[2,16]{1,0:T(2,128)}, u32[]{:S(2)}) copy-start(f32[2,16]{1,0:T(2,128)} %param.10) | copy-start | bytes 388
  5.5 11.1 %copy-start.5 = (s32[512]{0:T(512)S(1)}, s32[512]{0:T(512)}, u32[]{:S(2)}) copy-start(s32[512]{0:T(512)} %param.13) | copy-start | bytes 6148
  5.5 11.1 %copy-start.6 = (s32[512]{0:T(512)S(1)}, s32[512]{0:T(512)}, u32[]{:S(2)}) copy-start(s32[512]{0:T(512)} %param.11) | copy-start | bytes 6148
  5.5 11.1 %copy-start.7 = (s32[512]{0:T(512)S(1)}, s32[512]{0:T(512)}, u32[]{:S(2)}) copy-start(s32[512]{0:T(512)} %param.12) | copy-start | bytes 6148
  7.3 15.0 %collective-permute-start.4 = (bf16[64,384]{1,0:T(8,128)(2,1)}, bf16[64,384]{1,0:T(8,128)(2,1)S(1)}, u32[]{:S(2)}, u32[]{:S(2)}) collective-permute-start(bf16[64,384]{1,0:T(8,128)(2,1)} %get-tuple-element.17), channel_id=1, source_target_pairs={{0,1},{1,0},{2,3},{3,2},{4,5},{5,4},{6,7},{7,6},{8,9},{9,8},{10,11... | collective-permute-start | bytes 147464 | tf_op jit(solution)/shard_map/ppermute | solution.py:176
  8.2 14.1 %collective-permute-start.5 = (bf16[64,384]{1,0:T(8,128)(2,1)}, bf16[64,384]{1,0:T(8,128)(2,1)S(1)}, u32[]{:S(2)}, u32[]{:S(2)}) collective-permute-start(bf16[64,384]{1,0:T(8,128)(2,1)} %get-tuple-element.18), channel_id=1, source_target_pairs={{0,2},{2,0},{1,3},{3,1},{4,6},{6,4},{5,7},{7,5},{8,10},{10,8},{9,1... | collective-permute-start | bytes 147464 | tf_op jit(solution)/shard_map/ppermute | solution.py:177
  16.5 5.9 %collective-permute-start.6 = (bf16[64,384]{1,0:T(8,128)(2,1)}, bf16[64,384]{1,0:T(8,128)(2,1)S(1)}, u32[]{:S(2)}, u32[]{:S(2)}) collective-permute-start(bf16[64,384]{1,0:T(8,128)(2,1)} %get-tuple-element.19), channel_id=1, source_target_pairs={{0,3},{1,2},{2,1},{3,0},{4,7},{5,6},{6,5},{7,4},{8,11},{9,10},{10,... | collective-permute-start | bytes 147464 | tf_op jit(solution)/shard_map/ppermute | solution.py:178
  16.6 1.3 collective-permute-start.3
  22.4 8.9 %collective-permute-start.9 = (bf16[256,384]{1,0:T(8,128)(2,1)S(1)}, bf16[256,384]{1,0:T(8,128)(2,1)S(1)}, u32[]{:S(2)}, u32[]{:S(2)}) collective-permute-start(bf16[256,384]{1,0:T(8,128)(2,1)S(1)} %get-tuple-element.42), channel_id=1, source_target_pairs={{0,4},{4,8},{8,12},{12,0},{1,5},{5,9},{9,13},{13,1},{2,6},{6,10},{... | collective-permute-start | bytes 589832 | tf_op jit(solution)/shard_map/ppermute | solution.py:188
  24.0 15.9 %collective-permute-start.10 = (bf16[256,384]{1,0:T(8,128)(2,1)S(1)}, bf16[256,384]{1,0:T(8,128)(2,1)S(1)}, u32[]{:S(2)}, u32[]{:S(2)}) collective-permute-start(bf16[256,384]{1,0:T(8,128)(2,1)S(1)} %get-tuple-element.42), channel_id=1, source_target_pairs={{0,8},{4,12},{8,0},{12,4},{1,9},{5,13},{9,1},{13,5},{2,10},{6,14},... | collective-permute-start | bytes 589832 | tf_op jit(solution)/shard_map/ppermute | solution.py:188
  26.4 13.6 %collective-permute-start.11 = (bf16[256,384]{1,0:T(8,128)(2,1)S(1)}, bf16[256,384]{1,0:T(8,128)(2,1)S(1)}, u32[]{:S(2)}, u32[]{:S(2)}) collective-permute-start(bf16[256,384]{1,0:T(8,128)(2,1)S(1)} %get-tuple-element.42), channel_id=1, source_target_pairs={{0,12},{4,0},{8,4},{12,8},{1,13},{5,1},{9,5},{13,9},{2,14},{6,2},{... | collective-permute-start | bytes 589832 | tf_op jit(solution)/shard_map/ppermute | solution.py:188
  28.7 17.5 %collective-permute-start.7 = (bf16[256,1024]{1,0:T(8,128)(2,1)S(1)}, bf16[256,1024]{1,0:T(8,128)(2,1)S(1)}, u32[]{:S(2)}, u32[]{:S(2)}) collective-permute-start(bf16[256,1024]{1,0:T(8,128)(2,1)S(1)} %get-tuple-element.32), channel_id=1, source_target_pairs={{0,2},{2,0},{1,3},{3,1},{4,6},{6,4},{5,7},{7,5},{8,10},{10,8},{9,1... | collective-permute-start | bytes 1572872 | tf_op jit(solution)/shard_map/ppermute | solution.py:241
  30.0 22.5 %collective-permute-start.8 = (bf16[256,1024]{1,0:T(8,128)(2,1)S(1)}, bf16[256,1024]{1,0:T(8,128)(2,1)}, u32[]{:S(2)}, u32[]{:S(2)}) collective-permute-start(bf16[256,1024]{1,0:T(8,128)(2,1)S(1)} %get-tuple-element.31), channel_id=1, source_target_pairs={{0,2},{2,0},{1,3},{3,1},{4,6},{6,4},{5,7},{7,5},{8,10},{10,8},{9,1... | collective-permute-start | bytes 1572872 | tf_op jit(solution)/shard_map/ppermute | solution.py:241
  39.9 29.8 %collective-permute-start.12 = (bf16[512,1024]{1,0:T(8,128)(2,1)}, bf16[512,1024]{1,0:T(8,128)(2,1)}, u32[]{:S(2)}, u32[]{:S(2)}) collective-permute-start(bf16[512,1024]{1,0:T(8,128)(2,1)} %refs_0_.1), channel_id=1, source_target_pairs={{4,0},{2,6},{8,4},{6,10},{12,8},{10,14},{5,1},{3,7},{9,5},{7,11},{... | collective-permute-start | bytes 3145736 | tf_op jit(solution)/shard_map/ppermute | solution.py:242
  41.3 18.7 %collective-permute-start.21 = (bf16[1024,384]{1,0:T(8,128)(2,1)S(1)}, bf16[1024,384]{1,0:T(8,128)(2,1)S(1)}, u32[]{:S(2)}, u32[]{:S(2)}) collective-permute-start(bf16[1024,384]{1,0:T(8,128)(2,1)S(1)} %constant_dynamic-update-slice_fusion.9.refs_12_), channel_id=1, source_target_pairs={{0,16},{16,0},{1,17},{17,1},{2,18},{18,2},{3,19},{19,3},{4,20},{20... | collective-permute-start | bytes 2359304 | tf_op jit(solution)/shard_map/ppermute | solution.py:228
  52.5 28.5 %collective-permute-start.15 = (bf16[512,1024]{1,0:T(8,128)(2,1)}, bf16[512,1024]{1,0:T(8,128)(2,1)}, u32[]{:S(2)}, u32[]{:S(2)}) collective-permute-start(bf16[512,1024]{1,0:T(8,128)(2,1)} %refs_0_.1), channel_id=1, source_target_pairs={{0,1},{1,0},{2,3},{3,2},{4,5},{5,4},{6,7},{7,6},{8,9},{9,8},{10,11... | collective-permute-start | bytes 3145736 | tf_op jit(solution)/shard_map/ppermute | solution.py:247
  54.4 16.4 %collective-permute-start.13 = (bf16[256,1024]{1,0:T(8,128)(2,1)S(1)}, bf16[256,1024]{1,0:T(8,128)(2,1)}, u32[]{:S(2)}, u32[]{:S(2)}) collective-permute-start(bf16[256,1024]{1,0:T(8,128)(2,1)S(1)} %collective-permute-done.7.refs_1_), channel_id=1, source_target_pairs={{0,4},{6,2},{4,8},{10,6},{8,12},{14,10},{1,5},{7,3},{5,9},{11,7},{... | collective-permute-start | bytes 1572872 | tf_op jit(solution)/shard_map/ppermute | solution.py:243
  57.6 21.9 %collective-permute-start.14 = (bf16[256,1024]{1,0:T(8,128)(2,1)}, bf16[256,1024]{1,0:T(8,128)(2,1)}, u32[]{:S(2)}, u32[]{:S(2)}) collective-permute-start(bf16[256,1024]{1,0:T(8,128)(2,1)} %collective-permute-done.8.refs_2_), channel_id=1, source_target_pairs={{0,4},{6,2},{4,8},{10,6},{8,12},{14,10},{1,5},{7,3},{5,9},{11,7},{... | collective-permute-start | bytes 1572872 | tf_op jit(solution)/shard_map/ppermute | solution.py:243
  60.0 20.2 %collective-permute-start.16 = (bf16[256,1024]{1,0:T(8,128)(2,1)S(1)}, bf16[256,1024]{1,0:T(8,128)(2,1)}, u32[]{:S(2)}, u32[]{:S(2)}) collective-permute-start(bf16[256,1024]{1,0:T(8,128)(2,1)S(1)} %collective-permute-done.7.refs_1_), channel_id=1, source_target_pairs={{0,1},{1,0},{2,3},{3,2},{4,5},{5,4},{6,7},{7,6},{8,9},{9,8},{10,11... | collective-permute-start | bytes 1572872 | tf_op jit(solution)/shard_map/ppermute | solution.py:247
  61.4 0.8 copy-start
  69.7 13.0 %collective-permute-start.18 = (bf16[512,1024]{1,0:T(8,128)(2,1)}, bf16[512,1024]{1,0:T(8,128)(2,1)}, u32[]{:S(2)}, u32[]{:S(2)}) collective-permute-start(bf16[512,1024]{1,0:T(8,128)(2,1)} %collective-permute-done.12.refs_3_), channel_id=1, source_target_pairs={{0,1},{1,0},{2,3},{3,2},{4,5},{5,4},{6,7},{7,6},{8,9},{9,8},{10,11... | collective-permute-start | bytes 3145736 | tf_op jit(solution)/shard_map/ppermute | solution.py:247
  70.9 10.0 %collective-permute-start.17 = (bf16[256,1024]{1,0:T(8,128)(2,1)}, bf16[256,1024]{1,0:T(8,128)(2,1)S(1)}, u32[]{:S(2)}, u32[]{:S(2)}) collective-permute-start(bf16[256,1024]{1,0:T(8,128)(2,1)} %collective-permute-done.8.refs_2_), channel_id=1, source_target_pairs={{0,1},{1,0},{2,3},{3,2},{4,5},{5,4},{6,7},{7,6},{8,9},{9,8},{10,11... | collective-permute-start | bytes 1572872 | tf_op jit(solution)/shard_map/ppermute | solution.py:247
  79.4 2.5 %collective-permute-start.19 = (bf16[256,1024]{1,0:T(8,128)(2,1)}, bf16[256,1024]{1,0:T(8,128)(2,1)S(1)}, u32[]{:S(2)}, u32[]{:S(2)}) collective-permute-start(bf16[256,1024]{1,0:T(8,128)(2,1)} %collective-permute-done.13.refs_4_), channel_id=1, source_target_pairs={{0,1},{1,0},{2,3},{3,2},{4,5},{5,4},{6,7},{7,6},{8,9},{9,8},{10,11... | collective-permute-start | bytes 1572872 | tf_op jit(solution)/shard_map/ppermute | solution.py:247
  80.2 2.5 %collective-permute-start.20 = (bf16[256,1024]{1,0:T(8,128)(2,1)}, bf16[256,1024]{1,0:T(8,128)(2,1)S(1)}, u32[]{:S(2)}, u32[]{:S(2)}) collective-permute-start(bf16[256,1024]{1,0:T(8,128)(2,1)} %collective-permute-done.14.refs_5_), channel_id=1, source_target_pairs={{0,1},{1,0},{2,3},{3,2},{4,5},{5,4},{6,7},{7,6},{8,9},{9,8},{10,11... | collective-permute-start | bytes 1572872 | tf_op jit(solution)/shard_map/ppermute | solution.py:247
  80.2 14.6 %copy-start.4 = (bf16[64,1024]{1,0:T(8,128)(2,1)S(1)}, bf16[64,1024]{1,0:T(8,128)(2,1)}, u32[]{:S(2)}) copy-start(bf16[64,1024]{1,0:T(8,128)(2,1)} %param.9) | copy-start | bytes 393220
  82.7 1.0 copy-start.1
  94.8 17.6 %copy-start.3 = (bf16[256,2048]{1,0:T(8,128)(2,1)S(1)}, bf16[256,2048]{1,0:T(8,128)(2,1)}, u32[]{:S(2)}) copy-start(bf16[256,2048]{1,0:T(8,128)(2,1)} %get-tuple-element.27.qt_ref) | copy-start | bytes 3145732
  94.8 6.6 %collective-permute-start.25 = (bf16[64,1024]{1,0:T(8,128)(2,1)S(1)}, bf16[64,1024]{1,0:T(8,128)(2,1)S(1)}, u32[]{:S(2)}, u32[]{:S(2)}) collective-permute-start(bf16[64,1024]{1,0:T(8,128)(2,1)S(1)} %copy-done.4), channel_id=1, source_target_pairs={{0,4},{4,8},{8,12},{12,0},{1,5},{5,9},{9,13},{13,1},{2,6},{6,10},{... | collective-permute-start | bytes 393224 | tf_op jit(solution)/shard_map/ppermute | solution.py:188
  97.2 15.2 %copy-start.2 = (bf16[4096,256]{1,0:T(8,128)(2,1)S(1)}, bf16[4096,256]{1,0:T(8,128)(2,1)}, u32[]{:S(2)}) copy-start(bf16[4096,256]{1,0:T(8,128)(2,1)} %get-tuple-element.24.k_ref) | copy-start | bytes 6291460
  97.2 10.5 %collective-permute-start.26 = (bf16[64,1024]{1,0:T(8,128)(2,1)S(1)}, bf16[64,1024]{1,0:T(8,128)(2,1)S(1)}, u32[]{:S(2)}, u32[]{:S(2)}) collective-permute-start(bf16[64,1024]{1,0:T(8,128)(2,1)S(1)} %copy-done.4), channel_id=1, source_target_pairs={{0,8},{4,12},{8,0},{12,4},{1,9},{5,13},{9,1},{13,5},{2,10},{6,14},... | collective-permute-start | bytes 393224 | tf_op jit(solution)/shard_map/ppermute | solution.py:188
  97.3 10.4 %collective-permute-start.27 = (bf16[64,1024]{1,0:T(8,128)(2,1)S(1)}, bf16[64,1024]{1,0:T(8,128)(2,1)S(1)}, u32[]{:S(2)}, u32[]{:S(2)}) collective-permute-start(bf16[64,1024]{1,0:T(8,128)(2,1)S(1)} %copy-done.4), channel_id=1, source_target_pairs={{0,12},{4,0},{8,4},{12,8},{1,13},{5,1},{9,5},{13,9},{2,14},{6,2},{... | collective-permute-start | bytes 393224 | tf_op jit(solution)/shard_map/ppermute | solution.py:188
  107.7 20.6 %collective-permute-start.28 = (bf16[256,1024]{1,0:T(8,128)(2,1)S(1)}, bf16[256,1024]{1,0:T(8,128)(2,1)S(1)}, u32[]{:S(2)}, u32[]{:S(2)}) collective-permute-start(bf16[256,1024]{1,0:T(8,128)(2,1)S(1)} %constant_dynamic-update-slice_fusion.16.w0), channel_id=1, source_target_pairs={{0,2},{2,0},{1,3},{3,1},{4,6},{6,4},{5,7},{7,5},{8,10},{10,8},{9,1... | collective-permute-start | bytes 1572872 | tf_op jit(solution)/shard_map/ppermute | solution.py:330
  128.5 31.7 %collective-permute-start.29 = (bf16[2,256,1024]{2,1,0:T(8,128)(2,1)S(1)}, bf16[2,256,1024]{2,1,0:T(8,128)(2,1)S(1)}, u32[]{:S(2)}, u32[]{:S(2)}) collective-permute-start(bf16[2,256,1024]{2,1,0:T(8,128)(2,1)S(1)} %pad_maximum_fusion), channel_id=1, source_target_pairs={{0,1},{1,0},{2,3},{3,2},{4,5},{5,4},{6,7},{7,6},{8,9},{9,8},{10,11... | collective-permute-start | bytes 3145736 | tf_op jit(solution)/shard_map/ppermute | solution.py:331
  146.4 8.0 %collective-permute-start.23 = (bf16[512,256]{1,0:T(8,128)(2,1)S(1)}, bf16[512,256]{1,0:T(8,128)(2,1)S(1)}, u32[]{:S(2)}, u32[]{:S(2)}) collective-permute-start(bf16[512,256]{1,0:T(8,128)(2,1)S(1)} %get-tuple-element.34), channel_id=1, source_target_pairs={{0,2},{2,0},{1,3},{3,1},{4,6},{6,4},{5,7},{7,5},{8,10},{10,8},{9,1... | collective-permute-start | bytes 786440 | tf_op jit(solution)/shard_map/ppermute | solution.py:353
  146.5 13.7 %collective-permute-start.24 = (bf16[512,256]{1,0:T(8,128)(2,1)S(1)}, bf16[512,256]{1,0:T(8,128)(2,1)S(1)}, u32[]{:S(2)}, u32[]{:S(2)}) collective-permute-start(bf16[512,256]{1,0:T(8,128)(2,1)S(1)} %get-tuple-element.33), channel_id=1, source_target_pairs={{0,3},{1,2},{2,1},{3,0},{4,7},{5,6},{6,5},{7,4},{8,11},{9,10},{10,... | collective-permute-start | bytes 786440 | tf_op jit(solution)/shard_map/ppermute | solution.py:354
  148.2 12.0 %collective-permute-start.22 = (bf16[512,256]{1,0:T(8,128)(2,1)S(1)}, bf16[512,256]{1,0:T(8,128)(2,1)S(1)}, u32[]{:S(2)}, u32[]{:S(2)}) collective-permute-start(bf16[512,256]{1,0:T(8,128)(2,1)S(1)} %get-tuple-element.35), channel_id=1, source_target_pairs={{0,1},{1,0},{2,3},{3,2},{4,5},{5,4},{6,7},{7,6},{8,9},{9,8},{10,11... | collective-permute-start | bytes 786440 | tf_op jit(solution)/shard_map/ppermute | solution.py:356

commit v3 on v2

--- a/solution.py
+++ b/solution.py
@@ -12,7 +12,7 @@
 TIMES = 104
 SEG_BITS = 8
 TILE = 256
-CHUNKS = 2
+ID_ROWS = 16
 LOG2E = math.log2(math.e)
 F32 = jnp.float32
 BF16 = jnp.bfloat16
@@ -49,14 +49,39 @@
                         w[pl.ds(to, rows), pl.ds(at, wide)] = block[:, a * wide : (a + 1) * wide]
                 else:
                     w[pl.ds(to, rows), :] = block
-    for x, at in zip(xs, plan):
-        rows = x.shape[0]
-        out = jnp.dot(x[...], w[...], preferred_element_type=F32)
-        k_ref[at : at + rows, :] = out[:, cols : 2 * cols].astype(BF16)
-        vt_ref[:, at : at + rows] = out[:, 2 * cols :].astype(BF16).T
+    for x, (at, rows) in zip(xs, plan):
+        out = jnp.dot(x[0:rows, :], w[:, cols:], preferred_element_type=F32)
+        k_ref[at : at + rows, :] = out[:, :cols].astype(BF16)
+        vt_ref[:, at : at + rows] = out[:, cols:].astype(BF16).T
         if at in queries:
-            q = (out[:, :cols].astype(BF16) * 0.125).astype(BF16)
+            out = jnp.dot(x[0:rows, :], w[:, :cols], preferred_element_type=F32)
+            q = (out.astype(BF16) * 0.125).astype(BF16)
             qt_ref[:, queries[at] : queries[at] + rows] = q.T
+
+
+def mask_kernel(keys_ref, asks_ref, fk_ref, vk_ref, fqt_ref):
+    bit0, bit1, last = TIMES, TIMES + SEG_BITS, TIMES + 2 * SEG_BITS
+
+    def bit(seg, row, start):
+        return (seg >> jnp.clip(row - start, 0, 30)) & 1
+
+    for at in range(0, keys_ref.shape[1], 2 * TILE):
+        n = 2 * TILE
+        seg, var, time, gone = (keys_ref[i : i + 1, at : at + n] for i in range(4))
+        row = lax.broadcasted_iota(I32, (128, n), 0)
+        late = jnp.where(time > row, 1, 0)
+        outside = jnp.where(row == last, gone, 0)
+        off = jnp.where(row < bit0, late, jnp.where(row < bit1, bit(seg, row, bit0), 0))
+        off = jnp.where((row >= bit1) & (row < last), 1 - bit(seg, row, bit1), off) + outside
+        fk_ref[at : at + n, :] = (off.astype(F32) * -BIG).T.astype(BF16)
+        vk_ref[at : at + n, :] = jnp.broadcast_to(var, (128, n)).T
+    for at in range(0, asks_ref.shape[1], 2 * TILE):
+        n = 2 * TILE
+        seg, time = asks_ref[0:1, at : at + n], asks_ref[1:2, at : at + n]
+        row = lax.broadcasted_iota(I32, (128, n), 0)
+        on = jnp.where(row < bit0, jnp.where(time == row, 1, 0), jnp.where(row < bit1, 1 - bit(seg, row, bit0), 0))
+        on = jnp.where((row >= bit1) & (row < last), bit(seg, row, bit1), on) + jnp.where(row == last, 1, 0)
+        fqt_ref[:, at : at + n] = on.astype(F32).astype(BF16)
 
 
 def attend_kernel(
@@ -223,62 +248,67 @@
     plane_w = jnp.concatenate([picked[0]] + came, 0)
     w_parts = turns(plane_w, planes)
     turned = w_parts[1:]
+    half_w = jnp.concatenate(w_parts, 0)
     if couple:
-        half_w = jnp.concatenate(w_parts, 0)
         w_parts = [half_w, lax.ppermute(half_w, "groups", mate)]
     else:
-        w_parts = [jnp.concatenate(w_parts, 0)]
-
-    ids = jnp.stack([seg_id, var_id, time_id], 0)
-    ids = [ids] + [lax.ppermute(ids, a, to) for a, to in (("side", swap), (pair, native), (pair, direct))]
-    tokens_y = lax.optimization_barrier((tokens, came, ids))[0]
-    tokens_z = lax.optimization_barrier((tokens, turned))[0]
-    ids = jnp.concatenate(ids, 1)
-    ids = jnp.concatenate([ids, lax.ppermute(ids, "core", swap)], 1)
-
-    cut = rows // CHUNKS
-    pieces = [tokens_y[c * cut : (c + 1) * cut] for c in range(CHUNKS)]
-    other = [lax.ppermute(x, "side", swap) for x in pieces]
-    mine = lax.ppermute(tokens_z, pair, native)
-    theirs = [lax.ppermute(x, pair, passed) for x in other]
-    xs = [(0, tokens)] + [(rows + c * cut, x) for c, x in enumerate(other)]
-    xs = xs + [(2 * rows, mine)] + [(3 * rows + c * cut, x) for c, x in enumerate(theirs)]
-    tokens_c = lax.optimization_barrier((tokens, other))[0]
-    xs = xs + [(4 * rows + at, lax.ppermute(x if at else tokens_c, "core", swap)) for at, x in xs]
-    plan = tuple(at for at, _ in xs)
-    xs = [x for _, x in xs]
+        w_parts = [half_w]
+
+    cut = rows // 2
+    tokens = lax.optimization_barrier((tokens, picked))[0]
+    digits = jnp.stack([seg_id, var_id >> 4, var_id & 15, time_id], 0).astype(BF16).reshape(4 * rows // width, width)
+    digits = jnp.pad(digits, ((0, ID_ROWS - digits.shape[0]), (0, 0)))
+    first = jnp.concatenate([tokens[:cut], digits], 0)
+    whole = jnp.concatenate([tokens, digits], 0)
+    first, second, _ = lax.optimization_barrier((first, tokens[cut:], came))
+    other = [lax.ppermute(x, "side", swap) for x in (first, second)]
+    first_z = lax.optimization_barrier((first, turned))[0]
+    mine = [lax.ppermute(first_z, pair, native)]
+    theirs = [lax.ppermute(other[0], pair, passed)]
+    whole, second, passing, _, _ = lax.optimization_barrier(
+        (whole, second, other[1], (mine[0], theirs[0]), w_parts)
+    )
+    mine.append(lax.ppermute(second, pair, native))
+    theirs.append(lax.ppermute(passing, pair, passed))
+    other[1] = passing
+    peers = [lax.ppermute(x, "core", swap) for x in (whole, other[0], mine[0], theirs[0])]
+
+    def ids_of(x, n):
+        return x[n : n + 4 * rows // width].reshape(4, rows).astype(I32)
+
+    ids = [ids_of(x, cut) for x in (other[0], mine[0], theirs[0])]
+    ids += [ids_of(peers[0], rows)] + [ids_of(x, cut) for x in peers[1:]]
+    seg, hi, lo, time = jnp.concatenate([ids_of(digits, 0)] + ids, 1)
+    var = hi * 16 + lo
 
     nk = 8 * rows
     per = rows // TILE
     nt = 4 * per + 1
     nq = 2 * per
-    seg, var, time = ids
     below = jnp.where(side == 0, 3, 2)
     stream = jnp.arange(4, dtype=I32)
     there = jnp.where(stream == below, plane > 0, jnp.where(stream == 5 - below, plane < planes - 1, True))
     there = jnp.tile(there, 2)
-    gone = jnp.repeat(~there, rows)
-    col = lax.broadcasted_iota(I32, (1, 128), 1)
-    bit0, bit1, last = TIMES, TIMES + SEG_BITS, TIMES + 2 * SEG_BITS
-    one = (seg[:, None] >> jnp.clip(col - bit0, 0, 30)) & 1
-    zero = 1 - ((seg[:, None] >> jnp.clip(col - bit1, 0, 30)) & 1)
-    off = jnp.where(
-        col < bit0,
-        time[:, None] > col,
-        jnp.where(col < bit1, one == 1, jnp.where(col < last, zero == 1, (col == last) & gone[:, None])),
-    )
-    fk = jnp.where(off, -BIG, 0.0).astype(BF16)
+    gone = jnp.repeat(~there, rows).astype(I32)
 
     def asked(a):
         return jnp.concatenate([a[0:rows], a[4 * rows : 5 * rows], a[rows : 2 * rows], a[5 * rows : 6 * rows]], 0)
 
-    seg_q, var_q, time_q = asked(seg)[None, :], asked(var)[None, :], asked(time)[None, :]
-    row = lax.broadcasted_iota(I32, (128, 1), 0)
-    qone = ((seg_q >> jnp.clip(row - bit1, 0, 30)) & 1) == 1
-    qzero = ((seg_q >> jnp.clip(row - bit0, 0, 30)) & 1) == 0
-    on = jnp.where(row < bit0, time_q == row, jnp.where(row < bit1, qzero, jnp.where(row < last, qone, row == last)))
-    fqt = jnp.where(on, 1.0, 0.0).astype(BF16)
-    vk = jnp.broadcast_to(var[:, None], (nk, 128))
+    var_q = asked(var)
+    keys_ids = jnp.stack([seg, var, time, gone], 0)
+    vm = pl.BlockSpec(memory_space=pltpu.VMEM)
+    fk, vk, fqt = pl.pallas_call(
+        mask_kernel,
+        out_shape=[
+            jax.ShapeDtypeStruct((nk, 128), BF16),
+            jax.ShapeDtypeStruct((nk, 128), I32),
+            jax.ShapeDtypeStruct((128, 4 * rows), BF16),
+        ],
+        in_specs=[vm] * 2,
+        out_specs=[vm] * 3,
+        cost_estimate=work(2),
+        name="masks",
+    )(keys_ids, jnp.stack([asked(seg), asked(time)], 0))
 
     qtile = jnp.arange(4 * per, dtype=I32)
     qblock = qtile // per
@@ -296,17 +326,35 @@
     k_place = (jnp.where(k_block % 2 == core, 0, 4) + k_stream) * per + k_win % per
     code = (seg * 1024 + var).reshape(nk // TILE, TILE)
     lo, hi = code.min(1), code.max(1)
-    ask = jnp.concatenate([jnp.arange(per, dtype=I32) + b * per for b in (0, 4, 1, 5)])
-    share = (lo[k_place] <= hi[ask][:, None]) & (hi[k_place] >= lo[ask][:, None])
-    share = share & jnp.repeat(there, per)[k_place]
-    share = share & (jnp.abs(jnp.arange(nt, dtype=I32) - nt // 2) > 1)[None, :]
+    tile = jnp.arange(8 * per, dtype=I32)
+    t_block = tile // per
+    t_core = jnp.where(t_block // 4 == 0, core, 1 - core)
+    t_stream = t_block % 4
+    t_token = jnp.where(side == 0, (t_stream + 1) % 4, jnp.where(t_stream == 3, 3, 2 - t_stream))
+    apart = ((2 * t_token + t_core) * per + tile % per)[None, :] - q_win[:, None]
+    apart = jnp.abs(apart)
+    hi_q = jnp.concatenate([hi[b * per : (b + 1) * per] for b in (0, 4, 1, 5)])
+    lo_q = jnp.concatenate([lo[b * per : (b + 1) * per] for b in (0, 4, 1, 5)])
+    share = (lo[None, :] <= hi_q[:, None]) & (hi[None, :] >= lo_q[:, None])
+    share = share & jnp.repeat(there, per)[None, :] & (apart > 1) & (apart <= nt // 2)
     table = jnp.concatenate([k_place * TILE, share.any(1, keepdims=True).astype(I32)], 1).reshape(-1)
     delta = lax.dynamic_slice_in_dim(var_bias[0] - var_bias[1], (2 * side + core) * (heads // 4), heads // 4, 0)
 
-    vm = pl.BlockSpec(memory_space=pltpu.VMEM)
+    who = jnp.stack([me, plane, group % 2]).astype(I32)
+    masks = (fk, fqt, vk, table)
+    rest = [lax.ppermute(passing, "core", swap)]
+    lasts, masks = lax.optimization_barrier(((mine[1], theirs[1]), masks))
+    fk, fqt, vk, table = masks
+    rest += [lax.ppermute(x, "core", swap) for x in lasts]
+    held = [(0, rows, tokens), (4 * rows, rows, peers[0])]
+    for i, (one, two) in enumerate((other, (mine[0], lasts[0]), (theirs[0], lasts[1]))):
+        held += [((i + 1) * rows, cut, one), ((i + 1) * rows + cut, cut, two)]
+        held += [((i + 5) * rows, cut, peers[i + 1]), ((i + 5) * rows + cut, cut, rest[i])]
+    plan = tuple((at, n) for at, n, _ in held)
+    xs = [x for _, _, x in held]
     limit = pltpu.CompilerParams(vmem_limit_bytes=48 << 20)
     queries = {}
-    for at, x in zip(plan, xs):
+    for at, _ in plan:
         block = at // rows
         if block in (0, 1, 4, 5):
             queries[at] = {0: 0, 4: rows, 1: 2 * rows, 5: 3 * rows}[block] + at % rows
@@ -323,13 +371,10 @@
         compiler_params=limit,
         cost_estimate=work(12),
         name="project",
-    )(jnp.stack([me, plane, group % 2]).astype(I32), *xs, *w_parts)
-
-    late_w, qt = lax.optimization_barrier((w_out, qt))
-    wo = jnp.concatenate(turns(late_w, planes), 0)
-    wo_side = lax.ppermute(wo, "side", swap)
-    wo_core = lax.ppermute(jnp.stack([wo, wo_side]), "core", swap)
-    wo_parts = [wo, wo_core, wo_side]
+    )(who, *xs, *w_parts)
+
+    late_w = lax.optimization_barrier((w_out, lasts))[0]
+    wo = turns(late_w, planes)
 
     def attend(q0):
         return pl.pallas_call(
@@ -347,13 +392,21 @@
             compiler_params=limit,
             cost_estimate=work(16),
             name="attend",
-        )(table, delta, k, vt, qt, fk, fqt, vk, var_q)
+        )(table, delta, k, vt, qt, fk, fqt, vk, var_q[None, :])
 
     far = attend(nq)
-    far_side = lax.ppermute(far[:rows], "side", swap)
-    far_cross = lax.ppermute(far[rows:], ("side", "core"), cross)
+    far_side, far_cross = far[:rows], far[rows:]
+    wo, far_side, far_cross = lax.optimization_barrier((wo, far_side, far_cross))
+    wo = jnp.concatenate(wo, 0)
+    far_side = lax.ppermute(far_side, "side", swap)
+    far_cross = lax.ppermute(far_cross, ("side", "core"), cross)
+    wo_side = lax.ppermute(wo, "side", swap)
     near = attend(0)
-    near_core = lax.ppermute(near[rows:], "core", swap)
+    near_core, near = near[rows:], near[:rows]
+    near_core, far_side, far_cross, wo_side = lax.optimization_barrier((near_core, far_side, far_cross, wo_side))
+    near_core = lax.ppermute(near_core, "core", swap)
+    wo_core = lax.ppermute(jnp.stack([wo, wo_side]), "core", swap)
+    wo_parts = [wo, wo_core, wo_side]
     return pl.pallas_call(
         functools.partial(out_kernel, planes),
         out_shape=jax.ShapeDtypeStruct((rows, width), BF16),
@@ -363,7 +416,7 @@
         compiler_params=limit,
         cost_estimate=work(3),
         name="mixed",
-    )(jnp.stack([me, plane]).astype(I32), near[:rows], near_core, far_side, far_cross, *wo_parts)
+    )(jnp.stack([me, plane]).astype(I32), near, near_core, far_side, far_cross, *wo_parts)
 
 
 def solution(mesh):

time: 165 us -> 143 us (0.87)
  waiting for transfers between devices: 54.6 us -> 34.9 us
  Pallas kernels: 47.3 us -> 51.3 us
  local copies, waits for them, and re-layouts: 13.1 us -> 10.1 us
    ppermute x18 -> x16, waiting for transfers between devices: 36.5 us -> 21.7 us  [the longest x1 6.2 us: local(): mine = [lax.ppermute(first_z, pair, native)]]
    ppermute x18 -> x16, starting transfers between devices: 19.7 us -> 27.2 us  [the longest x1 7.34 us: local(): theirs.append(lax.ppermute(passing, pair, passed))]
    ppermute x6, waiting for transfers between devices: 17.7 us -> 11 us  [turns(): lax.ppermute(block, 'plane', [(i, (i + s) % planes) for i in range(planes)])]
    gather x8 -> x0, local copies, waits for them, and re-layouts: 5.22 us -> none  [the longest x2 1.32 us: local(): share = share & jnp.repeat(there, per)[k_place]]
    unnamed x32 -> x39, local copies, waits for them, and re-layouts: 2.94 us -> 7.73 us
    pallas_call x0 -> x1, Pallas kernels: none -> 3.53 us  [local(): pl.pallas_call(mask_kernel, out_shape=[jax.ShapeDtypeStruct((nk, 128), BF...]
    broadcast_in_dim x2 -> x1, local copies, waits for them, and re-layouts: 2.99 us -> 0.07 us  [local(): jnp.repeat(there, per)[None, :]]
    convert_element_type x2 -> x9, other arithmetic: 4.25 us -> 1.5 us  [the longest x8 1.5 us: ids_of(): return x[n:n + 4 * rows // width].reshape(4, rows).astype(I32)]
  transfers between devices with their start and end apart: 30 -> 28, of which waited for: 13 -> 9; matrix products, arithmetic and copies ran while one was open for 10% -> 8% of each run, Pallas kernels for 20% -> 33%
where the time goes in v3:
time: 143 us; the launch traced here: 142 us
  Pallas kernels  51.3 us (36%)
  starting transfers between devices  40.1 us (28%)
  waiting for transfers between devices  34.9 us (24%)
  local copies, waits for them, and re-layouts  10.1 us (7%)
  other arithmetic  5.61 us (4%)
    pallas_call x2, Pallas kernels, attend(): pl.pallas_call(functools.partial(attend_kernel, hsize, q0, nq), out_shape...  32.2 us
    ppermute x6, waiting for transfers between devices, turns(): lax.ppermute(block, 'plane', [(i, (i + s) % planes) for i in range(planes)])  11 us
    pallas_call x1, Pallas kernels, local(): pl.pallas_call(functools.partial(project_kernel, cols, plan, queries, pla...  10.9 us
    ppermute x6, starting transfers between devices, turns(): lax.ppermute(block, 'plane', [(i, (i + s) % planes) for i in range(planes)])  8.37 us
    unnamed x39, local copies, waits for them, and re-layouts  7.73 us
    ppermute x1, starting transfers between devices, local(): theirs.append(lax.ppermute(passing, pair, passed))  7.34 us
    ppermute x1, starting transfers between devices, local(): theirs = [lax.ppermute(other[0], pair, passed)]  7.06 us
    ppermute x1, waiting for transfers between devices, local(): mine = [lax.ppermute(first_z, pair, native)]  6.2 us
  transfers between devices with their start and end apart: 28, of which 9 were waited for; matrix products, arithmetic and copies ran while one was open for 8% of the time, Pallas kernels for 33%

profile of v3, /device:TPU:1, one launch (start us, length us, event | category | flops | bytes accessed | tf_op | source)
XLA Modules:
  0.0 142.5 jit_solution(3609415854594212671)
XLA Ops:
  0.0 0.6 pad_add_fusion.7.who_ref
  0.7 1.8 %pick.1 = (bf16[64,384]{1,0:T(8,128)(2,1)}, bf16[64,384]{1,0:T(8,128)(2,1)}, bf16[64,384]{1,0:T(8,128)(2,1)}, bf16[64,384]{1,0:T(8,128)(2,1)}) custom-call(s32[2]{0:T(128)} %pad_add_fusion.7.who_ref, bf16[64,3072]{1,0:T(8,128)(2,1)} %w_ref.1), custom_call_target="tpu_custom_call" | custom-call | flops 1100000000 | bytes 1048576 | tf_op jit(solution)/shard_map/pick/pallas_call | solution.py:239
  2.5 2.7 %collective-permute-start.1 = (bf16[64,384]{1,0:T(8,128)(2,1)}, bf16[64,384]{1,0:T(8,128)(2,1)S(1)}, u32[]{:S(2)}, u32[]{:S(2)}) collective-permute-start(bf16[64,384]{1,0:T(8,128)(2,1)} %get-tuple-element.41), channel_id=1, source_target_pairs={{0,2},{2,0},{1,3},{3,1},{4,6},{6,4},{5,7},{7,5},{8,10},{10,8},{9,1... | collective-permute-start | bytes 147464 | tf_op jit(solution)/shard_map/ppermute | solution.py:202
  5.3 1.4 %constant_dynamic-update-slice_fusion.10 = (bf16[1024,384]{1,0:T(8,128)(2,1)}, bf16[256,384]{1,0:T(8,128)(2,1)S(1)}) fusion(bf16[64,384]{1,0:T(8,128)(2,1)} %get-tuple-element.39), kind=kLoop, calls=%fused_computation.14 | loop fusion | bytes 147456
  6.7 0.9 fusion.25
  7.6 1.1 pad_maximum_fusion
  9.3 0.6 constant_dynamic-update-slice_fusion.9
  9.9 0.6 constant_dynamic-update-slice_fusion.8
  10.5 0.6 constant_dynamic-update-slice_fusion.7
  11.2 1.7 %collective-permute-start.4 = (bf16[256,384]{1,0:T(8,128)(2,1)S(1)}, bf16[256,384]{1,0:T(8,128)(2,1)S(1)}, u32[]{:S(2)}, u32[]{:S(2)}) collective-permute-start(bf16[256,384]{1,0:T(8,128)(2,1)S(1)} %get-tuple-element.90), channel_id=1, source_target_pairs={{0,4},{4,8},{8,12},{12,0},{1,5},{5,9},{9,13},{13,1},{2,6},{6,10},{... | collective-permute-start | bytes 589832 | tf_op jit(solution)/shard_map/ppermute | solution.py:213
  12.8 2.3 %collective-permute-start.5 = (bf16[256,384]{1,0:T(8,128)(2,1)S(1)}, bf16[256,384]{1,0:T(8,128)(2,1)S(1)}, u32[]{:S(2)}, u32[]{:S(2)}) collective-permute-start(bf16[256,384]{1,0:T(8,128)(2,1)S(1)} %get-tuple-element.90), channel_id=1, source_target_pairs={{0,8},{4,12},{8,0},{12,4},{1,9},{5,13},{9,1},{13,5},{2,10},{6,14},... | collective-permute-start | bytes 589832 | tf_op jit(solution)/shard_map/ppermute | solution.py:213
  15.1 1.1 collective-permute-start.6
  16.2 1.2 collective-permute-start.8
  17.7 2.3 %collective-permute-done.4 = bf16[256,384]{1,0:T(8,128)(2,1)S(1)} collective-permute-done((bf16[256,384]{1,0:T(8,128)(2,1)S(1)}, bf16[256,384]{1,0:T(8,128)(2,1)S(1)}, u32[]{:S(2)}, u32[]{:S(2)}) %collective-permute-start.4) | collective-permute-done | bytes 196640 | tf_op jit(solution)/shard_map/ppermute | solution.py:213
  20.0 8.7 %collective-permute-done.5 = bf16[256,384]{1,0:T(8,128)(2,1)S(1)} collective-permute-done((bf16[256,384]{1,0:T(8,128)(2,1)S(1)}, bf16[256,384]{1,0:T(8,128)(2,1)S(1)}, u32[]{:S(2)}, u32[]{:S(2)}) %collective-permute-start.5) | collective-permute-done | bytes 196640 | tf_op jit(solution)/shard_map/ppermute | solution.py:213
  28.7 1.3 collective-permute-start.7
  30.0 0.7 constant_dynamic-update-slice_fusion.6
  30.7 0.7 constant_dynamic-update-slice_fusion.5
  31.4 0.7 constant_dynamic-update-slice_fusion.4.refs_14_
  32.1 1.2 collective-permute-start.10
  33.3 7.1 %collective-permute-start.9 = (bf16[272,1024]{1,0:T(8,128)(2,1)S(1)}, bf16[272,1024]{1,0:T(8,128)(2,1)S(1)}, u32[]{:S(2)}, u32[]{:S(2)}) collective-permute-start(bf16[272,1024]{1,0:T(8,128)(2,1)S(1)} %collective-permute-done.8.refs_2_), channel_id=1, source_target_pairs={{0,4},{6,2},{4,8},{10,6},{8,12},{14,10},{1,5},{7,3},{5,9},{11,7},{... | collective-permute-start | bytes 1671176 | tf_op jit(solution)/shard_map/ppermute | solution.py:267
  40.4 1.1 collective-permute-start.14
  41.5 6.2 %collective-permute-done.7.refs_6_ = bf16[272,1024]{1,0:T(8,128)(2,1)S(1)} collective-permute-done((bf16[272,1024]{1,0:T(8,128)(2,1)S(1)}, bf16[272,1024]{1,0:T(8,128)(2,1)S(1)}, u32[]{:S(2)}, u32[]{:S(2)}) %collective-permute-start.7) | collective-permute-done | bytes 557088 | tf_op jit(solution)/shard_map/ppermute | solution.py:266
  47.8 1.0 collective-permute-start.15
  48.8 2.2 %collective-permute-done.10.refs_15_ = bf16[1024,384]{1,0:T(8,128)(2,1)} collective-permute-done((bf16[1024,384]{1,0:T(8,128)(2,1)}, bf16[1024,384]{1,0:T(8,128)(2,1)}, u32[]{:S(2)}, u32[]{:S(2)}) %collective-permute-start.10) | collective-permute-done | bytes 786464 | tf_op jit(solution)/shard_map/ppermute | solution.py:253
  51.6 7.3 %collective-permute-start.12 = (bf16[256,1024]{1,0:T(8,128)(2,1)S(1)}, bf16[256,1024]{1,0:T(8,128)(2,1)}, u32[]{:S(2)}, u32[]{:S(2)}) collective-permute-start(bf16[256,1024]{1,0:T(8,128)(2,1)S(1)} %collective-permute-done.3.refs_3_), channel_id=1, source_target_pairs={{0,4},{6,2},{4,8},{10,6},{8,12},{14,10},{1,5},{7,3},{5,9},{11,7},{... | collective-permute-start | bytes 1572872 | tf_op jit(solution)/shard_map/ppermute | solution.py:272
  58.9 1.6 %collective-permute-start.17 = (bf16[256,1024]{1,0:T(8,128)(2,1)S(1)}, bf16[256,1024]{1,0:T(8,128)(2,1)}, u32[]{:S(2)}, u32[]{:S(2)}) collective-permute-start(bf16[256,1024]{1,0:T(8,128)(2,1)S(1)} %collective-permute-done.3.refs_3_), channel_id=1, source_target_pairs={{0,1},{1,0},{2,3},{3,2},{4,5},{5,4},{6,7},{7,6},{8,9},{9,8},{10,11... | collective-permute-start | bytes 1572872 | tf_op jit(solution)/shard_map/ppermute | solution.py:345
  61.2 1.3 collective-permute-start.11
  62.5 2.0 %collective-permute-done.16.refs_12_ = bf16[272,1024]{1,0:T(8,128)(2,1)} collective-permute-done((bf16[272,1024]{1,0:T(8,128)(2,1)S(1)}, bf16[272,1024]{1,0:T(8,128)(2,1)}, u32[]{:S(2)}, u32[]{:S(2)}) %collective-permute-start.16) | collective-permute-done | bytes 557088 | tf_op jit(solution)/shard_map/ppermute | solution.py:274
  64.5 0.7 slice_convert_fusion
  65.2 0.7 slice_convert_fusion.3
  67.0 0.7 pad_add_fusion.keys_ref
  67.6 0.6 pad_add_fusion.1.asks_ref
  68.3 3.5 %masks.1 = (bf16[4096,128]{1,0:T(8,128)(2,1)}, s32[4096,128]{1,0:T(8,128)}, bf16[128,2048]{1,0:T(8,128)(2,1)}) custom-call(s32[4,4096]{1,0:T(4,128)} %pad_add_fusion.keys_ref, s32[2,2048]{1,0:T(2,128)} %pad_add_fusion.1.asks_ref), custom_call_target="tpu_custom_call" | custom-call | flops 2200000000 | bytes 1048576 | tf_op jit(solution)/shard_map/masks/pallas_call | solution.py:300
  71.8 5.1 %collective-permute-done.11.refs_7_ = bf16[256,1024]{1,0:T(8,128)(2,1)} collective-permute-done((bf16[256,1024]{1,0:T(8,128)(2,1)}, bf16[256,1024]{1,0:T(8,128)(2,1)}, u32[]{:S(2)}, u32[]{:S(2)}) %collective-permute-start.11) | collective-permute-done | bytes 524320 | tf_op jit(solution)/shard_map/ppermute | solution.py:271
  76.9 0.8 collective-permute-start.18
  77.9 0.7 collective-permute-start.20
  78.6 2.6 %collective-permute-start.22 = (bf16[64,1024]{1,0:T(8,128)(2,1)S(1)}, bf16[64,1024]{1,0:T(8,128)(2,1)S(1)}, u32[]{:S(2)}, u32[]{:S(2)}) collective-permute-start(bf16[64,1024]{1,0:T(8,128)(2,1)S(1)} %copy-done.6), channel_id=1, source_target_pairs={{0,12},{4,0},{8,4},{12,8},{1,13},{5,1},{9,5},{13,9},{2,14},{6,2},{... | collective-permute-start | bytes 393224 | tf_op jit(solution)/shard_map/ppermute | solution.py:213
  81.2 10.9 %project.1 = (bf16[4096,256]{1,0:T(8,128)(2,1)}, bf16[256,4096]{1,0:T(8,128)(2,1)}, bf16[256,2048]{1,0:T(8,128)(2,1)}) custom-call(s32[3]{0:T(128)S(1)} %pad_add_fusion.10.who_ref, bf16[512,1024]{1,0:T(8,128)(2,1)} %refs_0_, bf16[528,1024]{1,0:T(8,128)(2,1)} %collective-permute-done.13.refs_1_, bf16[272,1024]{1,0:T(8,128)(2,1)S(1)} %collective-permute-done.8.refs_2_, ...), custom_call_target="tpu_custom_call" | custom-call | flops 13200000000 | bytes 1048576 | tf_op jit(solution)/shard_map/project/pallas_call | solution.py:361
  92.2 1.6 %copy-done.2 = bf16[4096,256]{1,0:T(8,128)(2,1)S(1)} copy-done((bf16[4096,256]{1,0:T(8,128)(2,1)S(1)}, bf16[4096,256]{1,0:T(8,128)(2,1)}, u32[]{:S(2)}) %copy-start.2) | copy-done | bytes 2097176
  93.7 1.2 copy-done.3
  95.0 16.3 %attend.3 = bf16[1024,256]{1,0:T(8,128)(2,1)S(1)} custom-call(s32[80]{0:T(128)S(1)} %reshape.222.tab_ref, f32[4]{0:T(128)S(1)} %dynamic-slice_bitcast_fusion.delta_ref, bf16[4096,256]{1,0:T(8,128)(2,1)S(1)} %copy-done.2, bf16[256,4096]{1,0:T(8,128)(2,1)} %get-tuple-element.57.vt_ref, bf16[256,2048]{1,0:T(8,128)(2,1)S(1)} %copy-done.3, ...), custom_call_target="tpu_custom_call" | custom-call | flops 17600000000 | bytes 1048576 | tf_op jit(solution)/shard_map/attend/pallas_call | solution.py:380
  111.9 1.0 collective-permute-start.23
  112.9 2.1 %collective-permute-start.24 = (bf16[512,256]{1,0:T(8,128)(2,1)S(1)}, bf16[512,256]{1,0:T(8,128)(2,1)S(1)}, u32[]{:S(2)}, u32[]{:S(2)}) collective-permute-start(bf16[512,256]{1,0:T(8,128)(2,1)S(1)} %get-tuple-element.64), channel_id=1, source_target_pairs={{0,3},{1,2},{2,1},{3,0},{4,7},{5,6},{6,5},{7,4},{8,11},{9,10},{10,... | collective-permute-start | bytes 786440 | tf_op jit(solution)/shard_map/ppermute | solution.py:402
  115.1 15.9 %attend.2 = bf16[1024,256]{1,0:T(8,128)(2,1)S(1)} custom-call(s32[80]{0:T(128)S(1)} %reshape.222.tab_ref, f32[4]{0:T(128)S(1)} %dynamic-slice_bitcast_fusion.delta_ref, bf16[4096,256]{1,0:T(8,128)(2,1)S(1)} %copy-done.2, bf16[256,4096]{1,0:T(8,128)(2,1)} %get-tuple-element.57.vt_ref, bf16[256,2048]{1,0:T(8,128)(2,1)S(1)} %copy-done.4, ...), custom_call_target="tpu_custom_call" | custom-call | flops 17600000000 | bytes 1048576 | tf_op jit(solution)/shard_map/attend/pallas_call | solution.py:380
  131.0 5.3 %collective-permute-done.24.a3 = bf16[512,256]{1,0:T(8,128)(2,1)S(1)} collective-permute-done((bf16[512,256]{1,0:T(8,128)(2,1)S(1)}, bf16[512,256]{1,0:T(8,128)(2,1)S(1)}, u32[]{:S(2)}, u32[]{:S(2)}) %collective-permute-start.24) | collective-permute-done | bytes 262176 | tf_op jit(solution)/shard_map/ppermute | solution.py:402
  137.1 2.4 %collective-permute-done.26.a1 = bf16[512,256]{1,0:T(8,128)(2,1)S(1)} collective-permute-done((bf16[512,256]{1,0:T(8,128)(2,1)S(1)}, bf16[512,256]{1,0:T(8,128)(2,1)S(1)}, u32[]{:S(2)}, u32[]{:S(2)}) %collective-permute-start.26) | collective-permute-done | bytes 262176 | tf_op jit(solution)/shard_map/ppermute | solution.py:407
  139.6 2.9 %mixed.1 = bf16[512,1024]{1,0:T(8,128)(2,1)} custom-call(s32[2]{0:T(128)S(1)} %pad_add_fusion.6.who_ref, bf16[512,256]{1,0:T(8,128)(2,1)S(1)} %get-tuple-element.86.a0, bf16[512,256]{1,0:T(8,128)(2,1)S(1)} %collective-permute-done.26.a1, bf16[512,256]{1,0:T(8,128)(2,1)S(1)} %collective-permute-done.23.a2, bf16[512,256]{1,0:T(8,128)(2,1)S(1)} %collective-permute-done.24.a3, ...), custom_call_target="tpu_custom_call" | custom-call | flops 3300000000 | bytes 1048576 | tf_op jit(solution)/shard_map/mixed/pallas_call | solution.py:410
  (116 shorter events, 4.8 us)
Async XLA Ops:
  0.6 4.6 %copy-start.7 = (s32[512]{0:T(512)S(1)}, s32[512]{0:T(512)}, u32[]{:S(2)}) copy-start(s32[512]{0:T(512)} %param.12) | copy-start | bytes 6148
  0.6 4.6 %copy-start.8 = (s32[512]{0:T(512)S(1)}, s32[512]{0:T(512)}, u32[]{:S(2)}) copy-start(s32[512]{0:T(512)} %param.13) | copy-start | bytes 6148
  0.7 4.6 %copy-start.9 = (s32[512]{0:T(512)S(1)}, s32[512]{0:T(512)}, u32[]{:S(2)}) copy-start(s32[512]{0:T(512)} %param.11) | copy-start | bytes 6148
  0.7 6.1 %copy-start.5 = (bf16[512,1024]{1,0:T(8,128)(2,1)S(1)}, bf16[512,1024]{1,0:T(8,128)(2,1)}, u32[]{:S(2)}) copy-start(bf16[512,1024]{1,0:T(8,128)(2,1)} %refs_0_) | copy-start | bytes 3145732
  2.5 6.8 %collective-permute-start = (bf16[64,384]{1,0:T(8,128)(2,1)}, bf16[64,384]{1,0:T(8,128)(2,1)S(1)}, u32[]{:S(2)}, u32[]{:S(2)}) collective-permute-start(bf16[64,384]{1,0:T(8,128)(2,1)} %get-tuple-element.40), channel_id=1, source_target_pairs={{0,1},{1,0},{2,3},{3,2},{4,5},{5,4},{6,7},{7,6},{8,9},{9,8},{10,11... | collective-permute-start | bytes 147464 | tf_op jit(solution)/shard_map/ppermute | solution.py:201
  2.5 7.4 %collective-permute-start.1 = (bf16[64,384]{1,0:T(8,128)(2,1)}, bf16[64,384]{1,0:T(8,128)(2,1)S(1)}, u32[]{:S(2)}, u32[]{:S(2)}) collective-permute-start(bf16[64,384]{1,0:T(8,128)(2,1)} %get-tuple-element.41), channel_id=1, source_target_pairs={{0,2},{2,0},{1,3},{3,1},{4,6},{6,4},{5,7},{7,5},{8,10},{10,8},{9,1... | collective-permute-start | bytes 147464 | tf_op jit(solution)/shard_map/ppermute | solution.py:202
  5.2 5.3 %collective-permute-start.2 = (bf16[64,384]{1,0:T(8,128)(2,1)}, bf16[64,384]{1,0:T(8,128)(2,1)S(1)}, u32[]{:S(2)}, u32[]{:S(2)}) collective-permute-start(bf16[64,384]{1,0:T(8,128)(2,1)} %get-tuple-element.42), channel_id=1, source_target_pairs={{0,3},{1,2},{2,1},{3,0},{4,7},{5,6},{6,5},{7,4},{8,11},{9,10},{10,... | collective-permute-start | bytes 147464 | tf_op jit(solution)/shard_map/ppermute | solution.py:203
  8.7 8.8 %copy-start.10 = (f32[2,16]{1,0:T(2,128)S(1)}, f32[2,16]{1,0:T(2,128)}, u32[]{:S(2)}) copy-start(f32[2,16]{1,0:T(2,128)} %param.10) | copy-start | bytes 388
  11.2 8.8 %collective-permute-start.4 = (bf16[256,384]{1,0:T(8,128)(2,1)S(1)}, bf16[256,384]{1,0:T(8,128)(2,1)S(1)}, u32[]{:S(2)}, u32[]{:S(2)}) collective-permute-start(bf16[256,384]{1,0:T(8,128)(2,1)S(1)} %get-tuple-element.90), channel_id=1, source_target_pairs={{0,4},{4,8},{8,12},{12,0},{1,5},{5,9},{9,13},{13,1},{2,6},{6,10},{... | collective-permute-start | bytes 589832 | tf_op jit(solution)/shard_map/ppermute | solution.py:213
  12.8 15.9 %collective-permute-start.5 = (bf16[256,384]{1,0:T(8,128)(2,1)S(1)}, bf16[256,384]{1,0:T(8,128)(2,1)S(1)}, u32[]{:S(2)}, u32[]{:S(2)}) collective-permute-start(bf16[256,384]{1,0:T(8,128)(2,1)S(1)} %get-tuple-element.90), channel_id=1, source_target_pairs={{0,8},{4,12},{8,0},{12,4},{1,9},{5,13},{9,1},{13,5},{2,10},{6,14},... | collective-permute-start | bytes 589832 | tf_op jit(solution)/shard_map/ppermute | solution.py:213
  15.1 13.6 %collective-permute-start.6 = (bf16[256,384]{1,0:T(8,128)(2,1)S(1)}, bf16[256,384]{1,0:T(8,128)(2,1)S(1)}, u32[]{:S(2)}, u32[]{:S(2)}) collective-permute-start(bf16[256,384]{1,0:T(8,128)(2,1)S(1)} %get-tuple-element.90), channel_id=1, source_target_pairs={{0,12},{4,0},{8,4},{12,8},{1,13},{5,1},{9,5},{13,9},{2,14},{6,2},{... | collective-permute-start | bytes 589832 | tf_op jit(solution)/shard_map/ppermute | solution.py:213
  16.2 17.1 %collective-permute-start.8 = (bf16[272,1024]{1,0:T(8,128)(2,1)S(1)}, bf16[272,1024]{1,0:T(8,128)(2,1)S(1)}, u32[]{:S(2)}, u32[]{:S(2)}) collective-permute-start(bf16[272,1024]{1,0:T(8,128)(2,1)S(1)} %pad_maximum_fusion.2), channel_id=1, source_target_pairs={{0,2},{2,0},{1,3},{3,1},{4,6},{6,4},{5,7},{7,5},{8,10},{10,8},{9,1... | collective-permute-start | bytes 1671176 | tf_op jit(solution)/shard_map/ppermute | solution.py:264
  17.5 31.3 %collective-permute-start.3 = (bf16[256,1024]{1,0:T(8,128)(2,1)}, bf16[256,1024]{1,0:T(8,128)(2,1)S(1)}, u32[]{:S(2)}, u32[]{:S(2)}) collective-permute-start(bf16[256,1024]{1,0:T(8,128)(2,1)} %get-tuple-element.47), channel_id=1, source_target_pairs={{0,2},{2,0},{1,3},{3,1},{4,6},{6,4},{5,7},{7,5},{8,10},{10,8},{9,1... | collective-permute-start | bytes 1572872 | tf_op jit(solution)/shard_map/ppermute | solution.py:264
  28.7 19.1 %collective-permute-start.7 = (bf16[272,1024]{1,0:T(8,128)(2,1)S(1)}, bf16[272,1024]{1,0:T(8,128)(2,1)S(1)}, u32[]{:S(2)}, u32[]{:S(2)}) collective-permute-start(bf16[272,1024]{1,0:T(8,128)(2,1)S(1)} %pad_maximum_fusion.2), channel_id=1, source_target_pairs={{4,0},{2,6},{8,4},{6,10},{12,8},{10,14},{5,1},{3,7},{9,5},{7,11},{... | collective-permute-start | bytes 1671176 | tf_op jit(solution)/shard_map/ppermute | solution.py:266
  32.1 18.8 %collective-permute-start.10 = (bf16[1024,384]{1,0:T(8,128)(2,1)}, bf16[1024,384]{1,0:T(8,128)(2,1)}, u32[]{:S(2)}, u32[]{:S(2)}) collective-permute-start(bf16[1024,384]{1,0:T(8,128)(2,1)} %constant_dynamic-update-slice_fusion.4.refs_14_), channel_id=1, source_target_pairs={{0,16},{16,0},{1,17},{17,1},{2,18},{18,2},{3,19},{19,3},{4,20},{20... | collective-permute-start | bytes 2359304 | tf_op jit(solution)/shard_map/ppermute | solution.py:253
  33.3 18.2 %collective-permute-start.9 = (bf16[272,1024]{1,0:T(8,128)(2,1)S(1)}, bf16[272,1024]{1,0:T(8,128)(2,1)S(1)}, u32[]{:S(2)}, u32[]{:S(2)}) collective-permute-start(bf16[272,1024]{1,0:T(8,128)(2,1)S(1)} %collective-permute-done.8.refs_2_), channel_id=1, source_target_pairs={{0,4},{6,2},{4,8},{10,6},{8,12},{14,10},{1,5},{7,3},{5,9},{11,7},{... | collective-permute-start | bytes 1671176 | tf_op jit(solution)/shard_map/ppermute | solution.py:267
  40.4 20.1 %collective-permute-start.14 = (bf16[272,1024]{1,0:T(8,128)(2,1)S(1)}, bf16[272,1024]{1,0:T(8,128)(2,1)S(1)}, u32[]{:S(2)}, u32[]{:S(2)}) collective-permute-start(bf16[272,1024]{1,0:T(8,128)(2,1)S(1)} %collective-permute-done.8.refs_2_), channel_id=1, source_target_pairs={{0,1},{1,0},{2,3},{3,2},{4,5},{5,4},{6,7},{7,6},{8,9},{9,8},{10,11... | collective-permute-start | bytes 1671176 | tf_op jit(solution)/shard_map/ppermute | solution.py:274
  47.8 13.4 %collective-permute-start.15 = (bf16[272,1024]{1,0:T(8,128)(2,1)S(1)}, bf16[272,1024]{1,0:T(8,128)(2,1)S(1)}, u32[]{:S(2)}, u32[]{:S(2)}) collective-permute-start(bf16[272,1024]{1,0:T(8,128)(2,1)S(1)} %collective-permute-done.7.refs_6_), channel_id=1, source_target_pairs={{0,1},{1,0},{2,3},{3,2},{4,5},{5,4},{6,7},{7,6},{8,9},{9,8},{10,11... | collective-permute-start | bytes 1671176 | tf_op jit(solution)/shard_map/ppermute | solution.py:274
  51.6 25.4 %collective-permute-start.12 = (bf16[256,1024]{1,0:T(8,128)(2,1)S(1)}, bf16[256,1024]{1,0:T(8,128)(2,1)}, u32[]{:S(2)}, u32[]{:S(2)}) collective-permute-start(bf16[256,1024]{1,0:T(8,128)(2,1)S(1)} %collective-permute-done.3.refs_3_), channel_id=1, source_target_pairs={{0,4},{6,2},{4,8},{10,6},{8,12},{14,10},{1,5},{7,3},{5,9},{11,7},{... | collective-permute-start | bytes 1572872 | tf_op jit(solution)/shard_map/ppermute | solution.py:272
  58.9 19.7 %collective-permute-start.17 = (bf16[256,1024]{1,0:T(8,128)(2,1)S(1)}, bf16[256,1024]{1,0:T(8,128)(2,1)}, u32[]{:S(2)}, u32[]{:S(2)}) collective-permute-start(bf16[256,1024]{1,0:T(8,128)(2,1)S(1)} %collective-permute-done.3.refs_3_), channel_id=1, source_target_pairs={{0,1},{1,0},{2,3},{3,2},{4,5},{5,4},{6,7},{7,6},{8,9},{9,8},{10,11... | collective-permute-start | bytes 1572872 | tf_op jit(solution)/shard_map/ppermute | solution.py:345
  60.5 4.7 %collective-permute-start.13 = (bf16[528,1024]{1,0:T(8,128)(2,1)}, bf16[528,1024]{1,0:T(8,128)(2,1)}, u32[]{:S(2)}, u32[]{:S(2)}) collective-permute-start(bf16[528,1024]{1,0:T(8,128)(2,1)} %pad_maximum_fusion), channel_id=1, source_target_pairs={{0,1},{1,0},{2,3},{3,2},{4,5},{5,4},{6,7},{7,6},{8,9},{9,8},{10,11... | collective-permute-start | bytes 3244040 | tf_op jit(solution)/shard_map/ppermute | solution.py:274
  60.6 3.9 %collective-permute-start.16 = (bf16[272,1024]{1,0:T(8,128)(2,1)S(1)}, bf16[272,1024]{1,0:T(8,128)(2,1)}, u32[]{:S(2)}, u32[]{:S(2)}) collective-permute-start(bf16[272,1024]{1,0:T(8,128)(2,1)S(1)} %collective-permute-done.9.refs_10_), channel_id=1, source_target_pairs={{0,1},{1,0},{2,3},{3,2},{4,5},{5,4},{6,7},{7,6},{8,9},{9,8},{10,11... | collective-permute-start | bytes 1671176 | tf_op jit(solution)/shard_map/ppermute | solution.py:274
  61.2 15.7 %collective-permute-start.11 = (bf16[256,1024]{1,0:T(8,128)(2,1)}, bf16[256,1024]{1,0:T(8,128)(2,1)}, u32[]{:S(2)}, u32[]{:S(2)}) collective-permute-start(bf16[256,1024]{1,0:T(8,128)(2,1)} %get-tuple-element.47), channel_id=1, source_target_pairs={{4,0},{2,6},{8,4},{6,10},{12,8},{10,14},{5,1},{3,7},{9,5},{7,11},{... | collective-permute-start | bytes 1572872 | tf_op jit(solution)/shard_map/ppermute | solution.py:271
  68.3 9.6 %copy-start.6 = (bf16[64,1024]{1,0:T(8,128)(2,1)S(1)}, bf16[64,1024]{1,0:T(8,128)(2,1)}, u32[]{:S(2)}) copy-start(bf16[64,1024]{1,0:T(8,128)(2,1)} %param.9) | copy-start | bytes 393220
  76.9 4.3 %collective-permute-start.18 = (bf16[256,1024]{1,0:T(8,128)(2,1)}, bf16[256,1024]{1,0:T(8,128)(2,1)S(1)}, u32[]{:S(2)}, u32[]{:S(2)}) collective-permute-start(bf16[256,1024]{1,0:T(8,128)(2,1)} %collective-permute-done.11.refs_7_), channel_id=1, source_target_pairs={{0,1},{1,0},{2,3},{3,2},{4,5},{5,4},{6,7},{7,6},{8,9},{9,8},{10,11... | collective-permute-start | bytes 1572872 | tf_op jit(solution)/shard_map/ppermute | solution.py:348
  77.7 3.5 %collective-permute-start.19 = (bf16[256,1024]{1,0:T(8,128)(2,1)}, bf16[256,1024]{1,0:T(8,128)(2,1)S(1)}, u32[]{:S(2)}, u32[]{:S(2)}) collective-permute-start(bf16[256,1024]{1,0:T(8,128)(2,1)} %collective-permute-done.12.refs_11_), channel_id=1, source_target_pairs={{0,1},{1,0},{2,3},{3,2},{4,5},{5,4},{6,7},{7,6},{8,9},{9,8},{10,11... | collective-permute-start | bytes 1572872 | tf_op jit(solution)/shard_map/ppermute | solution.py:348
  77.9 33.4 %collective-permute-start.20 = (bf16[64,1024]{1,0:T(8,128)(2,1)S(1)}, bf16[64,1024]{1,0:T(8,128)(2,1)S(1)}, u32[]{:S(2)}, u32[]{:S(2)}) collective-permute-start(bf16[64,1024]{1,0:T(8,128)(2,1)S(1)} %copy-done.6), channel_id=1, source_target_pairs={{0,4},{4,8},{8,12},{12,0},{1,5},{5,9},{9,13},{13,1},{2,6},{6,10},{... | collective-permute-start | bytes 393224 | tf_op jit(solution)/shard_map/ppermute | solution.py:213
  78.6 32.7 %collective-permute-start.21 = (bf16[64,1024]{1,0:T(8,128)(2,1)S(1)}, bf16[64,1024]{1,0:T(8,128)(2,1)S(1)}, u32[]{:S(2)}, u32[]{:S(2)}) collective-permute-start(bf16[64,1024]{1,0:T(8,128)(2,1)S(1)} %copy-done.6), channel_id=1, source_target_pairs={{0,8},{4,12},{8,0},{12,4},{1,9},{5,13},{9,1},{13,5},{2,10},{6,14},... | collective-permute-start | bytes 393224 | tf_op jit(solution)/shard_map/ppermute | solution.py:213
  78.6 13.5 %copy-start = (bf16[4096,128]{1,0:T(8,128)(2,1)S(1)}, bf16[4096,128]{1,0:T(8,128)(2,1)}, u32[]{:S(2)}) copy-start(bf16[4096,128]{1,0:T(8,128)(2,1)} %get-tuple-element.59.fk_ref) | copy-start | bytes 3145732
  78.6 13.5 %copy-start.1 = (bf16[128,2048]{1,0:T(8,128)(2,1)S(1)}, bf16[128,2048]{1,0:T(8,128)(2,1)}, u32[]{:S(2)}) copy-start(bf16[128,2048]{1,0:T(8,128)(2,1)} %get-tuple-element.60.fqt_ref) | copy-start | bytes 1572868
  78.6 32.7 %collective-permute-start.22 = (bf16[64,1024]{1,0:T(8,128)(2,1)S(1)}, bf16[64,1024]{1,0:T(8,128)(2,1)S(1)}, u32[]{:S(2)}, u32[]{:S(2)}) collective-permute-start(bf16[64,1024]{1,0:T(8,128)(2,1)S(1)} %copy-done.6), channel_id=1, source_target_pairs={{0,12},{4,0},{8,4},{12,8},{1,13},{5,1},{9,5},{13,9},{2,14},{6,2},{... | collective-permute-start | bytes 393224 | tf_op jit(solution)/shard_map/ppermute | solution.py:213
  92.1 1.6 %copy-start.2 = (bf16[4096,256]{1,0:T(8,128)(2,1)S(1)}, bf16[4096,256]{1,0:T(8,128)(2,1)}, u32[]{:S(2)}) copy-start(bf16[4096,256]{1,0:T(8,128)(2,1)} %get-tuple-element.56.k_ref) | copy-start | bytes 6291460
  93.7 1.2 copy-start.3
  111.3 3.8 %copy-start.4 = (bf16[256,2048]{1,0:T(8,128)(2,1)S(1)}, bf16[256,2048]{1,0:T(8,128)(2,1)}, u32[]{:S(2)}) copy-start(bf16[256,2048]{1,0:T(8,128)(2,1)} %get-tuple-element.58.qt_ref) | copy-start | bytes 3145732
  111.4 25.0 %collective-permute-start.25 = (bf16[256,1024]{1,0:T(8,128)(2,1)S(1)}, bf16[256,1024]{1,0:T(8,128)(2,1)S(1)}, u32[]{:S(2)}, u32[]{:S(2)}) collective-permute-start(bf16[256,1024]{1,0:T(8,128)(2,1)S(1)} %constant_dynamic-update-slice_fusion.19.w0), channel_id=1, source_target_pairs={{0,2},{2,0},{1,3},{3,1},{4,6},{6,4},{5,7},{7,5},{8,10},{10,8},{9,1... | collective-permute-start | bytes 1572872 | tf_op jit(solution)/shard_map/ppermute | solution.py:403
  111.9 19.1 %collective-permute-start.23 = (bf16[512,256]{1,0:T(8,128)(2,1)S(1)}, bf16[512,256]{1,0:T(8,128)(2,1)S(1)}, u32[]{:S(2)}, u32[]{:S(2)}) collective-permute-start(bf16[512,256]{1,0:T(8,128)(2,1)S(1)} %get-tuple-element.63), channel_id=1, source_target_pairs={{0,2},{2,0},{1,3},{3,1},{4,6},{6,4},{5,7},{7,5},{8,10},{10,8},{9,1... | collective-permute-start | bytes 786440 | tf_op jit(solution)/shard_map/ppermute | solution.py:401
  112.9 23.4 %collective-permute-start.24 = (bf16[512,256]{1,0:T(8,128)(2,1)S(1)}, bf16[512,256]{1,0:T(8,128)(2,1)S(1)}, u32[]{:S(2)}, u32[]{:S(2)}) collective-permute-start(bf16[512,256]{1,0:T(8,128)(2,1)S(1)} %get-tuple-element.64), channel_id=1, source_target_pairs={{0,3},{1,2},{2,1},{3,0},{4,7},{5,6},{6,5},{7,4},{8,11},{9,10},{10,... | collective-permute-start | bytes 786440 | tf_op jit(solution)/shard_map/ppermute | solution.py:402
  136.5 3.1 %collective-permute-start.27 = (bf16[2,256,1024]{2,1,0:T(8,128)(2,1)S(1)}, bf16[2,256,1024]{2,1,0:T(8,128)(2,1)S(1)}, u32[]{:S(2)}, u32[]{:S(2)}) collective-permute-start(bf16[2,256,1024]{2,1,0:T(8,128)(2,1)S(1)} %pad_maximum_fusion.1), channel_id=1, source_target_pairs={{0,1},{1,0},{2,3},{3,2},{4,5},{5,4},{6,7},{7,6},{8,9},{9,8},{10,11... | collective-permute-start | bytes 3145736 | tf_op jit(solution)/shard_map/ppermute | solution.py:408
  136.6 3.0 %collective-permute-start.26 = (bf16[512,256]{1,0:T(8,128)(2,1)S(1)}, bf16[512,256]{1,0:T(8,128)(2,1)S(1)}, u32[]{:S(2)}, u32[]{:S(2)}) collective-permute-start(bf16[512,256]{1,0:T(8,128)(2,1)S(1)} %get-tuple-element.69), channel_id=1, source_target_pairs={{0,1},{1,0},{2,3},{3,2},{4,5},{5,4},{6,7},{7,6},{8,9},{9,8},{10,11... | collective-permute-start | bytes 786440 | tf_op jit(solution)/shard_map/ppermute | solution.py:407

commit v4 on v3

--- a/solution.py
+++ b/solution.py
@@ -260,7 +260,8 @@
     digits = jnp.pad(digits, ((0, ID_ROWS - digits.shape[0]), (0, 0)))
     first = jnp.concatenate([tokens[:cut], digits], 0)
     whole = jnp.concatenate([tokens, digits], 0)
-    first, second, _ = lax.optimization_barrier((first, tokens[cut:], came))
+    wo = turns(lax.optimization_barrier((w_out, picked))[0], planes)
+    first, second, _, wo = lax.optimization_barrier((first, tokens[cut:], came, wo))
     other = [lax.ppermute(x, "side", swap) for x in (first, second)]
     first_z = lax.optimization_barrier((first, turned))[0]
     mine = [lax.ppermute(first_z, pair, native)]
@@ -352,7 +353,7 @@
         held += [((i + 5) * rows, cut, peers[i + 1]), ((i + 5) * rows + cut, cut, rest[i])]
     plan = tuple((at, n) for at, n, _ in held)
     xs = [x for _, _, x in held]
-    limit = pltpu.CompilerParams(vmem_limit_bytes=48 << 20)
+    limit = pltpu.CompilerParams(vmem_limit_bytes=28 << 20)
     queries = {}
     for at, _ in plan:
         block = at // rows
@@ -373,8 +374,8 @@
         name="project",
     )(who, *xs, *w_parts)
 
-    late_w = lax.optimization_barrier((w_out, lasts))[0]
-    wo = turns(late_w, planes)
+    wo, k, vt, qt = lax.optimization_barrier((jnp.concatenate(wo, 0), k, vt, qt))
+    wo_side = lax.ppermute(wo, "side", swap)
 
     def attend(q0):
         return pl.pallas_call(
@@ -395,17 +396,14 @@
         )(table, delta, k, vt, qt, fk, fqt, vk, var_q[None, :])
 
     far = attend(nq)
-    far_side, far_cross = far[:rows], far[rows:]
-    wo, far_side, far_cross = lax.optimization_barrier((wo, far_side, far_cross))
-    wo = jnp.concatenate(wo, 0)
+    far_side, far_cross, wo_side = lax.optimization_barrier((far[:rows], far[rows:], wo_side))
     far_side = lax.ppermute(far_side, "side", swap)
     far_cross = lax.ppermute(far_cross, ("side", "core"), cross)
-    wo_side = lax.ppermute(wo, "side", swap)
+    wo_core = lax.ppermute(jnp.stack([wo, wo_side]), "core", swap)
     near = attend(0)
     near_core, near = near[rows:], near[:rows]
-    near_core, far_side, far_cross, wo_side = lax.optimization_barrier((near_core, far_side, far_cross, wo_side))
+    near_core, far_side, far_cross, wo_core = lax.optimization_barrier((near_core, far_side, far_cross, wo_core))
     near_core = lax.ppermute(near_core, "core", swap)
-    wo_core = lax.ppermute(jnp.stack([wo, wo_side]), "core", swap)
     wo_parts = [wo, wo_core, wo_side]
     return pl.pallas_call(
         functools.partial(out_kernel, planes),

time: 143 us -> 135 us (0.944)
  waiting for transfers between devices: 34.9 us -> 18.7 us
  other arithmetic: 5.61 us -> 16.2 us
  Pallas kernels: 51.3 us -> 44.2 us
  starting transfers between devices: 40.1 us -> 42.8 us
  local copies, waits for them, and re-layouts: 10.1 us -> 11.9 us
    ppermute x1, waiting for transfers between devices: 5.33 us -> 0.01 us  [local(): far_cross = lax.ppermute(far_cross, ('side', 'core'), cross)]
    ppermute x1, waiting for transfers between devices: 5.1 us -> 0.01 us  [local(): mine.append(lax.ppermute(second, pair, native))]
    pallas_call x2, Pallas kernels: 32.2 us -> 27.4 us  [attend(): pl.pallas_call(functools.partial(attend_kernel, hsize, q0, nq), out_shape...]
    ppermute x1, starting transfers between devices: 0.5 us -> 3.47 us  [local(): wo_side = lax.ppermute(wo, 'side', swap)]
    pallas_call x1, Pallas kernels: 10.9 us -> 8.56 us  [local(): pl.pallas_call(functools.partial(project_kernel, cols, plan, queries, pla...]
    add x1, other arithmetic: 0.09 us -> 2.36 us  [local(): code = (seg * 1024 + var).reshape(nk // TILE, TILE)]
    ppermute x1, waiting for transfers between devices: 2.19 us -> 0.01 us  [local(): w_parts = [half_w, lax.ppermute(half_w, 'groups', mate)]]
    ppermute x4, waiting for transfers between devices: 1.99 us -> 0.01 us  [local(): lax.ppermute(x, 'core', swap)]
  transfers between devices with their start and end apart: 28 -> 28, of which waited for: 9 -> 7; matrix products, arithmetic and copies ran while one was open for 8% -> 20% of each run, Pallas kernels for 33% -> 23%
where the time goes in v4:
time: 135 us; the launch traced here: 134 us
  Pallas kernels  44.2 us (33%)
  starting transfers between devices  42.8 us (32%)
  waiting for transfers between devices  18.7 us (14%)
  other arithmetic  16.2 us (12%)
  local copies, waits for them, and re-layouts  11.9 us (9%)
    pallas_call x2, Pallas kernels, attend(): pl.pallas_call(functools.partial(attend_kernel, hsize, q0, nq), out_shape...  27.4 us
    ppermute x6, waiting for transfers between devices, turns(): lax.ppermute(block, 'plane', [(i, (i + s) % planes) for i in range(planes)])  10.3 us
    pallas_call x1, Pallas kernels, local(): pl.pallas_call(functools.partial(project_kernel, cols, plan, queries, pla...  8.56 us
    ppermute x6, starting transfers between devices, turns(): lax.ppermute(block, 'plane', [(i, (i + s) % planes) for i in range(planes)])  8.44 us
    ppermute x1, starting transfers between devices, local(): theirs = [lax.ppermute(other[0], pair, passed)]  6.92 us
    ppermute x1, starting transfers between devices, local(): theirs.append(lax.ppermute(passing, pair, passed))  6.59 us
    ppermute x1, waiting for transfers between devices, local(): mine = [lax.ppermute(first_z, pair, native)]  5.98 us
    unnamed x40, local copies, waits for them, and re-layouts  5.88 us
  transfers between devices with their start and end apart: 28, of which 7 were waited for; matrix products, arithmetic and copies ran while one was open for 20% of the time, Pallas kernels for 23%

profile of v4, /device:TPU:1, one launch (start us, length us, event | category | flops | bytes accessed | tf_op | source)
XLA Modules:
  0.0 134.1 jit_solution(7304060257152928966)
XLA Ops:
  0.6 1.8 %pick.1 = (bf16[64,384]{1,0:T(8,128)(2,1)}, bf16[64,384]{1,0:T(8,128)(2,1)}, bf16[64,384]{1,0:T(8,128)(2,1)}, bf16[64,384]{1,0:T(8,128)(2,1)}) custom-call(s32[2]{0:T(128)} %pad_add_fusion.7.who_ref, bf16[64,3072]{1,0:T(8,128)(2,1)} %w_ref.1), custom_call_target="tpu_custom_call" | custom-call | flops 1100000000 | bytes 1048576 | tf_op jit(solution)/shard_map/pick/pallas_call | solution.py:239
  2.5 2.7 %collective-permute-start.1 = (bf16[64,384]{1,0:T(8,128)(2,1)}, bf16[64,384]{1,0:T(8,128)(2,1)S(1)}, u32[]{:S(2)}, u32[]{:S(2)}) collective-permute-start(bf16[64,384]{1,0:T(8,128)(2,1)} %get-tuple-element.46), channel_id=1, source_target_pairs={{0,2},{2,0},{1,3},{3,1},{4,6},{6,4},{5,7},{7,5},{8,10},{10,8},{9,1... | collective-permute-start | bytes 147464 | tf_op jit(solution)/shard_map/ppermute | solution.py:202
  5.2 1.7 %collective-permute-start.3 = (bf16[64,1024]{1,0:T(8,128)(2,1)S(1)}, bf16[64,1024]{1,0:T(8,128)(2,1)S(1)}, u32[]{:S(2)}, u32[]{:S(2)}) collective-permute-start(bf16[64,1024]{1,0:T(8,128)(2,1)S(1)} %copy-done.4), channel_id=1, source_target_pairs={{0,4},{4,8},{8,12},{12,0},{1,5},{5,9},{9,13},{13,1},{2,6},{6,10},{... | collective-permute-start | bytes 393224 | tf_op jit(solution)/shard_map/ppermute | solution.py:213
  6.9 2.3 %collective-permute-start.4 = (bf16[64,1024]{1,0:T(8,128)(2,1)S(1)}, bf16[64,1024]{1,0:T(8,128)(2,1)S(1)}, u32[]{:S(2)}, u32[]{:S(2)}) collective-permute-start(bf16[64,1024]{1,0:T(8,128)(2,1)S(1)} %copy-done.4), channel_id=1, source_target_pairs={{0,8},{4,12},{8,0},{12,4},{1,9},{5,13},{9,1},{13,5},{2,10},{6,14},... | collective-permute-start | bytes 393224 | tf_op jit(solution)/shard_map/ppermute | solution.py:213
  9.2 0.8 constant_dynamic-update-slice_fusion.10
  10.7 0.9 fusion.25
  11.6 1.1 pad_maximum_fusion
  12.6 0.8 pad_maximum_fusion.2
  15.6 0.7 and.202
  16.3 0.6 copy.11
  16.9 1.1 collective-permute-start.5
  18.6 2.9 %collective-permute-start.9 = (bf16[256,384]{1,0:T(8,128)(2,1)S(1)}, bf16[256,384]{1,0:T(8,128)(2,1)S(1)}, u32[]{:S(2)}, u32[]{:S(2)}) collective-permute-start(bf16[256,384]{1,0:T(8,128)(2,1)S(1)} %get-tuple-element.100), channel_id=1, source_target_pairs={{0,12},{4,0},{8,4},{12,8},{1,13},{5,1},{9,5},{13,9},{2,14},{6,2},{... | collective-permute-start | bytes 589832 | tf_op jit(solution)/shard_map/ppermute | solution.py:213
  21.5 0.6 copy-done.6
  22.1 1.2 collective-permute-start.11
  24.1 1.3 collective-permute-done.7
  25.4 8.8 %collective-permute-done.8 = bf16[256,384]{1,0:T(8,128)(2,1)S(1)} collective-permute-done((bf16[256,384]{1,0:T(8,128)(2,1)S(1)}, bf16[256,384]{1,0:T(8,128)(2,1)S(1)}, u32[]{:S(2)}, u32[]{:S(2)}) %collective-permute-start.8) | collective-permute-done | bytes 196640 | tf_op jit(solution)/shard_map/ppermute | solution.py:213
  34.4 1.3 collective-permute-start.10
  35.8 1.3 collective-permute-start.13
  37.1 6.9 %collective-permute-start.12 = (bf16[272,1024]{1,0:T(8,128)(2,1)S(1)}, bf16[272,1024]{1,0:T(8,128)(2,1)S(1)}, u32[]{:S(2)}, u32[]{:S(2)}) collective-permute-start(bf16[272,1024]{1,0:T(8,128)(2,1)S(1)} %collective-permute-done.11.refs_2_), channel_id=1, source_target_pairs={{0,4},{6,2},{4,8},{10,6},{8,12},{14,10},{1,5},{7,3},{5,9},{11,7},{... | collective-permute-start | bytes 1671176 | tf_op jit(solution)/shard_map/ppermute | solution.py:268
  44.0 1.7 %collective-permute-start.17 = (bf16[272,1024]{1,0:T(8,128)(2,1)S(1)}, bf16[272,1024]{1,0:T(8,128)(2,1)}, u32[]{:S(2)}, u32[]{:S(2)}) collective-permute-start(bf16[272,1024]{1,0:T(8,128)(2,1)S(1)} %collective-permute-done.11.refs_2_), channel_id=1, source_target_pairs={{0,1},{1,0},{2,3},{3,2},{4,5},{5,4},{6,7},{7,6},{8,9},{9,8},{10,11... | collective-permute-start | bytes 1671176 | tf_op jit(solution)/shard_map/ppermute | solution.py:275
  46.9 6.0 %collective-permute-done.10.refs_6_ = bf16[272,1024]{1,0:T(8,128)(2,1)S(1)} collective-permute-done((bf16[272,1024]{1,0:T(8,128)(2,1)}, bf16[272,1024]{1,0:T(8,128)(2,1)S(1)}, u32[]{:S(2)}, u32[]{:S(2)}) %collective-permute-start.10) | collective-permute-done | bytes 557088 | tf_op jit(solution)/shard_map/ppermute | solution.py:267
  52.9 1.6 %collective-permute-start.18 = (bf16[272,1024]{1,0:T(8,128)(2,1)S(1)}, bf16[272,1024]{1,0:T(8,128)(2,1)}, u32[]{:S(2)}, u32[]{:S(2)}) collective-permute-start(bf16[272,1024]{1,0:T(8,128)(2,1)S(1)} %collective-permute-done.10.refs_6_), channel_id=1, source_target_pairs={{0,1},{1,0},{2,3},{3,2},{4,5},{5,4},{6,7},{7,6},{8,9},{9,8},{10,11... | collective-permute-start | bytes 1671176 | tf_op jit(solution)/shard_map/ppermute | solution.py:275
  55.1 6.6 %collective-permute-start.15 = (bf16[256,1024]{1,0:T(8,128)(2,1)}, bf16[256,1024]{1,0:T(8,128)(2,1)}, u32[]{:S(2)}, u32[]{:S(2)}) collective-permute-start(bf16[256,1024]{1,0:T(8,128)(2,1)} %collective-permute-done.6.refs_3_), channel_id=1, source_target_pairs={{0,4},{6,2},{4,8},{10,6},{8,12},{14,10},{1,5},{7,3},{5,9},{11,7},{... | collective-permute-start | bytes 1572872 | tf_op jit(solution)/shard_map/ppermute | solution.py:273
  61.7 2.2 %collective-permute-start.20 = (bf16[256,1024]{1,0:T(8,128)(2,1)}, bf16[256,1024]{1,0:T(8,128)(2,1)}, u32[]{:S(2)}, u32[]{:S(2)}) collective-permute-start(bf16[256,1024]{1,0:T(8,128)(2,1)} %collective-permute-done.6.refs_3_), channel_id=1, source_target_pairs={{0,1},{1,0},{2,3},{3,2},{4,5},{5,4},{6,7},{7,6},{8,9},{9,8},{10,11... | collective-permute-start | bytes 1572872 | tf_op jit(solution)/shard_map/ppermute | solution.py:346
  64.0 0.7 slice_convert_fusion.2
  66.5 1.3 collective-permute-start.14
  67.8 0.7 slice_convert_fusion.1
  68.5 0.7 slice_convert_fusion
  69.3 0.7 slice_convert_fusion.3
  71.8 0.6 constant_dynamic-update-slice_fusion.12
  73.0 2.4 %add_reduce_fusion = (s32[4096]{0:T(1024)}, s32[1,4096]{1,0:T(1,128)S(1)}, s32[1,4096]{1,0:T(1,128)}, s32[1,4096]{1,0:T(1,128)}) fusion(s32[4,4096]{1,0:T(4,128)} %constant_dynamic-update-slice_fusion.11), kind=kLoop, calls=%fused_computation.27 | loop fusion | flops 16384 | bytes 131072 | tf_op jit(solution)/shard_map/add | solution.py:328
  75.3 0.7 add.227
  76.4 0.9 fusion.13
  77.5 0.7 pad_add_fusion.2
  78.2 1.4 %pad_add_fusion.keys_ref = s32[4,4096]{1,0:T(4,128)} fusion(s32[1,4096]{1,0:T(1,128)} %bitcast.36, s32[1,4096]{1,0:T(1,128)} %get-tuple-element.98, s32[1,4096]{1,0:T(1,128)S(1)} %get-tuple-element.88, s32[1,4096]{1,0:T(1,128)} %get-tuple-element.97), kind=kLoop, calls=%fused_computation.4 | loop fusion | flops 49152 | bytes 131072 | tf_op jit(solution)/shard_map/stack | solution.py:299
  79.7 0.7 pad_add_fusion.3
  80.4 0.6 pad_add_fusion.1.asks_ref
  81.0 3.5 %masks.1 = (bf16[4096,128]{1,0:T(8,128)(2,1)}, s32[4096,128]{1,0:T(8,128)}, bf16[128,2048]{1,0:T(8,128)(2,1)}) custom-call(s32[4,4096]{1,0:T(4,128)} %pad_add_fusion.keys_ref, s32[2,2048]{1,0:T(2,128)} %pad_add_fusion.1.asks_ref), custom_call_target="tpu_custom_call" | custom-call | flops 2200000000 | bytes 1048576 | tf_op jit(solution)/shard_map/masks/pallas_call | solution.py:301
  85.2 1.1 pad_maximum_fusion.3.w0
  86.7 0.7 collective-permute-done.22.refs_13_
  87.5 8.6 %project.1 = (bf16[4096,256]{1,0:T(8,128)(2,1)S(1)}, bf16[256,4096]{1,0:T(8,128)(2,1)S(1)}, bf16[256,2048]{1,0:T(8,128)(2,1)S(1)}) custom-call(s32[3]{0:T(128)S(1)} %pad_add_fusion.10.who_ref, bf16[512,1024]{1,0:T(8,128)(2,1)S(1)} %copy-done, bf16[528,1024]{1,0:T(8,128)(2,1)} %collective-permute-done.16.refs_1_, ...), custom_call_target="tpu_custom_call" | custom-call | flops 13200000000 | bytes 1048576 | tf_op jit(solution)/shard_map/project/pallas_call | solution.py:362
  96.0 3.5 %collective-permute-start.23 = (bf16[256,1024]{1,0:T(8,128)(2,1)S(1)}, bf16[256,1024]{1,0:T(8,128)(2,1)S(1)}, u32[]{:S(2)}, u32[]{:S(2)}) collective-permute-start(bf16[256,1024]{1,0:T(8,128)(2,1)S(1)} %pad_maximum_fusion.3.w0), channel_id=1, source_target_pairs={{0,2},{2,0},{1,3},{3,1},{4,6},{6,4},{5,7},{7,5},{8,10},{10,8},{9,1... | collective-permute-start | bytes 1572872 | tf_op jit(solution)/shard_map/ppermute | solution.py:378
  99.5 13.8 %attend.3 = bf16[1024,256]{1,0:T(8,128)(2,1)S(1)} custom-call(s32[80]{0:T(128)S(1)} %reshape.222.tab_ref, f32[4]{0:T(128)S(1)} %dynamic-slice_bitcast_fusion.delta_ref, bf16[4096,256]{1,0:T(8,128)(2,1)S(1)} %get-tuple-element.69.k_ref, bf16[256,4096]{1,0:T(8,128)(2,1)S(1)} %get-tuple-element.70.vt_ref, bf16[256,2048]{1,0:T(8,128)(2,1)S(1)} %get-tuple-element.71.qt_ref, ...), custom_call_target="tpu_custom_call" | custom-call | flops 17600000000 | bytes 1048576 | tf_op jit(solution)/shard_map/attend/pallas_call | solution.py:381
  113.5 0.7 collective-permute-start.26
  114.2 1.7 %collective-permute-start.25 = (bf16[512,256]{1,0:T(8,128)(2,1)S(1)}, bf16[512,256]{1,0:T(8,128)(2,1)S(1)}, u32[]{:S(2)}, u32[]{:S(2)}) collective-permute-start(bf16[512,256]{1,0:T(8,128)(2,1)S(1)} %get-tuple-element.77), channel_id=1, source_target_pairs={{0,3},{1,2},{2,1},{3,0},{4,7},{5,6},{6,5},{7,4},{8,11},{9,10},{10,... | collective-permute-start | bytes 786440 | tf_op jit(solution)/shard_map/ppermute | solution.py:401
  115.9 13.6 %attend.2 = bf16[1024,256]{1,0:T(8,128)(2,1)S(1)} custom-call(s32[80]{0:T(128)S(1)} %reshape.222.tab_ref, f32[4]{0:T(128)S(1)} %dynamic-slice_bitcast_fusion.delta_ref, bf16[4096,256]{1,0:T(8,128)(2,1)S(1)} %get-tuple-element.69.k_ref, bf16[256,4096]{1,0:T(8,128)(2,1)S(1)} %get-tuple-element.70.vt_ref, bf16[256,2048]{1,0:T(8,128)(2,1)S(1)} %get-tuple-element.71.qt_ref, ...), custom_call_target="tpu_custom_call" | custom-call | flops 17600000000 | bytes 1048576 | tf_op jit(solution)/shard_map/attend/pallas_call | solution.py:381
  129.9 1.3 collective-permute-done.27.a1
  131.2 2.9 %mixed.1 = bf16[512,1024]{1,0:T(8,128)(2,1)} custom-call(s32[2]{0:T(128)S(1)} %pad_add_fusion.6.who_ref, bf16[512,256]{1,0:T(8,128)(2,1)S(1)} %get-tuple-element.96.a0, bf16[512,256]{1,0:T(8,128)(2,1)S(1)} %collective-permute-done.27.a1, bf16[512,256]{1,0:T(8,128)(2,1)S(1)} %collective-permute-done.24.a2, bf16[512,256]{1,0:T(8,128)(2,1)S(1)} %collective-permute-done.25.a3, ...), custom_call_target="tpu_custom_call" | custom-call | flops 3300000000 | bytes 1048576 | tf_op jit(solution)/shard_map/mixed/pallas_call | solution.py:408
  (117 shorter events, 13.2 us)
Async XLA Ops:
  0.6 4.6 %copy-start.4 = (bf16[64,1024]{1,0:T(8,128)(2,1)S(1)}, bf16[64,1024]{1,0:T(8,128)(2,1)}, u32[]{:S(2)}) copy-start(bf16[64,1024]{1,0:T(8,128)(2,1)} %param.9) | copy-start | bytes 393220
  0.6 9.4 %copy-start.8 = (s32[512]{0:T(512)S(1)}, s32[512]{0:T(512)}, u32[]{:S(2)}) copy-start(s32[512]{0:T(512)} %param.12) | copy-start | bytes 6148
  0.6 9.4 %copy-start.9 = (s32[512]{0:T(512)S(1)}, s32[512]{0:T(512)}, u32[]{:S(2)}) copy-start(s32[512]{0:T(512)} %param.13) | copy-start | bytes 6148
  0.6 9.4 %copy-start.10 = (s32[512]{0:T(512)S(1)}, s32[512]{0:T(512)}, u32[]{:S(2)}) copy-start(s32[512]{0:T(512)} %param.11) | copy-start | bytes 6148
  0.6 10.1 %copy-start = (bf16[512,1024]{1,0:T(8,128)(2,1)S(1)}, bf16[512,1024]{1,0:T(8,128)(2,1)}, u32[]{:S(2)}) copy-start(bf16[512,1024]{1,0:T(8,128)(2,1)} %refs_0_) | copy-start | bytes 3145732
  2.4 14.5 %collective-permute-start = (bf16[64,384]{1,0:T(8,128)(2,1)}, bf16[64,384]{1,0:T(8,128)(2,1)S(1)}, u32[]{:S(2)}, u32[]{:S(2)}) collective-permute-start(bf16[64,384]{1,0:T(8,128)(2,1)} %get-tuple-element.45), channel_id=1, source_target_pairs={{0,1},{1,0},{2,3},{3,2},{4,5},{5,4},{6,7},{7,6},{8,9},{9,8},{10,11... | collective-permute-start | bytes 147464 | tf_op jit(solution)/shard_map/ppermute | solution.py:201
  2.5 15.5 %collective-permute-start.1 = (bf16[64,384]{1,0:T(8,128)(2,1)}, bf16[64,384]{1,0:T(8,128)(2,1)S(1)}, u32[]{:S(2)}, u32[]{:S(2)}) collective-permute-start(bf16[64,384]{1,0:T(8,128)(2,1)} %get-tuple-element.46), channel_id=1, source_target_pairs={{0,2},{2,0},{1,3},{3,1},{4,6},{6,4},{5,7},{7,5},{8,10},{10,8},{9,1... | collective-permute-start | bytes 147464 | tf_op jit(solution)/shard_map/ppermute | solution.py:202
  5.2 12.9 %collective-permute-start.2 = (bf16[64,384]{1,0:T(8,128)(2,1)}, bf16[64,384]{1,0:T(8,128)(2,1)S(1)}, u32[]{:S(2)}, u32[]{:S(2)}) collective-permute-start(bf16[64,384]{1,0:T(8,128)(2,1)} %get-tuple-element.47), channel_id=1, source_target_pairs={{0,3},{1,2},{2,1},{3,0},{4,7},{5,6},{6,5},{7,4},{8,11},{9,10},{10,... | collective-permute-start | bytes 147464 | tf_op jit(solution)/shard_map/ppermute | solution.py:203
  5.2 13.4 %collective-permute-start.3 = (bf16[64,1024]{1,0:T(8,128)(2,1)S(1)}, bf16[64,1024]{1,0:T(8,128)(2,1)S(1)}, u32[]{:S(2)}, u32[]{:S(2)}) collective-permute-start(bf16[64,1024]{1,0:T(8,128)(2,1)S(1)} %copy-done.4), channel_id=1, source_target_pairs={{0,4},{4,8},{8,12},{12,0},{1,5},{5,9},{9,13},{13,1},{2,6},{6,10},{... | collective-permute-start | bytes 393224 | tf_op jit(solution)/shard_map/ppermute | solution.py:213
  6.9 14.6 %collective-permute-start.4 = (bf16[64,1024]{1,0:T(8,128)(2,1)S(1)}, bf16[64,1024]{1,0:T(8,128)(2,1)S(1)}, u32[]{:S(2)}, u32[]{:S(2)}) collective-permute-start(bf16[64,1024]{1,0:T(8,128)(2,1)S(1)} %copy-done.4), channel_id=1, source_target_pairs={{0,8},{4,12},{8,0},{12,4},{1,9},{5,13},{9,1},{13,5},{2,10},{6,14},... | collective-permute-start | bytes 393224 | tf_op jit(solution)/shard_map/ppermute | solution.py:213
  12.6 10.7 %copy-start.11 = (f32[2,16]{1,0:T(2,128)S(1)}, f32[2,16]{1,0:T(2,128)}, u32[]{:S(2)}) copy-start(f32[2,16]{1,0:T(2,128)} %param.10) | copy-start | bytes 388
  16.9 4.5 %collective-permute-start.5 = (bf16[64,1024]{1,0:T(8,128)(2,1)S(1)}, bf16[64,1024]{1,0:T(8,128)(2,1)S(1)}, u32[]{:S(2)}, u32[]{:S(2)}) collective-permute-start(bf16[64,1024]{1,0:T(8,128)(2,1)S(1)} %copy-done.4), channel_id=1, source_target_pairs={{0,12},{4,0},{8,4},{12,8},{1,13},{5,1},{9,5},{13,9},{2,14},{6,2},{... | collective-permute-start | bytes 393224 | tf_op jit(solution)/shard_map/ppermute | solution.py:213
  18.1 7.4 %collective-permute-start.7 = (bf16[256,384]{1,0:T(8,128)(2,1)S(1)}, bf16[256,384]{1,0:T(8,128)(2,1)S(1)}, u32[]{:S(2)}, u32[]{:S(2)}) collective-permute-start(bf16[256,384]{1,0:T(8,128)(2,1)S(1)} %get-tuple-element.100), channel_id=1, source_target_pairs={{0,4},{4,8},{8,12},{12,0},{1,5},{5,9},{9,13},{13,1},{2,6},{6,10},{... | collective-permute-start | bytes 589832 | tf_op jit(solution)/shard_map/ppermute | solution.py:213
  18.5 15.7 %collective-permute-start.8 = (bf16[256,384]{1,0:T(8,128)(2,1)S(1)}, bf16[256,384]{1,0:T(8,128)(2,1)S(1)}, u32[]{:S(2)}, u32[]{:S(2)}) collective-permute-start(bf16[256,384]{1,0:T(8,128)(2,1)S(1)} %get-tuple-element.100), channel_id=1, source_target_pairs={{0,8},{4,12},{8,0},{12,4},{1,9},{5,13},{9,1},{13,5},{2,10},{6,14},... | collective-permute-start | bytes 589832 | tf_op jit(solution)/shard_map/ppermute | solution.py:213
  18.6 2.9 %copy-start.5 = (bf16[64,1024]{1,0:T(8,128)(2,1)}, bf16[64,1024]{1,0:T(8,128)(2,1)S(1)}, u32[]{:S(2)}) copy-start(bf16[64,1024]{1,0:T(8,128)(2,1)S(1)} %collective-permute-done.3) | copy-start | bytes 393220
  18.6 15.8 %collective-permute-start.9 = (bf16[256,384]{1,0:T(8,128)(2,1)S(1)}, bf16[256,384]{1,0:T(8,128)(2,1)S(1)}, u32[]{:S(2)}, u32[]{:S(2)}) collective-permute-start(bf16[256,384]{1,0:T(8,128)(2,1)S(1)} %get-tuple-element.100), channel_id=1, source_target_pairs={{0,12},{4,0},{8,4},{12,8},{1,13},{5,1},{9,5},{13,9},{2,14},{6,2},{... | collective-permute-start | bytes 589832 | tf_op jit(solution)/shard_map/ppermute | solution.py:213
  21.5 0.6 copy-start.6
  22.1 15.0 %copy-start.7 = (bf16[64,1024]{1,0:T(8,128)(2,1)}, bf16[64,1024]{1,0:T(8,128)(2,1)S(1)}, u32[]{:S(2)}) copy-start(bf16[64,1024]{1,0:T(8,128)(2,1)S(1)} %collective-permute-done.5) | copy-start | bytes 393220
  22.1 15.0 %collective-permute-start.11 = (bf16[272,1024]{1,0:T(8,128)(2,1)}, bf16[272,1024]{1,0:T(8,128)(2,1)S(1)}, u32[]{:S(2)}, u32[]{:S(2)}) collective-permute-start(bf16[272,1024]{1,0:T(8,128)(2,1)} %pad_maximum_fusion.2), channel_id=1, source_target_pairs={{0,2},{2,0},{1,3},{3,1},{4,6},{6,4},{5,7},{7,5},{8,10},{10,8},{9,1... | collective-permute-start | bytes 1671176 | tf_op jit(solution)/shard_map/ppermute | solution.py:265
  23.9 31.2 %collective-permute-start.6 = (bf16[256,1024]{1,0:T(8,128)(2,1)}, bf16[256,1024]{1,0:T(8,128)(2,1)}, u32[]{:S(2)}, u32[]{:S(2)}) collective-permute-start(bf16[256,1024]{1,0:T(8,128)(2,1)} %get-tuple-element.53), channel_id=1, source_target_pairs={{0,2},{2,0},{1,3},{3,1},{4,6},{6,4},{5,7},{7,5},{8,10},{10,8},{9,1... | collective-permute-start | bytes 1572872 | tf_op jit(solution)/shard_map/ppermute | solution.py:265
  34.4 18.5 %collective-permute-start.10 = (bf16[272,1024]{1,0:T(8,128)(2,1)}, bf16[272,1024]{1,0:T(8,128)(2,1)S(1)}, u32[]{:S(2)}, u32[]{:S(2)}) collective-permute-start(bf16[272,1024]{1,0:T(8,128)(2,1)} %pad_maximum_fusion.2), channel_id=1, source_target_pairs={{4,0},{2,6},{8,4},{6,10},{12,8},{10,14},{5,1},{3,7},{9,5},{7,11},{... | collective-permute-start | bytes 1671176 | tf_op jit(solution)/shard_map/ppermute | solution.py:267
  35.8 19.3 %collective-permute-start.13 = (bf16[1024,384]{1,0:T(8,128)(2,1)S(1)}, bf16[1024,384]{1,0:T(8,128)(2,1)}, u32[]{:S(2)}, u32[]{:S(2)}) collective-permute-start(bf16[1024,384]{1,0:T(8,128)(2,1)S(1)} %constant_dynamic-update-slice_fusion.4.refs_14_), channel_id=1, source_target_pairs={{0,16},{16,0},{1,17},{17,1},{2,18},{18,2},{3,19},{19,3},{4,20},{20... | collective-permute-start | bytes 2359304 | tf_op jit(solution)/shard_map/ppermute | solution.py:253
  37.1 18.0 %collective-permute-start.12 = (bf16[272,1024]{1,0:T(8,128)(2,1)S(1)}, bf16[272,1024]{1,0:T(8,128)(2,1)S(1)}, u32[]{:S(2)}, u32[]{:S(2)}) collective-permute-start(bf16[272,1024]{1,0:T(8,128)(2,1)S(1)} %collective-permute-done.11.refs_2_), channel_id=1, source_target_pairs={{0,4},{6,2},{4,8},{10,6},{8,12},{14,10},{1,5},{7,3},{5,9},{11,7},{... | collective-permute-start | bytes 1671176 | tf_op jit(solution)/shard_map/ppermute | solution.py:268
  44.0 19.9 %collective-permute-start.17 = (bf16[272,1024]{1,0:T(8,128)(2,1)S(1)}, bf16[272,1024]{1,0:T(8,128)(2,1)}, u32[]{:S(2)}, u32[]{:S(2)}) collective-permute-start(bf16[272,1024]{1,0:T(8,128)(2,1)S(1)} %collective-permute-done.11.refs_2_), channel_id=1, source_target_pairs={{0,1},{1,0},{2,3},{3,2},{4,5},{5,4},{6,7},{7,6},{8,9},{9,8},{10,11... | collective-permute-start | bytes 1671176 | tf_op jit(solution)/shard_map/ppermute | solution.py:275
  52.9 13.6 %collective-permute-start.18 = (bf16[272,1024]{1,0:T(8,128)(2,1)S(1)}, bf16[272,1024]{1,0:T(8,128)(2,1)}, u32[]{:S(2)}, u32[]{:S(2)}) collective-permute-start(bf16[272,1024]{1,0:T(8,128)(2,1)S(1)} %collective-permute-done.10.refs_6_), channel_id=1, source_target_pairs={{0,1},{1,0},{2,3},{3,2},{4,5},{5,4},{6,7},{7,6},{8,9},{9,8},{10,11... | collective-permute-start | bytes 1671176 | tf_op jit(solution)/shard_map/ppermute | solution.py:275
  55.1 29.4 %collective-permute-start.15 = (bf16[256,1024]{1,0:T(8,128)(2,1)}, bf16[256,1024]{1,0:T(8,128)(2,1)}, u32[]{:S(2)}, u32[]{:S(2)}) collective-permute-start(bf16[256,1024]{1,0:T(8,128)(2,1)} %collective-permute-done.6.refs_3_), channel_id=1, source_target_pairs={{0,4},{6,2},{4,8},{10,6},{8,12},{14,10},{1,5},{7,3},{5,9},{11,7},{... | collective-permute-start | bytes 1572872 | tf_op jit(solution)/shard_map/ppermute | solution.py:273
  61.7 24.7 %collective-permute-start.20 = (bf16[256,1024]{1,0:T(8,128)(2,1)}, bf16[256,1024]{1,0:T(8,128)(2,1)}, u32[]{:S(2)}, u32[]{:S(2)}) collective-permute-start(bf16[256,1024]{1,0:T(8,128)(2,1)} %collective-permute-done.6.refs_3_), channel_id=1, source_target_pairs={{0,1},{1,0},{2,3},{3,2},{4,5},{5,4},{6,7},{7,6},{8,9},{9,8},{10,11... | collective-permute-start | bytes 1572872 | tf_op jit(solution)/shard_map/ppermute | solution.py:346
  63.9 5.3 %collective-permute-start.16 = (bf16[528,1024]{1,0:T(8,128)(2,1)}, bf16[528,1024]{1,0:T(8,128)(2,1)}, u32[]{:S(2)}, u32[]{:S(2)}) collective-permute-start(bf16[528,1024]{1,0:T(8,128)(2,1)} %pad_maximum_fusion), channel_id=1, source_target_pairs={{0,1},{1,0},{2,3},{3,2},{4,5},{5,4},{6,7},{7,6},{8,9},{9,8},{10,11... | collective-permute-start | bytes 3244040 | tf_op jit(solution)/shard_map/ppermute | solution.py:275
  64.7 3.8 %collective-permute-start.19 = (bf16[272,1024]{1,0:T(8,128)(2,1)S(1)}, bf16[272,1024]{1,0:T(8,128)(2,1)}, u32[]{:S(2)}, u32[]{:S(2)}) collective-permute-start(bf16[272,1024]{1,0:T(8,128)(2,1)S(1)} %collective-permute-done.12.refs_10_), channel_id=1, source_target_pairs={{0,1},{1,0},{2,3},{3,2},{4,5},{5,4},{6,7},{7,6},{8,9},{9,8},{10,11... | collective-permute-start | bytes 1671176 | tf_op jit(solution)/shard_map/ppermute | solution.py:275
  66.5 18.0 %collective-permute-start.14 = (bf16[256,1024]{1,0:T(8,128)(2,1)}, bf16[256,1024]{1,0:T(8,128)(2,1)}, u32[]{:S(2)}, u32[]{:S(2)}) collective-permute-start(bf16[256,1024]{1,0:T(8,128)(2,1)} %get-tuple-element.53), channel_id=1, source_target_pairs={{4,0},{2,6},{8,4},{6,10},{12,8},{10,14},{5,1},{3,7},{9,5},{7,11},{... | collective-permute-start | bytes 1572872 | tf_op jit(solution)/shard_map/ppermute | solution.py:272
  81.0 4.1 %copy-start.12 = (f32[1,16]{1,0:T(1,128)S(1)}, f32[1,16]{1,0:T(1,128)}, u32[]{:S(2)}) copy-start(f32[1,16]{1,0:T(1,128)} %slice_subtract_fusion) | copy-start | bytes 196
  84.5 2.2 %collective-permute-start.21 = (bf16[256,1024]{1,0:T(8,128)(2,1)}, bf16[256,1024]{1,0:T(8,128)(2,1)S(1)}, u32[]{:S(2)}, u32[]{:S(2)}) collective-permute-start(bf16[256,1024]{1,0:T(8,128)(2,1)} %collective-permute-done.14.refs_7_), channel_id=1, source_target_pairs={{0,1},{1,0},{2,3},{3,2},{4,5},{5,4},{6,7},{7,6},{8,9},{9,8},{10,11... | collective-permute-start | bytes 1572872 | tf_op jit(solution)/shard_map/ppermute | solution.py:349
  84.6 2.9 %collective-permute-start.22 = (bf16[256,1024]{1,0:T(8,128)(2,1)}, bf16[256,1024]{1,0:T(8,128)(2,1)S(1)}, u32[]{:S(2)}, u32[]{:S(2)}) collective-permute-start(bf16[256,1024]{1,0:T(8,128)(2,1)} %collective-permute-done.15.refs_11_), channel_id=1, source_target_pairs={{0,1},{1,0},{2,3},{3,2},{4,5},{5,4},{6,7},{7,6},{8,9},{9,8},{10,11... | collective-permute-start | bytes 1572872 | tf_op jit(solution)/shard_map/ppermute | solution.py:349
  86.3 13.2 %copy-start.1 = (s32[4096,128]{1,0:T(8,128)S(1)}, s32[4096,128]{1,0:T(8,128)}, u32[]{:S(2)}) copy-start(s32[4096,128]{1,0:T(8,128)} %get-tuple-element.74.vk_ref) | copy-start | bytes 6291460
  86.4 13.2 %copy-start.2 = (bf16[4096,128]{1,0:T(8,128)(2,1)S(1)}, bf16[4096,128]{1,0:T(8,128)(2,1)}, u32[]{:S(2)}) copy-start(bf16[4096,128]{1,0:T(8,128)(2,1)} %get-tuple-element.72.fk_ref) | copy-start | bytes 3145732
  86.4 13.2 %copy-start.3 = (bf16[128,2048]{1,0:T(8,128)(2,1)S(1)}, bf16[128,2048]{1,0:T(8,128)(2,1)}, u32[]{:S(2)}) copy-start(bf16[128,2048]{1,0:T(8,128)(2,1)} %get-tuple-element.73.fqt_ref) | copy-start | bytes 1572868
  96.0 17.4 %collective-permute-start.23 = (bf16[256,1024]{1,0:T(8,128)(2,1)S(1)}, bf16[256,1024]{1,0:T(8,128)(2,1)S(1)}, u32[]{:S(2)}, u32[]{:S(2)}) collective-permute-start(bf16[256,1024]{1,0:T(8,128)(2,1)S(1)} %pad_maximum_fusion.3.w0), channel_id=1, source_target_pairs={{0,2},{2,0},{1,3},{3,1},{4,6},{6,4},{5,7},{7,5},{8,10},{10,8},{9,1... | collective-permute-start | bytes 1572872 | tf_op jit(solution)/shard_map/ppermute | solution.py:378
  113.5 16.0 %collective-permute-start.26 = (bf16[2,256,1024]{2,1,0:T(8,128)(2,1)S(1)}, bf16[2,256,1024]{2,1,0:T(8,128)(2,1)S(1)}, u32[]{:S(2)}, u32[]{:S(2)}) collective-permute-start(bf16[2,256,1024]{2,1,0:T(8,128)(2,1)S(1)} %pad_maximum_fusion.1), channel_id=1, source_target_pairs={{0,1},{1,0},{2,3},{3,2},{4,5},{5,4},{6,7},{7,6},{8,9},{9,8},{10,11... | collective-permute-start | bytes 3145736 | tf_op jit(solution)/shard_map/ppermute | solution.py:402
  114.2 15.3 %collective-permute-start.24 = (bf16[512,256]{1,0:T(8,128)(2,1)S(1)}, bf16[512,256]{1,0:T(8,128)(2,1)S(1)}, u32[]{:S(2)}, u32[]{:S(2)}) collective-permute-start(bf16[512,256]{1,0:T(8,128)(2,1)S(1)} %get-tuple-element.76), channel_id=1, source_target_pairs={{0,2},{2,0},{1,3},{3,1},{4,6},{6,4},{5,7},{7,5},{8,10},{10,8},{9,1... | collective-permute-start | bytes 786440 | tf_op jit(solution)/shard_map/ppermute | solution.py:400
  114.2 15.3 %collective-permute-start.25 = (bf16[512,256]{1,0:T(8,128)(2,1)S(1)}, bf16[512,256]{1,0:T(8,128)(2,1)S(1)}, u32[]{:S(2)}, u32[]{:S(2)}) collective-permute-start(bf16[512,256]{1,0:T(8,128)(2,1)S(1)} %get-tuple-element.77), channel_id=1, source_target_pairs={{0,3},{1,2},{2,1},{3,0},{4,7},{5,6},{6,5},{7,4},{8,11},{9,10},{10,... | collective-permute-start | bytes 786440 | tf_op jit(solution)/shard_map/ppermute | solution.py:401
  129.6 1.6 %collective-permute-start.27 = (bf16[512,256]{1,0:T(8,128)(2,1)S(1)}, bf16[512,256]{1,0:T(8,128)(2,1)S(1)}, u32[]{:S(2)}, u32[]{:S(2)}) collective-permute-start(bf16[512,256]{1,0:T(8,128)(2,1)S(1)} %get-tuple-element.79), channel_id=1, source_target_pairs={{0,1},{1,0},{2,3},{3,2},{4,5},{5,4},{6,7},{7,6},{8,9},{9,8},{10,11... | collective-permute-start | bytes 786440 | tf_op jit(solution)/shard_map/ppermute | solution.py:406

commit v5 on v4

--- a/solution.py
+++ b/solution.py
@@ -353,7 +353,7 @@
         held += [((i + 5) * rows, cut, peers[i + 1]), ((i + 5) * rows + cut, cut, rest[i])]
     plan = tuple((at, n) for at, n, _ in held)
     xs = [x for _, _, x in held]
-    limit = pltpu.CompilerParams(vmem_limit_bytes=28 << 20)
+    limit = pltpu.CompilerParams(vmem_limit_bytes=24 << 20)
     queries = {}
     for at, _ in plan:
         block = at // rows

time: 135 us -> 135 us (level)
  no operation moved by 1% of the time
where the time goes in v5:
time: 135 us; the launch traced here: 134 us
  Pallas kernels  44.2 us (33%)
  starting transfers between devices  42.8 us (32%)
  waiting for transfers between devices  18.7 us (14%)
  other arithmetic  16.2 us (12%)
  local copies, waits for them, and re-layouts  11.9 us (9%)
    pallas_call x2, Pallas kernels, attend(): pl.pallas_call(functools.partial(attend_kernel, hsize, q0, nq), out_shape...  27.4 us
    ppermute x6, waiting for transfers between devices, turns(): lax.ppermute(block, 'plane', [(i, (i + s) % planes) for i in range(planes)])  10.3 us
    pallas_call x1, Pallas kernels, local(): pl.pallas_call(functools.partial(project_kernel, cols, plan, queries, pla...  8.56 us
    ppermute x6, starting transfers between devices, turns(): lax.ppermute(block, 'plane', [(i, (i + s) % planes) for i in range(planes)])  8.44 us
    ppermute x1, starting transfers between devices, local(): theirs = [lax.ppermute(other[0], pair, passed)]  6.92 us
    ppermute x1, starting transfers between devices, local(): theirs.append(lax.ppermute(passing, pair, passed))  6.59 us
    ppermute x1, waiting for transfers between devices, local(): mine = [lax.ppermute(first_z, pair, native)]  5.98 us
    unnamed x40, local copies, waits for them, and re-layouts  5.88 us
  transfers between devices with their start and end apart: 28, of which 7 were waited for; matrix products, arithmetic and copies ran while one was open for 20% of the time, Pallas kernels for 23%

profile of v5, /device:TPU:1, one launch (start us, length us, event | category | flops | bytes accessed | tf_op | source)
XLA Modules:
  0.0 134.1 jit_solution(2418131520951300874)
XLA Ops:
  0.6 1.8 %pick.1 = (bf16[64,384]{1,0:T(8,128)(2,1)}, bf16[64,384]{1,0:T(8,128)(2,1)}, bf16[64,384]{1,0:T(8,128)(2,1)}, bf16[64,384]{1,0:T(8,128)(2,1)}) custom-call(s32[2]{0:T(128)} %pad_add_fusion.7.who_ref, bf16[64,3072]{1,0:T(8,128)(2,1)} %w_ref.1), custom_call_target="tpu_custom_call" | custom-call | flops 1100000000 | bytes 1048576 | tf_op jit(solution)/shard_map/pick/pallas_call | solution.py:239
  2.5 2.7 %collective-permute-start.1 = (bf16[64,384]{1,0:T(8,128)(2,1)}, bf16[64,384]{1,0:T(8,128)(2,1)S(1)}, u32[]{:S(2)}, u32[]{:S(2)}) collective-permute-start(bf16[64,384]{1,0:T(8,128)(2,1)} %get-tuple-element.46), channel_id=1, source_target_pairs={{0,2},{2,0},{1,3},{3,1},{4,6},{6,4},{5,7},{7,5},{8,10},{10,8},{9,1... | collective-permute-start | bytes 147464 | tf_op jit(solution)/shard_map/ppermute | solution.py:202
  5.2 1.7 %collective-permute-start.3 = (bf16[64,1024]{1,0:T(8,128)(2,1)S(1)}, bf16[64,1024]{1,0:T(8,128)(2,1)S(1)}, u32[]{:S(2)}, u32[]{:S(2)}) collective-permute-start(bf16[64,1024]{1,0:T(8,128)(2,1)S(1)} %copy-done.4), channel_id=1, source_target_pairs={{0,4},{4,8},{8,12},{12,0},{1,5},{5,9},{9,13},{13,1},{2,6},{6,10},{... | collective-permute-start | bytes 393224 | tf_op jit(solution)/shard_map/ppermute | solution.py:213
  6.9 2.3 %collective-permute-start.4 = (bf16[64,1024]{1,0:T(8,128)(2,1)S(1)}, bf16[64,1024]{1,0:T(8,128)(2,1)S(1)}, u32[]{:S(2)}, u32[]{:S(2)}) collective-permute-start(bf16[64,1024]{1,0:T(8,128)(2,1)S(1)} %copy-done.4), channel_id=1, source_target_pairs={{0,8},{4,12},{8,0},{12,4},{1,9},{5,13},{9,1},{13,5},{2,10},{6,14},... | collective-permute-start | bytes 393224 | tf_op jit(solution)/shard_map/ppermute | solution.py:213
  9.2 0.8 constant_dynamic-update-slice_fusion.10
  10.7 0.9 fusion.25
  11.6 1.1 pad_maximum_fusion
  12.6 0.8 pad_maximum_fusion.2
  15.6 0.7 and.202
  16.3 0.6 copy.11
  16.9 1.1 collective-permute-start.5
  18.6 2.9 %collective-permute-start.9 = (bf16[256,384]{1,0:T(8,128)(2,1)S(1)}, bf16[256,384]{1,0:T(8,128)(2,1)S(1)}, u32[]{:S(2)}, u32[]{:S(2)}) collective-permute-start(bf16[256,384]{1,0:T(8,128)(2,1)S(1)} %get-tuple-element.100), channel_id=1, source_target_pairs={{0,12},{4,0},{8,4},{12,8},{1,13},{5,1},{9,5},{13,9},{2,14},{6,2},{... | collective-permute-start | bytes 589832 | tf_op jit(solution)/shard_map/ppermute | solution.py:213
  21.5 0.6 copy-done.6
  22.1 1.2 collective-permute-start.11
  24.1 1.3 collective-permute-done.7
  25.4 8.8 %collective-permute-done.8 = bf16[256,384]{1,0:T(8,128)(2,1)S(1)} collective-permute-done((bf16[256,384]{1,0:T(8,128)(2,1)S(1)}, bf16[256,384]{1,0:T(8,128)(2,1)S(1)}, u32[]{:S(2)}, u32[]{:S(2)}) %collective-permute-start.8) | collective-permute-done | bytes 196640 | tf_op jit(solution)/shard_map/ppermute | solution.py:213
  34.4 1.3 collective-permute-start.10
  35.8 1.3 collective-permute-start.13
  37.1 6.9 %collective-permute-start.12 = (bf16[272,1024]{1,0:T(8,128)(2,1)S(1)}, bf16[272,1024]{1,0:T(8,128)(2,1)S(1)}, u32[]{:S(2)}, u32[]{:S(2)}) collective-permute-start(bf16[272,1024]{1,0:T(8,128)(2,1)S(1)} %collective-permute-done.11.refs_2_), channel_id=1, source_target_pairs={{0,4},{6,2},{4,8},{10,6},{8,12},{14,10},{1,5},{7,3},{5,9},{11,7},{... | collective-permute-start | bytes 1671176 | tf_op jit(solution)/shard_map/ppermute | solution.py:268
  44.0 1.7 %collective-permute-start.17 = (bf16[272,1024]{1,0:T(8,128)(2,1)S(1)}, bf16[272,1024]{1,0:T(8,128)(2,1)}, u32[]{:S(2)}, u32[]{:S(2)}) collective-permute-start(bf16[272,1024]{1,0:T(8,128)(2,1)S(1)} %collective-permute-done.11.refs_2_), channel_id=1, source_target_pairs={{0,1},{1,0},{2,3},{3,2},{4,5},{5,4},{6,7},{7,6},{8,9},{9,8},{10,11... | collective-permute-start | bytes 1671176 | tf_op jit(solution)/shard_map/ppermute | solution.py:275
  46.9 6.0 %collective-permute-done.10.refs_6_ = bf16[272,1024]{1,0:T(8,128)(2,1)S(1)} collective-permute-done((bf16[272,1024]{1,0:T(8,128)(2,1)}, bf16[272,1024]{1,0:T(8,128)(2,1)S(1)}, u32[]{:S(2)}, u32[]{:S(2)}) %collective-permute-start.10) | collective-permute-done | bytes 557088 | tf_op jit(solution)/shard_map/ppermute | solution.py:267
  52.9 1.6 %collective-permute-start.18 = (bf16[272,1024]{1,0:T(8,128)(2,1)S(1)}, bf16[272,1024]{1,0:T(8,128)(2,1)}, u32[]{:S(2)}, u32[]{:S(2)}) collective-permute-start(bf16[272,1024]{1,0:T(8,128)(2,1)S(1)} %collective-permute-done.10.refs_6_), channel_id=1, source_target_pairs={{0,1},{1,0},{2,3},{3,2},{4,5},{5,4},{6,7},{7,6},{8,9},{9,8},{10,11... | collective-permute-start | bytes 1671176 | tf_op jit(solution)/shard_map/ppermute | solution.py:275
  55.1 6.6 %collective-permute-start.15 = (bf16[256,1024]{1,0:T(8,128)(2,1)}, bf16[256,1024]{1,0:T(8,128)(2,1)}, u32[]{:S(2)}, u32[]{:S(2)}) collective-permute-start(bf16[256,1024]{1,0:T(8,128)(2,1)} %collective-permute-done.6.refs_3_), channel_id=1, source_target_pairs={{0,4},{6,2},{4,8},{10,6},{8,12},{14,10},{1,5},{7,3},{5,9},{11,7},{... | collective-permute-start | bytes 1572872 | tf_op jit(solution)/shard_map/ppermute | solution.py:273
  61.7 2.2 %collective-permute-start.20 = (bf16[256,1024]{1,0:T(8,128)(2,1)}, bf16[256,1024]{1,0:T(8,128)(2,1)}, u32[]{:S(2)}, u32[]{:S(2)}) collective-permute-start(bf16[256,1024]{1,0:T(8,128)(2,1)} %collective-permute-done.6.refs_3_), channel_id=1, source_target_pairs={{0,1},{1,0},{2,3},{3,2},{4,5},{5,4},{6,7},{7,6},{8,9},{9,8},{10,11... | collective-permute-start | bytes 1572872 | tf_op jit(solution)/shard_map/ppermute | solution.py:346
  64.0 0.7 slice_convert_fusion.2
  66.5 1.3 collective-permute-start.14
  67.8 0.7 slice_convert_fusion.1
  68.5 0.7 slice_convert_fusion
  69.3 0.7 slice_convert_fusion.3
  71.8 0.6 constant_dynamic-update-slice_fusion.12
  73.0 2.4 %add_reduce_fusion = (s32[4096]{0:T(1024)}, s32[1,4096]{1,0:T(1,128)S(1)}, s32[1,4096]{1,0:T(1,128)}, s32[1,4096]{1,0:T(1,128)}) fusion(s32[4,4096]{1,0:T(4,128)} %constant_dynamic-update-slice_fusion.11), kind=kLoop, calls=%fused_computation.27 | loop fusion | flops 16384 | bytes 131072 | tf_op jit(solution)/shard_map/add | solution.py:328
  75.3 0.7 add.227
  76.4 0.9 fusion.13
  77.5 0.7 pad_add_fusion.2
  78.2 1.4 %pad_add_fusion.keys_ref = s32[4,4096]{1,0:T(4,128)} fusion(s32[1,4096]{1,0:T(1,128)} %bitcast.36, s32[1,4096]{1,0:T(1,128)} %get-tuple-element.98, s32[1,4096]{1,0:T(1,128)S(1)} %get-tuple-element.88, s32[1,4096]{1,0:T(1,128)} %get-tuple-element.97), kind=kLoop, calls=%fused_computation.4 | loop fusion | flops 49152 | bytes 131072 | tf_op jit(solution)/shard_map/stack | solution.py:299
  79.7 0.7 pad_add_fusion.3
  80.4 0.6 pad_add_fusion.1.asks_ref
  81.0 3.5 %masks.1 = (bf16[4096,128]{1,0:T(8,128)(2,1)}, s32[4096,128]{1,0:T(8,128)}, bf16[128,2048]{1,0:T(8,128)(2,1)}) custom-call(s32[4,4096]{1,0:T(4,128)} %pad_add_fusion.keys_ref, s32[2,2048]{1,0:T(2,128)} %pad_add_fusion.1.asks_ref), custom_call_target="tpu_custom_call" | custom-call | flops 2200000000 | bytes 1048576 | tf_op jit(solution)/shard_map/masks/pallas_call | solution.py:301
  85.2 1.1 pad_maximum_fusion.3.w0
  86.7 0.7 collective-permute-done.22.refs_13_
  87.5 8.6 %project.1 = (bf16[4096,256]{1,0:T(8,128)(2,1)S(1)}, bf16[256,4096]{1,0:T(8,128)(2,1)S(1)}, bf16[256,2048]{1,0:T(8,128)(2,1)S(1)}) custom-call(s32[3]{0:T(128)S(1)} %pad_add_fusion.10.who_ref, bf16[512,1024]{1,0:T(8,128)(2,1)S(1)} %copy-done, bf16[528,1024]{1,0:T(8,128)(2,1)} %collective-permute-done.16.refs_1_, ...), custom_call_target="tpu_custom_call" | custom-call | flops 13200000000 | bytes 1048576 | tf_op jit(solution)/shard_map/project/pallas_call | solution.py:362
  96.0 3.5 %collective-permute-start.23 = (bf16[256,1024]{1,0:T(8,128)(2,1)S(1)}, bf16[256,1024]{1,0:T(8,128)(2,1)S(1)}, u32[]{:S(2)}, u32[]{:S(2)}) collective-permute-start(bf16[256,1024]{1,0:T(8,128)(2,1)S(1)} %pad_maximum_fusion.3.w0), channel_id=1, source_target_pairs={{0,2},{2,0},{1,3},{3,1},{4,6},{6,4},{5,7},{7,5},{8,10},{10,8},{9,1... | collective-permute-start | bytes 1572872 | tf_op jit(solution)/shard_map/ppermute | solution.py:378
  99.5 13.8 %attend.3 = bf16[1024,256]{1,0:T(8,128)(2,1)S(1)} custom-call(s32[80]{0:T(128)S(1)} %reshape.222.tab_ref, f32[4]{0:T(128)S(1)} %dynamic-slice_bitcast_fusion.delta_ref, bf16[4096,256]{1,0:T(8,128)(2,1)S(1)} %get-tuple-element.69.k_ref, bf16[256,4096]{1,0:T(8,128)(2,1)S(1)} %get-tuple-element.70.vt_ref, bf16[256,2048]{1,0:T(8,128)(2,1)S(1)} %get-tuple-element.71.qt_ref, ...), custom_call_target="tpu_custom_call" | custom-call | flops 17600000000 | bytes 1048576 | tf_op jit(solution)/shard_map/attend/pallas_call | solution.py:381
  113.5 0.7 collective-permute-start.26
  114.2 1.7 %collective-permute-start.25 = (bf16[512,256]{1,0:T(8,128)(2,1)S(1)}, bf16[512,256]{1,0:T(8,128)(2,1)S(1)}, u32[]{:S(2)}, u32[]{:S(2)}) collective-permute-start(bf16[512,256]{1,0:T(8,128)(2,1)S(1)} %get-tuple-element.77), channel_id=1, source_target_pairs={{0,3},{1,2},{2,1},{3,0},{4,7},{5,6},{6,5},{7,4},{8,11},{9,10},{10,... | collective-permute-start | bytes 786440 | tf_op jit(solution)/shard_map/ppermute | solution.py:401
  115.9 13.6 %attend.2 = bf16[1024,256]{1,0:T(8,128)(2,1)S(1)} custom-call(s32[80]{0:T(128)S(1)} %reshape.222.tab_ref, f32[4]{0:T(128)S(1)} %dynamic-slice_bitcast_fusion.delta_ref, bf16[4096,256]{1,0:T(8,128)(2,1)S(1)} %get-tuple-element.69.k_ref, bf16[256,4096]{1,0:T(8,128)(2,1)S(1)} %get-tuple-element.70.vt_ref, bf16[256,2048]{1,0:T(8,128)(2,1)S(1)} %get-tuple-element.71.qt_ref, ...), custom_call_target="tpu_custom_call" | custom-call | flops 17600000000 | bytes 1048576 | tf_op jit(solution)/shard_map/attend/pallas_call | solution.py:381
  129.9 1.3 collective-permute-done.27.a1
  131.2 2.9 %mixed.1 = bf16[512,1024]{1,0:T(8,128)(2,1)} custom-call(s32[2]{0:T(128)S(1)} %pad_add_fusion.6.who_ref, bf16[512,256]{1,0:T(8,128)(2,1)S(1)} %get-tuple-element.96.a0, bf16[512,256]{1,0:T(8,128)(2,1)S(1)} %collective-permute-done.27.a1, bf16[512,256]{1,0:T(8,128)(2,1)S(1)} %collective-permute-done.24.a2, bf16[512,256]{1,0:T(8,128)(2,1)S(1)} %collective-permute-done.25.a3, ...), custom_call_target="tpu_custom_call" | custom-call | flops 3300000000 | bytes 1048576 | tf_op jit(solution)/shard_map/mixed/pallas_call | solution.py:408
  (117 shorter events, 13.2 us)
Async XLA Ops:
  0.6 4.6 %copy-start.4 = (bf16[64,1024]{1,0:T(8,128)(2,1)S(1)}, bf16[64,1024]{1,0:T(8,128)(2,1)}, u32[]{:S(2)}) copy-start(bf16[64,1024]{1,0:T(8,128)(2,1)} %param.9) | copy-start | bytes 393220
  0.6 9.4 %copy-start.8 = (s32[512]{0:T(512)S(1)}, s32[512]{0:T(512)}, u32[]{:S(2)}) copy-start(s32[512]{0:T(512)} %param.12) | copy-start | bytes 6148
  0.6 9.4 %copy-start.9 = (s32[512]{0:T(512)S(1)}, s32[512]{0:T(512)}, u32[]{:S(2)}) copy-start(s32[512]{0:T(512)} %param.13) | copy-start | bytes 6148
  0.6 9.4 %copy-start.10 = (s32[512]{0:T(512)S(1)}, s32[512]{0:T(512)}, u32[]{:S(2)}) copy-start(s32[512]{0:T(512)} %param.11) | copy-start | bytes 6148
  0.6 10.1 %copy-start = (bf16[512,1024]{1,0:T(8,128)(2,1)S(1)}, bf16[512,1024]{1,0:T(8,128)(2,1)}, u32[]{:S(2)}) copy-start(bf16[512,1024]{1,0:T(8,128)(2,1)} %refs_0_) | copy-start | bytes 3145732
  2.4 14.5 %collective-permute-start = (bf16[64,384]{1,0:T(8,128)(2,1)}, bf16[64,384]{1,0:T(8,128)(2,1)S(1)}, u32[]{:S(2)}, u32[]{:S(2)}) collective-permute-start(bf16[64,384]{1,0:T(8,128)(2,1)} %get-tuple-element.45), channel_id=1, source_target_pairs={{0,1},{1,0},{2,3},{3,2},{4,5},{5,4},{6,7},{7,6},{8,9},{9,8},{10,11... | collective-permute-start | bytes 147464 | tf_op jit(solution)/shard_map/ppermute | solution.py:201
  2.5 15.5 %collective-permute-start.1 = (bf16[64,384]{1,0:T(8,128)(2,1)}, bf16[64,384]{1,0:T(8,128)(2,1)S(1)}, u32[]{:S(2)}, u32[]{:S(2)}) collective-permute-start(bf16[64,384]{1,0:T(8,128)(2,1)} %get-tuple-element.46), channel_id=1, source_target_pairs={{0,2},{2,0},{1,3},{3,1},{4,6},{6,4},{5,7},{7,5},{8,10},{10,8},{9,1... | collective-permute-start | bytes 147464 | tf_op jit(solution)/shard_map/ppermute | solution.py:202
  5.2 12.9 %collective-permute-start.2 = (bf16[64,384]{1,0:T(8,128)(2,1)}, bf16[64,384]{1,0:T(8,128)(2,1)S(1)}, u32[]{:S(2)}, u32[]{:S(2)}) collective-permute-start(bf16[64,384]{1,0:T(8,128)(2,1)} %get-tuple-element.47), channel_id=1, source_target_pairs={{0,3},{1,2},{2,1},{3,0},{4,7},{5,6},{6,5},{7,4},{8,11},{9,10},{10,... | collective-permute-start | bytes 147464 | tf_op jit(solution)/shard_map/ppermute | solution.py:203
  5.2 13.4 %collective-permute-start.3 = (bf16[64,1024]{1,0:T(8,128)(2,1)S(1)}, bf16[64,1024]{1,0:T(8,128)(2,1)S(1)}, u32[]{:S(2)}, u32[]{:S(2)}) collective-permute-start(bf16[64,1024]{1,0:T(8,128)(2,1)S(1)} %copy-done.4), channel_id=1, source_target_pairs={{0,4},{4,8},{8,12},{12,0},{1,5},{5,9},{9,13},{13,1},{2,6},{6,10},{... | collective-permute-start | bytes 393224 | tf_op jit(solution)/shard_map/ppermute | solution.py:213
  6.9 14.6 %collective-permute-start.4 = (bf16[64,1024]{1,0:T(8,128)(2,1)S(1)}, bf16[64,1024]{1,0:T(8,128)(2,1)S(1)}, u32[]{:S(2)}, u32[]{:S(2)}) collective-permute-start(bf16[64,1024]{1,0:T(8,128)(2,1)S(1)} %copy-done.4), channel_id=1, source_target_pairs={{0,8},{4,12},{8,0},{12,4},{1,9},{5,13},{9,1},{13,5},{2,10},{6,14},... | collective-permute-start | bytes 393224 | tf_op jit(solution)/shard_map/ppermute | solution.py:213
  12.6 10.7 %copy-start.11 = (f32[2,16]{1,0:T(2,128)S(1)}, f32[2,16]{1,0:T(2,128)}, u32[]{:S(2)}) copy-start(f32[2,16]{1,0:T(2,128)} %param.10) | copy-start | bytes 388
  16.9 4.5 %collective-permute-start.5 = (bf16[64,1024]{1,0:T(8,128)(2,1)S(1)}, bf16[64,1024]{1,0:T(8,128)(2,1)S(1)}, u32[]{:S(2)}, u32[]{:S(2)}) collective-permute-start(bf16[64,1024]{1,0:T(8,128)(2,1)S(1)} %copy-done.4), channel_id=1, source_target_pairs={{0,12},{4,0},{8,4},{12,8},{1,13},{5,1},{9,5},{13,9},{2,14},{6,2},{... | collective-permute-start | bytes 393224 | tf_op jit(solution)/shard_map/ppermute | solution.py:213
  18.1 7.4 %collective-permute-start.7 = (bf16[256,384]{1,0:T(8,128)(2,1)S(1)}, bf16[256,384]{1,0:T(8,128)(2,1)S(1)}, u32[]{:S(2)}, u32[]{:S(2)}) collective-permute-start(bf16[256,384]{1,0:T(8,128)(2,1)S(1)} %get-tuple-element.100), channel_id=1, source_target_pairs={{0,4},{4,8},{8,12},{12,0},{1,5},{5,9},{9,13},{13,1},{2,6},{6,10},{... | collective-permute-start | bytes 589832 | tf_op jit(solution)/shard_map/ppermute | solution.py:213
  18.5 15.7 %collective-permute-start.8 = (bf16[256,384]{1,0:T(8,128)(2,1)S(1)}, bf16[256,384]{1,0:T(8,128)(2,1)S(1)}, u32[]{:S(2)}, u32[]{:S(2)}) collective-permute-start(bf16[256,384]{1,0:T(8,128)(2,1)S(1)} %get-tuple-element.100), channel_id=1, source_target_pairs={{0,8},{4,12},{8,0},{12,4},{1,9},{5,13},{9,1},{13,5},{2,10},{6,14},... | collective-permute-start | bytes 589832 | tf_op jit(solution)/shard_map/ppermute | solution.py:213
  18.6 2.9 %copy-start.5 = (bf16[64,1024]{1,0:T(8,128)(2,1)}, bf16[64,1024]{1,0:T(8,128)(2,1)S(1)}, u32[]{:S(2)}) copy-start(bf16[64,1024]{1,0:T(8,128)(2,1)S(1)} %collective-permute-done.3) | copy-start | bytes 393220
  18.6 15.8 %collective-permute-start.9 = (bf16[256,384]{1,0:T(8,128)(2,1)S(1)}, bf16[256,384]{1,0:T(8,128)(2,1)S(1)}, u32[]{:S(2)}, u32[]{:S(2)}) collective-permute-start(bf16[256,384]{1,0:T(8,128)(2,1)S(1)} %get-tuple-element.100), channel_id=1, source_target_pairs={{0,12},{4,0},{8,4},{12,8},{1,13},{5,1},{9,5},{13,9},{2,14},{6,2},{... | collective-permute-start | bytes 589832 | tf_op jit(solution)/shard_map/ppermute | solution.py:213
  21.5 0.6 copy-start.6
  22.1 15.0 %copy-start.7 = (bf16[64,1024]{1,0:T(8,128)(2,1)}, bf16[64,1024]{1,0:T(8,128)(2,1)S(1)}, u32[]{:S(2)}) copy-start(bf16[64,1024]{1,0:T(8,128)(2,1)S(1)} %collective-permute-done.5) | copy-start | bytes 393220
  22.1 15.0 %collective-permute-start.11 = (bf16[272,1024]{1,0:T(8,128)(2,1)}, bf16[272,1024]{1,0:T(8,128)(2,1)S(1)}, u32[]{:S(2)}, u32[]{:S(2)}) collective-permute-start(bf16[272,1024]{1,0:T(8,128)(2,1)} %pad_maximum_fusion.2), channel_id=1, source_target_pairs={{0,2},{2,0},{1,3},{3,1},{4,6},{6,4},{5,7},{7,5},{8,10},{10,8},{9,1... | collective-permute-start | bytes 1671176 | tf_op jit(solution)/shard_map/ppermute | solution.py:265
  23.9 31.2 %collective-permute-start.6 = (bf16[256,1024]{1,0:T(8,128)(2,1)}, bf16[256,1024]{1,0:T(8,128)(2,1)}, u32[]{:S(2)}, u32[]{:S(2)}) collective-permute-start(bf16[256,1024]{1,0:T(8,128)(2,1)} %get-tuple-element.53), channel_id=1, source_target_pairs={{0,2},{2,0},{1,3},{3,1},{4,6},{6,4},{5,7},{7,5},{8,10},{10,8},{9,1... | collective-permute-start | bytes 1572872 | tf_op jit(solution)/shard_map/ppermute | solution.py:265
  34.4 18.5 %collective-permute-start.10 = (bf16[272,1024]{1,0:T(8,128)(2,1)}, bf16[272,1024]{1,0:T(8,128)(2,1)S(1)}, u32[]{:S(2)}, u32[]{:S(2)}) collective-permute-start(bf16[272,1024]{1,0:T(8,128)(2,1)} %pad_maximum_fusion.2), channel_id=1, source_target_pairs={{4,0},{2,6},{8,4},{6,10},{12,8},{10,14},{5,1},{3,7},{9,5},{7,11},{... | collective-permute-start | bytes 1671176 | tf_op jit(solution)/shard_map/ppermute | solution.py:267
  35.8 19.3 %collective-permute-start.13 = (bf16[1024,384]{1,0:T(8,128)(2,1)S(1)}, bf16[1024,384]{1,0:T(8,128)(2,1)}, u32[]{:S(2)}, u32[]{:S(2)}) collective-permute-start(bf16[1024,384]{1,0:T(8,128)(2,1)S(1)} %constant_dynamic-update-slice_fusion.4.refs_14_), channel_id=1, source_target_pairs={{0,16},{16,0},{1,17},{17,1},{2,18},{18,2},{3,19},{19,3},{4,20},{20... | collective-permute-start | bytes 2359304 | tf_op jit(solution)/shard_map/ppermute | solution.py:253
  37.1 18.0 %collective-permute-start.12 = (bf16[272,1024]{1,0:T(8,128)(2,1)S(1)}, bf16[272,1024]{1,0:T(8,128)(2,1)S(1)}, u32[]{:S(2)}, u32[]{:S(2)}) collective-permute-start(bf16[272,1024]{1,0:T(8,128)(2,1)S(1)} %collective-permute-done.11.refs_2_), channel_id=1, source_target_pairs={{0,4},{6,2},{4,8},{10,6},{8,12},{14,10},{1,5},{7,3},{5,9},{11,7},{... | collective-permute-start | bytes 1671176 | tf_op jit(solution)/shard_map/ppermute | solution.py:268
  44.0 19.9 %collective-permute-start.17 = (bf16[272,1024]{1,0:T(8,128)(2,1)S(1)}, bf16[272,1024]{1,0:T(8,128)(2,1)}, u32[]{:S(2)}, u32[]{:S(2)}) collective-permute-start(bf16[272,1024]{1,0:T(8,128)(2,1)S(1)} %collective-permute-done.11.refs_2_), channel_id=1, source_target_pairs={{0,1},{1,0},{2,3},{3,2},{4,5},{5,4},{6,7},{7,6},{8,9},{9,8},{10,11... | collective-permute-start | bytes 1671176 | tf_op jit(solution)/shard_map/ppermute | solution.py:275
  52.9 13.6 %collective-permute-start.18 = (bf16[272,1024]{1,0:T(8,128)(2,1)S(1)}, bf16[272,1024]{1,0:T(8,128)(2,1)}, u32[]{:S(2)}, u32[]{:S(2)}) collective-permute-start(bf16[272,1024]{1,0:T(8,128)(2,1)S(1)} %collective-permute-done.10.refs_6_), channel_id=1, source_target_pairs={{0,1},{1,0},{2,3},{3,2},{4,5},{5,4},{6,7},{7,6},{8,9},{9,8},{10,11... | collective-permute-start | bytes 1671176 | tf_op jit(solution)/shard_map/ppermute | solution.py:275
  55.1 29.4 %collective-permute-start.15 = (bf16[256,1024]{1,0:T(8,128)(2,1)}, bf16[256,1024]{1,0:T(8,128)(2,1)}, u32[]{:S(2)}, u32[]{:S(2)}) collective-permute-start(bf16[256,1024]{1,0:T(8,128)(2,1)} %collective-permute-done.6.refs_3_), channel_id=1, source_target_pairs={{0,4},{6,2},{4,8},{10,6},{8,12},{14,10},{1,5},{7,3},{5,9},{11,7},{... | collective-permute-start | bytes 1572872 | tf_op jit(solution)/shard_map/ppermute | solution.py:273
  61.7 24.7 %collective-permute-start.20 = (bf16[256,1024]{1,0:T(8,128)(2,1)}, bf16[256,1024]{1,0:T(8,128)(2,1)}, u32[]{:S(2)}, u32[]{:S(2)}) collective-permute-start(bf16[256,1024]{1,0:T(8,128)(2,1)} %collective-permute-done.6.refs_3_), channel_id=1, source_target_pairs={{0,1},{1,0},{2,3},{3,2},{4,5},{5,4},{6,7},{7,6},{8,9},{9,8},{10,11... | collective-permute-start | bytes 1572872 | tf_op jit(solution)/shard_map/ppermute | solution.py:346
  63.9 5.3 %collective-permute-start.16 = (bf16[528,1024]{1,0:T(8,128)(2,1)}, bf16[528,1024]{1,0:T(8,128)(2,1)}, u32[]{:S(2)}, u32[]{:S(2)}) collective-permute-start(bf16[528,1024]{1,0:T(8,128)(2,1)} %pad_maximum_fusion), channel_id=1, source_target_pairs={{0,1},{1,0},{2,3},{3,2},{4,5},{5,4},{6,7},{7,6},{8,9},{9,8},{10,11... | collective-permute-start | bytes 3244040 | tf_op jit(solution)/shard_map/ppermute | solution.py:275
  64.7 3.8 %collective-permute-start.19 = (bf16[272,1024]{1,0:T(8,128)(2,1)S(1)}, bf16[272,1024]{1,0:T(8,128)(2,1)}, u32[]{:S(2)}, u32[]{:S(2)}) collective-permute-start(bf16[272,1024]{1,0:T(8,128)(2,1)S(1)} %collective-permute-done.12.refs_10_), channel_id=1, source_target_pairs={{0,1},{1,0},{2,3},{3,2},{4,5},{5,4},{6,7},{7,6},{8,9},{9,8},{10,11... | collective-permute-start | bytes 1671176 | tf_op jit(solution)/shard_map/ppermute | solution.py:275
  66.5 18.0 %collective-permute-start.14 = (bf16[256,1024]{1,0:T(8,128)(2,1)}, bf16[256,1024]{1,0:T(8,128)(2,1)}, u32[]{:S(2)}, u32[]{:S(2)}) collective-permute-start(bf16[256,1024]{1,0:T(8,128)(2,1)} %get-tuple-element.53), channel_id=1, source_target_pairs={{4,0},{2,6},{8,4},{6,10},{12,8},{10,14},{5,1},{3,7},{9,5},{7,11},{... | collective-permute-start | bytes 1572872 | tf_op jit(solution)/shard_map/ppermute | solution.py:272
  81.0 4.1 %copy-start.12 = (f32[1,16]{1,0:T(1,128)S(1)}, f32[1,16]{1,0:T(1,128)}, u32[]{:S(2)}) copy-start(f32[1,16]{1,0:T(1,128)} %slice_subtract_fusion) | copy-start | bytes 196
  84.5 2.2 %collective-permute-start.21 = (bf16[256,1024]{1,0:T(8,128)(2,1)}, bf16[256,1024]{1,0:T(8,128)(2,1)S(1)}, u32[]{:S(2)}, u32[]{:S(2)}) collective-permute-start(bf16[256,1024]{1,0:T(8,128)(2,1)} %collective-permute-done.14.refs_7_), channel_id=1, source_target_pairs={{0,1},{1,0},{2,3},{3,2},{4,5},{5,4},{6,7},{7,6},{8,9},{9,8},{10,11... | collective-permute-start | bytes 1572872 | tf_op jit(solution)/shard_map/ppermute | solution.py:349
  84.6 2.9 %collective-permute-start.22 = (bf16[256,1024]{1,0:T(8,128)(2,1)}, bf16[256,1024]{1,0:T(8,128)(2,1)S(1)}, u32[]{:S(2)}, u32[]{:S(2)}) collective-permute-start(bf16[256,1024]{1,0:T(8,128)(2,1)} %collective-permute-done.15.refs_11_), channel_id=1, source_target_pairs={{0,1},{1,0},{2,3},{3,2},{4,5},{5,4},{6,7},{7,6},{8,9},{9,8},{10,11... | collective-permute-start | bytes 1572872 | tf_op jit(solution)/shard_map/ppermute | solution.py:349
  86.3 13.2 %copy-start.1 = (s32[4096,128]{1,0:T(8,128)S(1)}, s32[4096,128]{1,0:T(8,128)}, u32[]{:S(2)}) copy-start(s32[4096,128]{1,0:T(8,128)} %get-tuple-element.74.vk_ref) | copy-start | bytes 6291460
  86.4 13.2 %copy-start.2 = (bf16[4096,128]{1,0:T(8,128)(2,1)S(1)}, bf16[4096,128]{1,0:T(8,128)(2,1)}, u32[]{:S(2)}) copy-start(bf16[4096,128]{1,0:T(8,128)(2,1)} %get-tuple-element.72.fk_ref) | copy-start | bytes 3145732
  86.4 13.2 %copy-start.3 = (bf16[128,2048]{1,0:T(8,128)(2,1)S(1)}, bf16[128,2048]{1,0:T(8,128)(2,1)}, u32[]{:S(2)}) copy-start(bf16[128,2048]{1,0:T(8,128)(2,1)} %get-tuple-element.73.fqt_ref) | copy-start | bytes 1572868
  96.0 17.4 %collective-permute-start.23 = (bf16[256,1024]{1,0:T(8,128)(2,1)S(1)}, bf16[256,1024]{1,0:T(8,128)(2,1)S(1)}, u32[]{:S(2)}, u32[]{:S(2)}) collective-permute-start(bf16[256,1024]{1,0:T(8,128)(2,1)S(1)} %pad_maximum_fusion.3.w0), channel_id=1, source_target_pairs={{0,2},{2,0},{1,3},{3,1},{4,6},{6,4},{5,7},{7,5},{8,10},{10,8},{9,1... | collective-permute-start | bytes 1572872 | tf_op jit(solution)/shard_map/ppermute | solution.py:378
  113.5 16.0 %collective-permute-start.26 = (bf16[2,256,1024]{2,1,0:T(8,128)(2,1)S(1)}, bf16[2,256,1024]{2,1,0:T(8,128)(2,1)S(1)}, u32[]{:S(2)}, u32[]{:S(2)}) collective-permute-start(bf16[2,256,1024]{2,1,0:T(8,128)(2,1)S(1)} %pad_maximum_fusion.1), channel_id=1, source_target_pairs={{0,1},{1,0},{2,3},{3,2},{4,5},{5,4},{6,7},{7,6},{8,9},{9,8},{10,11... | collective-permute-start | bytes 3145736 | tf_op jit(solution)/shard_map/ppermute | solution.py:402
  114.2 15.3 %collective-permute-start.24 = (bf16[512,256]{1,0:T(8,128)(2,1)S(1)}, bf16[512,256]{1,0:T(8,128)(2,1)S(1)}, u32[]{:S(2)}, u32[]{:S(2)}) collective-permute-start(bf16[512,256]{1,0:T(8,128)(2,1)S(1)} %get-tuple-element.76), channel_id=1, source_target_pairs={{0,2},{2,0},{1,3},{3,1},{4,6},{6,4},{5,7},{7,5},{8,10},{10,8},{9,1... | collective-permute-start | bytes 786440 | tf_op jit(solution)/shard_map/ppermute | solution.py:400
  114.2 15.3 %collective-permute-start.25 = (bf16[512,256]{1,0:T(8,128)(2,1)S(1)}, bf16[512,256]{1,0:T(8,128)(2,1)S(1)}, u32[]{:S(2)}, u32[]{:S(2)}) collective-permute-start(bf16[512,256]{1,0:T(8,128)(2,1)S(1)} %get-tuple-element.77), channel_id=1, source_target_pairs={{0,3},{1,2},{2,1},{3,0},{4,7},{5,6},{6,5},{7,4},{8,11},{9,10},{10,... | collective-permute-start | bytes 786440 | tf_op jit(solution)/shard_map/ppermute | solution.py:401
  129.6 1.6 %collective-permute-start.27 = (bf16[512,256]{1,0:T(8,128)(2,1)S(1)}, bf16[512,256]{1,0:T(8,128)(2,1)S(1)}, u32[]{:S(2)}, u32[]{:S(2)}) collective-permute-start(bf16[512,256]{1,0:T(8,128)(2,1)S(1)} %get-tuple-element.79), channel_id=1, source_target_pairs={{0,1},{1,0},{2,3},{3,2},{4,5},{5,4},{6,7},{7,6},{8,9},{9,8},{10,11... | collective-permute-start | bytes 786440 | tf_op jit(solution)/shard_map/ppermute | solution.py:406
